TPU v7x, 32 devices: a whole 2x2x4 slice. The times are simulated.
32 devices in a mesh: groups: 2 (over x), seq: 16 (over z, y, core).
Axes of the slice: x: 2, y: 2, z: 4, core: 2. Of those that a mesh axis runs over, the one named last changes fastest.
Arguments:
- mixed_qkv: bfloat16 [4096, 8192], P(('groups', 'seq')), parts along dimension 0, may hold values from -6 to 6
- conv_weight: bfloat16 [4, 8192], replicated, may hold values from -3 to 3
- beta_logit: bfloat16 [4096, 32], P(('groups', 'seq')), parts along dimension 0
- log_decay: float32 [4096, 32], P(('groups', 'seq')), parts along dimension 0
- gate_in: bfloat16 [4096, 4096], P(('groups', 'seq')), parts along dimension 0, may hold values from -6 to 6
- norm_gain: float32 [128], replicated, may hold values from 0.1 to 1.9
Outputs:
- layer_out: bfloat16 [4096, 4096], P(('groups', 'seq')), parts along dimension 0
There are 2 independent parts, one for each index of `groups`. A program takes and returns all parts, laid end to end along the dimension named above; an argument that names none is the same for every part. Nothing has to cross between parts.
All inputs are finite; a program needn't handle non-finite values.
Results may differ from a plain program's by a relative error of at most 0.0044.
Values may be sent and summed in bfloat16 or wider, within the bound.
No kernel may reach another device: no remote copies, remote signals or barrier semaphores. Data moves between devices by JAX's collectives and lax.ppermute only.
A program may use at most 128 MiB of HBM per device.

v0:
```python
import jax
import jax.numpy as jnp
from jax import lax
from jax.sharding import PartitionSpec as P

KH = 16
VH = 32
DH = 128
CH = 128


HIGHEST = lax.Precision.HIGHEST


def from_behind(block, axis, distance):
    devices = range(lax.axis_size(axis))
    route = [(i - distance, i) for i in devices if i - distance in devices]
    return lax.ppermute(block, axis, route)


def unit_rows(values):
    return values * lax.rsqrt(jnp.sum(values * values, axis=-1, keepdims=True) + 1e-06)


def convolve(padded, conv_weight, row_count):
    tap_count = conv_weight.shape[0]
    conv_sum = jnp.zeros((row_count, padded.shape[1]), jnp.float32)
    for tap_index in range(tap_count):
        conv_sum = conv_sum + padded[tap_index : tap_index + row_count].astype(
            jnp.float32
        ) * conv_weight[tap_index].astype(jnp.float32)
    return jax.nn.silu(conv_sum).astype(jnp.bfloat16)


def split_heads(conv_out):
    row_count = conv_out.shape[0]
    key_cols = KH * DH
    query_rows = unit_rows(
        conv_out[:, :key_cols].astype(jnp.float32).reshape(row_count, KH, DH)
    ) * DH ** (-0.5)
    key_rows = unit_rows(
        conv_out[:, key_cols : 2 * key_cols].astype(jnp.float32).reshape(row_count, KH, DH)
    )
    value_rows = conv_out[:, 2 * key_cols :].astype(jnp.float32).reshape(row_count, VH, DH)
    return (query_rows, key_rows, value_rows)


def span_terms(query_rows, key_rows, value_rows, beta_rows, decay_log):
    block_len = query_rows.shape[0]
    head_width = query_rows.shape[2]
    head_repeat = value_rows.shape[1] // key_rows.shape[1]
    lower_mask = jnp.tril(jnp.ones((block_len, block_len), jnp.float32))
    identity_block = jnp.eye(block_len, dtype=jnp.float32)
    strict_mask = lower_mask - identity_block
    cumulative = jnp.dot(lower_mask, decay_log, precision=HIGHEST).T
    log_gaps = cumulative[:, :, None] - cumulative[:, None, :]
    decay_pair = jnp.exp(jnp.minimum(log_gaps, 0.0)) * lower_mask
    key_dot = jnp.repeat(
        jnp.einsum("tgd,sgd->gts", key_rows, key_rows, precision=HIGHEST), head_repeat, axis=0
    )
    query_dot = jnp.repeat(
        jnp.einsum("tgd,sgd->gts", query_rows, key_rows, precision=HIGHEST), head_repeat, axis=0
    )
    keys_head = jnp.repeat(key_rows, head_repeat, axis=1).transpose(1, 0, 2)
    query_head = jnp.repeat(query_rows, head_repeat, axis=1).transpose(1, 0, 2)
    values_head = value_rows.transpose(1, 0, 2)
    beta_head = beta_rows.T
    growth = jnp.exp(cumulative)
    system = identity_block + beta_head[:, :, None] * decay_pair * key_dot * strict_mask
    right_side = jnp.concatenate(
        [(beta_head * growth)[:, :, None] * keys_head, beta_head[:, :, None] * values_head], axis=2
    )
    solved = jax.scipy.linalg.solve_triangular(system, right_side, lower=True, unit_diagonal=True)
    w_rows = solved[:, :, :head_width]
    u_rows = solved[:, :, head_width:]
    mixing = decay_pair * query_dot
    local_out = jnp.einsum("hts,hsd->htd", mixing, u_rows, precision=HIGHEST)
    carry_map = growth[:, :, None] * query_head - jnp.einsum(
        "hts,hsk->htk", mixing, w_rows, precision=HIGHEST
    )
    key_tail = jnp.exp(cumulative[:, -1:] - cumulative)[:, :, None] * keys_head
    transition = growth[:, -1][:, None, None] * jnp.eye(head_width, dtype=jnp.float32) - jnp.einsum(
        "hsk,hsj->hkj", w_rows, key_tail, precision=HIGHEST
    )
    state_add = jnp.einsum("hsv,hsk->hvk", u_rows, key_tail, precision=HIGHEST)
    return (carry_map, local_out, transition, state_add)


def gated_norm(core_out, gate_in, norm_gain):
    mean_sq = jnp.mean(core_out * core_out, axis=-1, keepdims=True)
    gate_val = gate_in.astype(jnp.float32).reshape(core_out.shape)
    scaled = core_out * lax.rsqrt(mean_sq + 1e-06) * norm_gain * jax.nn.silu(gate_val)
    return scaled.astype(jnp.bfloat16).reshape(
        core_out.shape[0], core_out.shape[1] * core_out.shape[2]
    )


def compose(first_pair, second_pair):
    first_trans, first_add = first_pair
    second_trans, second_add = second_pair
    joined_trans = jnp.einsum("hij,hjk->hik", first_trans, second_trans, precision=HIGHEST)
    joined_add = jnp.einsum("hvk,hkj->hvj", first_add, second_trans, precision=HIGHEST) + second_add
    return (joined_trans, joined_add)


def owner_chain(device_trans, device_add):
    seq_count = lax.axis_size("seq")
    col_parts = max(seq_count // VH, 1)
    head_pack = max(VH // seq_count, 1)
    head_groups = VH // head_pack
    col_width = DH // col_parts
    send_trans = jnp.broadcast_to(
        device_trans.reshape(head_groups, 1, head_pack, DH, DH),
        (head_groups, col_parts, head_pack, DH, DH),
    ).reshape(seq_count, head_pack, DH, DH)
    send_add = (
        device_add.reshape(head_groups, head_pack, col_parts, col_width, DH)
        .transpose(0, 2, 1, 3, 4)
        .reshape(seq_count, head_pack, col_width, DH)
    )
    recv_trans, recv_add = (
        lax.all_to_all(send_trans, "seq", split_axis=0, concat_axis=0, tiled=True),
        lax.all_to_all(send_add, "seq", split_axis=0, concat_axis=0, tiled=True),
    )

    def walk_step(state_now, pieces):
        trans_piece, add_piece = pieces
        moved = jnp.einsum("pvk,pkj->pvj", state_now, trans_piece, precision=HIGHEST) + add_piece
        return (moved, state_now)

    _, entering = lax.scan(
        walk_step, jnp.zeros((head_pack, col_width, DH), jnp.float32), (recv_trans, recv_add)
    )
    returned = lax.all_to_all(entering, "seq", split_axis=0, concat_axis=0, tiled=True)
    return (
        returned.reshape(head_groups, col_parts, head_pack, col_width, DH)
        .transpose(0, 2, 1, 3, 4)
        .reshape(VH, DH, DH)
    )


def local(mixed_qkv, conv_weight, beta_logit, log_decay, gate_in, norm_gain):
    row_count = mixed_qkv.shape[0]
    tap_count = conv_weight.shape[0]
    rim_rows = from_behind(mixed_qkv[row_count - (tap_count - 1) :], "seq", 1)
    conv_out = convolve(jnp.concatenate([rim_rows, mixed_qkv], axis=0), conv_weight, row_count)
    query_rows, key_rows, value_rows = split_heads(conv_out)
    beta_rows = jax.nn.sigmoid(beta_logit.astype(jnp.float32))
    span_count = row_count // CH
    carry_map, local_out, transition, state_add = jax.vmap(span_terms)(
        query_rows.reshape(span_count, CH, KH, DH),
        key_rows.reshape(span_count, CH, KH, DH),
        value_rows.reshape(span_count, CH, VH, DH),
        beta_rows.reshape(span_count, CH, VH),
        log_decay.reshape(span_count, CH, VH),
    )

    def compose_step(so_far, pieces):
        return (compose(so_far, pieces), None)

    device_trans, device_add = (transition[0], state_add[0])
    start_state = owner_chain(device_trans, device_add)

    def advance(state_now, pieces):
        map_piece, out_piece, trans_piece, add_piece = pieces
        core_piece = out_piece + jnp.einsum("htk,hvk->htv", map_piece, state_now, precision=HIGHEST)
        moved = jnp.einsum("hvk,hkj->hvj", state_now, trans_piece, precision=HIGHEST) + add_piece
        return (moved, core_piece)

    _, core_out = lax.scan(advance, start_state, (carry_map, local_out, transition, state_add))
    core_out = core_out.transpose(0, 2, 1, 3).reshape(row_count, VH, DH)
    return gated_norm(core_out, gate_in, norm_gain)


def solution(mesh):
    return jax.shard_map(
        local,
        mesh=mesh,
        in_specs=(
            P(("groups", "seq"), None),
            P(),
            P(("groups", "seq"), None),
            P(("groups", "seq"), None),
            P(("groups", "seq"), None),
            P(),
        ),
        out_specs=P(("groups", "seq"), None),
        check_vma=False,
    )
```

profile of v0, /device:TPU:13, one launch (start us, length us, event | category | flops | bytes accessed | tf_op | source)
XLA Modules:
  0.0 573.3 jit_solution(9342081820979151264)
XLA Ops:
  1.0 3.7 collective-permute-start
  7.6 1.4 fusion.47
  9.8 4.1 copy.35
  13.9 1.8 copy.34
  15.7 10.7 %multiply_convert_fusion = bf16[128,8192]{0,1:T(8,128)(2,1)S(1)} fusion(bf16[128,8192]{0,1:T(8,128)(2,1)} %copy.35, bf16[3,8192]{0,1:T(8,128)(2,1)} %copy.34, f32[8192]{0:T(1024)S(1)} %bitcast.156, f32[8192]{0:T(1024)S(1)} %bitcast.157, f32[8192]{0:T(1024)S(1)} %bitcast.155, f32[8192]{0:T(1024)S(1)} %bitcast.154), kind=kLoop, calls=%fused_computation.18 | loop fusion | flops 26214400 | bytes 4374528 | tf_op jit(solution)/shard_map/convert_element_type | solution.py:32
  28.2 1.2 copy.38
  30.8 1.6 broadcast_multiply_fusion
  32.3 2.3 fusion.50
  34.6 1.9 bitcast_multiply_fusion.5
  37.4 1.3 select_add_fusion
  38.7 315.1 %custom-call.4 = f32[1,32,1,128,128]{3,4,2,1,0:T(8,128)} custom-call(f32[1,32,1,128,128]{4,3,2,1,0:T(8,128)S(1)} %select_add_fusion), custom_call_target="InvertDiagBlocksLowerTriangular" | custom-call | tf_op jit(solution)/shard_map/vmap(jit(_solve_triangular))/vmap()/triangular_solve | solution.py:73
  356.1 3.8 fusion.11
  359.9 5.1 multiply_subtract_fusion
  365.1 3.0 copy.43
  368.1 5.0 all-to-all-start
  373.1 6.4 %fusion.21 = f32[32,128,128]{1,2,0:T(8,128)} fusion(f32[1,32,128,128]{3,2,1,0:T(8,128)S(1)} %get-tuple-element.87, f32[1,32,128,256]{3,2,1,0:T(8,128)} %copy-done.1), kind=kOutput, calls=%fused_computation.39 | convolution fusion | flops 805306368 | bytes 6291456 | tf_op jit(solution)/shard_map/vmap(hsv,hsk->hvk)/dot_general | solution.py:85
  379.5 41.1 %all-to-all-done = f32[16,2,128,128]{2,3,1,0:T(8,128)} async-done(((f32[16,2,128,128]{2,3,1,0:T(8,128)}), f32[16,2,128,128]{2,3,1,0:T(8,128)}, u32[]{:S(2)}, u32[]{:S(2)}) %all-to-all-start) | async-done | bytes 2097184 | tf_op jit(solution)/shard_map/all_to_all | solution.py:122
  420.6 4.9 all-to-all-start.1
  425.5 47.4 %all-to-all-done.1 = f32[16,2,128,128]{2,3,1,0:T(8,128)S(1)} async-done(((f32[16,2,128,128]{2,3,1,0:T(8,128)}), f32[16,2,128,128]{2,3,1,0:T(8,128)S(1)}, u32[]{:S(2)}, u32[]{:S(2)}) %all-to-all-start.1) | async-done | bytes 2097184 | tf_op jit(solution)/shard_map/all_to_all | solution.py:123
  472.9 30.0 %while.3 = (s32[]{:T(128)}, f32[2,128,128]{1,2,0:T(8,128)S(1)}, f32[16,2,128,128]{2,3,1,0:T(8,128)}, f32[16,2,128,128]{2,3,1,0:T(8,128)}, f32[16,2,128,128]{2,3,1,0:T(8,128)S(1)}, /*index=5*/s32[]{:T(128)}, s32[]{:T(128)}) while((s32[]{:T(128)}, f32[2,128,128]{1,2,0:T(8,128)S(1)}, f32[16,2,128,128]{2,3,1,0:T(8,128)}, ...), condition=%wide.region_3.4_spmd.clone, body=%wide.region_2.3_spmd.clone.sunk | while | flops 50429952 | bytes 1050211 | solution.py:131
  473.6 1.2 fusion.64
  475.5 1.2 fusion.64
  481.1 1.2 fusion.64
  484.9 1.2 fusion.64
  503.0 5.2 all-to-all-start.2
  508.9 2.3 fusion.49
  511.8 3.7 fusion.19
  515.5 40.1 %all-to-all-done.2 = f32[16,2,128,128]{2,3,1,0:T(8,128)} async-done(((f32[16,2,128,128]{2,3,1,0:T(8,128)}), f32[16,2,128,128]{2,3,1,0:T(8,128)}, u32[]{:S(2)}, u32[]{:S(2)}) %all-to-all-start.2) | async-done | bytes 2097184 | tf_op jit(solution)/shard_map/all_to_all | solution.py:134
  555.6 5.8 %fusion.25 = f32[32,128,128]{1,2,0:T(8,128)S(1)} fusion(f32[32,128,128]{1,2,0:T(8,128)} %bitcast.53, f32[1,32,128,128]{3,2,1,0:T(8,128)} %fusion.19), kind=kOutput, calls=%fused_computation.43 | convolution fusion | flops 805306368 | bytes 6291456 | tf_op jit(solution)/shard_map/while/body/eval_jaxpr/htk,hvk->htv/dot_general | solution.py:166
  561.5 5.3 fusion.20
  566.7 1.9 copy.48
  569.9 3.0 fusion.28
  (106 shorter events, 38.1 us)
Async XLA Ops:
  0.0 6.4 %copy-start = (f32[128,32]{0,1:T(8,128)S(1)}, f32[128,32]{0,1:T(8,128)}, u32[]{:S(2)}) copy-start(f32[128,32]{0,1:T(8,128)} %param.11) | copy-start | bytes 49156
  1.0 12.9 %collective-permute-start = (bf16[3,8192]{1,0:T(4,128)(2,1)S(1)}, bf16[3,8192]{1,0:T(4,128)(2,1)S(1)}, u32[]{:S(2)}, u32[]{:S(2)}) collective-permute-start(bf16[3,8192]{1,0:T(4,128)(2,1)S(1)} %slice.51), channel_id=1, source_target_pairs={{0,1},{1,2},{2,3},{3,4},{4,5},{5,6},{6,7},{7,8},{8,9},{9,10},{10,1... | collective-permute-start | bytes 147464 | tf_op jit(solution)/shard_map/ppermute | solution.py:18
  26.4 1.8 copy-start.4
  28.2 1.4 slice-start
  28.2 1.9 copy-start.13
  28.2 2.0 copy-start.14
  36.6 0.8 copy-start.9
  37.4 316.5 %copy-start.10 = (f32[32,128]{1,0:T(8,128)S(1)}, f32[32,128]{1,0:T(8,128)}, u32[]{:S(2)}) copy-start(f32[32,128]{1,0:T(8,128)} %get-tuple-element.93) | copy-start | bytes 49156
  37.4 316.5 %copy-start.11 = (f32[32,128]{1,0:T(8,128)S(1)}, f32[32,128]{1,0:T(8,128)}, u32[]{:S(2)}) copy-start(f32[32,128]{1,0:T(8,128)} %get-tuple-element.94) | copy-start | bytes 49156
  353.9 1.6 copy-start.5
  353.9 2.2 copy-start.6
  356.1 3.8 copy-start.15
  359.9 5.2 copy-start.1
  368.1 52.6 %all-to-all-start = ((f32[16,2,128,128]{2,3,1,0:T(8,128)}), f32[16,2,128,128]{2,3,1,0:T(8,128)}, u32[]{:S(2)}, u32[]{:S(2)}) async-start(f32[16,2,128,128]{2,3,1,0:T(8,128)} %copy.43), calls=%async_computation | async-start | bytes 4194304 | tf_op jit(solution)/shard_map/all_to_all | solution.py:122
  420.6 52.3 %all-to-all-start.1 = ((f32[16,2,128,128]{2,3,1,0:T(8,128)}), f32[16,2,128,128]{2,3,1,0:T(8,128)S(1)}, u32[]{:S(2)}, u32[]{:S(2)}) async-start(f32[16,2,128,128]{2,3,1,0:T(8,128)} %bitcast.144), calls=%async_computation.1 | async-start | bytes 4194304 | tf_op jit(solution)/shard_map/all_to_all | solution.py:123
  503.0 5.3 copy-start.16
  503.0 5.3 copy-start.7
  503.0 5.5 copy-start.12
  503.0 52.6 %all-to-all-start.2 = ((f32[16,2,128,128]{2,3,1,0:T(8,128)}), f32[16,2,128,128]{2,3,1,0:T(8,128)}, u32[]{:S(2)}, u32[]{:S(2)}) async-start(f32[16,2,128,128]{2,3,1,0:T(8,128)} %get-tuple-element.53), calls=%async_computation.2 | async-start | bytes 4194304 | tf_op jit(solution)/shard_map/all_to_all | solution.py:134
  508.9 2.9 copy-start.2
  555.6 5.9 %copy-start.3 = (f32[1,32,128,256]{3,2,1,0:T(8,128)S(1)}, f32[1,32,128,256]{3,2,1,0:T(8,128)}, u32[]{:S(2)}) copy-start(f32[1,32,128,256]{3,2,1,0:T(8,128)} %copy-done.1) | copy-start | bytes 12582916
  568.7 1.2 copy-start.8
where the time goes:
time: 580 us; the launch traced here: 573 us
  other arithmetic  352 us (61%)
  waiting for transfers between devices  129 us (22%)
  matrix products  53.7 us (9%)
  local copies, waits for them, and re-layouts  19.1 us (3%)
  starting transfers between devices  18.9 us (3%)
    another operation x5, other arithmetic, span_terms(): jax.scipy.linalg.solve_triangular(system, right_side, lower=True, unit_di...  317 us
    all_to_all x1, waiting for transfers between devices, owner_chain(): lax.all_to_all(send_add, 'seq', split_axis=0, concat_axis=0, tiled=True)  47.4 us
    all_to_all x1, waiting for transfers between devices, owner_chain(): lax.all_to_all(send_trans, 'seq', split_axis=0, concat_axis=0, tiled=True)  41.1 us
    all_to_all x1, waiting for transfers between devices, owner_chain(): lax.all_to_all(entering, 'seq', split_axis=0, concat_axis=0, tiled=True)  40.1 us
    dot_general x16, matrix products, walk_step(): jnp.einsum('pvk,pkj->pvj', state_now, trans_piece, precision=HIGHEST)  18.7 us
  transfers between devices with their start and end apart: 4, of which 3 were waited for; matrix products, arithmetic and copies ran while one was open for 4% of the time, Pallas kernels for 0%

commit v1 on v0

v1 whole, which is shorter than its diff:
```python
import functools

import jax
import jax.numpy as jnp
from jax import lax
from jax.experimental import pallas as pl
from jax.experimental.pallas import tpu as pltpu
from jax.sharding import PartitionSpec as P

KH = 16
VH = 32
DH = 128
CH = 128
CHIPS = 4
PIECE = 4
ROWS = PIECE * DH + 16
WIDE = 2 * DH

F32 = jnp.float32
BF16 = jnp.bfloat16


def dot(a, b):
    return jnp.dot(a, b, preferred_element_type=F32)


def halves(x):
    high = x.astype(BF16)
    return high, (x - high.astype(F32)).astype(BF16)


def decay_rows(decays):
    high, low = halves(decays)
    return jnp.concatenate([high, low], axis=0)


def decays_of(rows):
    rows = rows.astype(F32)
    return rows[:8] + rows[8:]


def head_slice(h):
    return slice(h * DH, (h + 1) * DH)


def terms_kernel(
    sc_ref, xq, xk, xv, pq, pk, pv, wq, wk, wv, rows_ref, masks_ref, ma_ref, loc_ref, car_ref, scr
):
    convs = []
    at = 0
    for x_ref, p_ref, w_ref in ((xq, pq, wq), (xk, pk, wk), (xv, pv, wv)):
        width = x_ref.shape[1]
        cols = slice(at, at + width)
        scr[0:8, cols] = p_ref[...].astype(F32)
        scr[8 : 8 + CH, cols] = x_ref[...].astype(F32)
        w = w_ref[...].astype(F32)
        total = scr[5 : 5 + CH, cols] * w[0:1]
        for tap in range(1, 4):
            total = total + scr[5 + tap : 5 + tap + CH, cols] * w[tap : tap + 1]
        convs.append((total / (1.0 + jnp.exp(-total))).astype(BF16))
        at += width
    cq, ck, cv = convs

    rows = rows_ref[0]
    cols = rows.T
    grow_cols = jnp.exp(cols)
    tail_rows = jnp.exp(rows[:, CH - 1 : CH] - rows)
    ma_ref[0, PIECE * DH :, :] = decay_rows(
        jnp.broadcast_to(jnp.exp(rows[:, CH - 1 : CH]), (8, WIDE))
    )

    t_at = lax.broadcasted_iota(jnp.int32, (CH, CH), 0)
    s_at = lax.broadcasted_iota(jnp.int32, (CH, CH), 1)
    lower = t_at >= s_at
    strict = t_at > s_at
    unit = (t_at == s_at).astype(F32)

    per_head = []
    for g in range(PIECE // 2):
        q_b, k_b = cq[:, head_slice(g)], ck[:, head_slice(g)]
        q_f, k_f = q_b.astype(F32), k_b.astype(F32)
        k_t = k_f.T
        rq_col = lax.rsqrt(jnp.sum(q_f * q_f, axis=1, keepdims=True) + 1e-06) * DH ** (-0.5)
        rk_col = lax.rsqrt(jnp.sum(k_f * k_f, axis=1, keepdims=True) + 1e-06)
        rk_row = lax.rsqrt(jnp.sum(k_t * k_t, axis=0, keepdims=True) + 1e-06)
        gram = dot(jnp.concatenate([q_b, k_b], axis=0), k_t.astype(BF16))
        query_dot = gram[:CH] * rq_col * rk_row
        key_dot = gram[CH:] * rk_col * rk_row
        for i in range(2):
            h = 2 * g + i
            pair = jnp.where(lower, jnp.exp(jnp.minimum(cols[:, h : h + 1] - rows[h : h + 1], 0.0)), 0.0)
            system = jnp.where(strict, key_dot * pair * cols[:, 4 + h : 5 + h], 0.0)
            per_head.append(
                dict(
                    h=h,
                    mixing=halves(query_dot * pair),
                    system=system.astype(BF16),
                    key_gain=(k_f * (grow_cols[:, h : h + 1] * rk_col)).astype(BF16),
                    query=q_f * (grow_cols[:, h : h + 1] * rq_col),
                    tail=halves(k_t * (rk_row * tail_rows[h : h + 1])),
                )
            )
            first = unit - system * masks_ref[0].astype(F32)
            per_head[-1]["inv"] = halves(first)

    for level in range(1, 7):
        mask = masks_ref[level]
        steps = [dot(p["inv"][0], p["system"] * mask) for p in per_head]
        steps = [dot(s.astype(BF16), p["inv"][0]) for s, p in zip(steps, per_head)]
        for s, p in zip(steps, per_head):
            high, low = halves(s)
            p["inv"] = (p["inv"][0] - high, p["inv"][1] - low)

    for p in per_head:
        h = p["h"]
        inv = halves((p["inv"][0].astype(F32) + p["inv"][1].astype(F32)) * rows[4 + h : 5 + h])
        right = jnp.concatenate([p["key_gain"], cv[:, head_slice(h)]], axis=1)
        p["solved"] = dot(
            jnp.concatenate(inv, axis=1), jnp.concatenate([right, right], axis=0)
        ).astype(BF16)
    for p in per_head:
        h = p["h"]
        left = jnp.concatenate(
            [jnp.concatenate(p["mixing"], axis=1), jnp.concatenate(p["tail"], axis=1)], axis=0
        )
        both = dot(left, jnp.concatenate([p["solved"], p["solved"]], axis=0))
        ma_ref[0, head_slice(h), :] = both[CH:].astype(BF16)
        loc_ref[0, h] = both[:CH, DH:]
        car_ref[0, h] = jnp.concatenate(halves(p["query"] - both[:CH, :DH]), axis=1)


def block_terms(owner, mixed_qkv, rim, conv_weight, rows, masks):
    pieces = VH // 2 // PIECE
    kd, vd = PIECE // 2 * DH, PIECE * DH
    key_blocks = KH * DH // kd

    def at(first):
        return lambda i, sc: (0, first + pieces * sc[0] + i)

    specs = []
    for height in (CH, 8, conv_weight.shape[0]):
        specs += [
            pl.BlockSpec((height, kd), at(0)),
            pl.BlockSpec((height, kd), at(key_blocks)),
            pl.BlockSpec((height, vd), at(2 * KH * DH // vd)),
        ]
    out_specs = [
        pl.BlockSpec((1, ROWS, WIDE), lambda i, sc: (i, 0, 0)),
        pl.BlockSpec((1, PIECE, CH, DH), lambda i, sc: (i, 0, 0, 0)),
        pl.BlockSpec((1, PIECE, CH, WIDE), lambda i, sc: (i, 0, 0, 0)),
    ]
    return pl.pallas_call(
        terms_kernel,
        out_shape=[
            jax.ShapeDtypeStruct((pieces, ROWS, WIDE), BF16),
            jax.ShapeDtypeStruct((pieces, PIECE, CH, DH), F32),
            jax.ShapeDtypeStruct((pieces, PIECE, CH, WIDE), BF16),
        ],
        grid_spec=pltpu.PrefetchScalarGridSpec(
            num_scalar_prefetch=1,
            grid=(pieces,),
            in_specs=specs
            + [
                pl.BlockSpec((1, 8, CH), lambda i, sc: (pieces * sc[0] + i, 0, 0)),
                pl.BlockSpec((7, CH, CH), lambda i, sc: (0, 0, 0)),
            ],
            out_specs=out_specs,
            scratch_shapes=[pltpu.VMEM((CH + 8, 2 * kd + vd), F32)],
        ),
        cost_estimate=pl.CostEstimate(flops=2_000_000_000, bytes_accessed=6_000_000, transcendentals=0),
        name="block_terms",
    )(
        owner,
        *([mixed_qkv] * 3),
        *([rim] * 3),
        *([conv_weight] * 3),
        rows,
        masks,
    )


def compose_kernel(sc_ref, mine_ref, theirs_ref, out_ref):
    is_first = sc_ref[0] == 0
    mine_g, theirs_g = decays_of(mine_ref[0, PIECE * DH :]), decays_of(theirs_ref[0, PIECE * DH :])
    first_g = jnp.where(is_first, mine_g, theirs_g)
    second_g = jnp.where(is_first, theirs_g, mine_g)
    for h in range(PIECE):
        mine, theirs = mine_ref[0, head_slice(h)], theirs_ref[0, head_slice(h)]
        first = jnp.where(is_first, mine, theirs)
        second = jnp.where(is_first, theirs, mine)
        product = dot(second[:, :DH], first)
        kept = jnp.concatenate(
            [second[:, :DH].astype(F32) * first_g[h : h + 1, :DH], second[:, DH:].astype(F32)],
            axis=1,
        )
        joined = first.astype(F32) * second_g[h : h + 1] - product + kept
        out_ref[head_slice(h), :] = joined.astype(BF16)
    out_ref[PIECE * DH :, :] = decay_rows(first_g * second_g)


def compose(place, mine, theirs, offset):
    spec = pl.BlockSpec((1, ROWS, WIDE), lambda i, sc: (sc[1] ^ offset, 0, 0))
    return pl.pallas_call(
        compose_kernel,
        out_shape=jax.ShapeDtypeStruct((ROWS, WIDE), BF16),
        grid_spec=pltpu.PrefetchScalarGridSpec(
            num_scalar_prefetch=1,
            grid=(1,),
            in_specs=[spec, spec],
            out_specs=pl.BlockSpec((ROWS, WIDE), lambda i, sc: (0, 0)),
        ),
        cost_estimate=pl.CostEstimate(flops=40_000_000, bytes_accessed=900_000, transcendentals=0),
        name="compose",
    )(place, mine, theirs)


def advance(ref, slot, h, state):
    decays = decays_of(ref[slot, PIECE * DH :])
    mats = ref[slot, head_slice(h)]
    return (
        state.astype(F32) * decays[h : h + 1, :DH]
        - dot(mats[:, :DH], state)
        + mats[:, DH:].astype(F32)
    )


def gather_kernel(sc_ref, p0, p1, p2, p3, in_ref, order_ref, out_ref):
    for offset, piece in enumerate((p0, p1, p2, p3)):
        order_ref[sc_ref[1] ^ offset] = piece[...]
    for h in range(PIECE):
        state = in_ref[h]
        for chip in range(CHIPS):
            state = advance(order_ref, chip, h, state).astype(BF16)
        out_ref[h] = state


def spread_kernel(sc_ref, order_ref, in_ref, o0, o1, o2, o3, scr):
    for h in range(PIECE):
        state = in_ref[h]
        for chip in range(CHIPS):
            scr[chip, h] = state
            if chip < CHIPS - 1:
                state = advance(order_ref, chip, h, state).astype(BF16)
    for offset, out in enumerate((o0, o1, o2, o3)):
        out[...] = scr[sc_ref[1] ^ offset]


def scalar_call(kernel, place, args, out_shape, scratch=(), name=None):
    vmem = pl.BlockSpec(memory_space=pltpu.VMEM)
    return pl.pallas_call(
        kernel,
        out_shape=out_shape,
        in_specs=[pl.BlockSpec(memory_space=pltpu.SMEM)] + [vmem] * len(args),
        out_specs=jax.tree.map(lambda _: vmem, out_shape),
        scratch_shapes=list(scratch),
        cost_estimate=pl.CostEstimate(flops=100_000_000, bytes_accessed=2_000_000, transcendentals=0),
        name=name,
    )(place, *args)


def enter_kernel(sc_ref, mine_ref, theirs_ref, p0, p1, p2, p3, keep_ref, send_ref, scr):
    for offset, piece in enumerate((p0, p1, p2, p3)):
        scr[sc_ref[1] ^ offset] = piece[...]

    def finish(first_ref, start_ref, next_ref):
        for i in range(CHIPS):
            for h in range(PIECE):
                start = scr[i, h]
                start_ref[i, h] = start
                next_ref[i, h] = advance(first_ref, i, h, start).astype(BF16)

    @pl.when(sc_ref[0] == 0)
    def _():
        finish(mine_ref, keep_ref, send_ref)

    @pl.when(sc_ref[0] == 1)
    def _():
        finish(theirs_ref, send_ref, keep_ref)


def finish_kernel(sc_ref, loc_ref, car_ref, state_ref, gate_ref, gain_ref, *refs):
    out_ref = refs[-1]
    for h in range(PIECE):
        state = state_ref[0, h]
        core = loc_ref[0, h] + dot(car_ref[0, h], jnp.concatenate([state, state], axis=0))
        mean_sq = jnp.mean(core * core, axis=1, keepdims=True)
        gate = gate_ref[:, head_slice(h)].astype(F32)
        scaled = core * lax.rsqrt(mean_sq + 1e-06) * gain_ref[...] * (gate / (1.0 + jnp.exp(-gate)))
        out_ref[:, head_slice(h)] = scaled.astype(BF16)


def finish(owner, local_out, carry_map, state, gate_in, gain, so_far):
    pieces = VH // 2 // PIECE
    cols = pl.BlockSpec((CH, PIECE * DH), lambda i, sc: (0, pieces * sc[0] + i))
    in_specs = [
        pl.BlockSpec((1, PIECE, CH, DH), lambda i, sc: (i, 0, 0, 0)),
        pl.BlockSpec((1, PIECE, CH, WIDE), lambda i, sc: (i, 0, 0, 0)),
        pl.BlockSpec((1, PIECE, DH, DH), lambda i, sc: (i, 0, 0, 0)),
        cols,
        pl.BlockSpec((1, DH), lambda i, sc: (0, 0)),
    ]
    args = [owner, local_out, carry_map, state, gate_in, gain]
    aliases = {}
    if so_far is not None:
        in_specs.append(pl.BlockSpec(memory_space=pl.ANY))
        aliases = {len(args): 0}
        args.append(so_far)
    return pl.pallas_call(
        finish_kernel,
        out_shape=jax.ShapeDtypeStruct(gate_in.shape, BF16),
        grid_spec=pltpu.PrefetchScalarGridSpec(
            num_scalar_prefetch=1, grid=(pieces,), in_specs=in_specs, out_specs=cols
        ),
        input_output_aliases=aliases,
        cost_estimate=pl.CostEstimate(flops=300_000_000, bytes_accessed=4_000_000, transcendentals=0),
        name="finish",
    )(*args)


def shift(block, distance):
    count = lax.axis_size("seq")
    return lax.ppermute(block, "seq", [(i, i + distance) for i in range(count - distance)])


def swap(block, distance):
    return lax.ppermute(block, "seq", [(i, i ^ distance) for i in range(lax.axis_size("seq"))])


def level_masks():
    t_at = lax.broadcasted_iota(jnp.int32, (7, CH, CH), 1)
    s_at = lax.broadcasted_iota(jnp.int32, (7, CH, CH), 2)
    level = lax.broadcasted_iota(jnp.int32, (7, CH, CH), 0)
    return ((t_at > s_at) & ((t_at ^ s_at) >> level == 1)).astype(BF16)


def local(mixed_qkv, conv_weight, beta_logit, log_decay, gate_in, norm_gain):
    at = lax.axis_index("seq")
    core, chip = at % 2, (at // 2) % CHIPS
    rim = shift(mixed_qkv[CH - 8 :], 1)
    mine_at, theirs_at = core[None], (1 - core)[None]
    place = jnp.stack([core, chip])

    upper = jnp.triu(jnp.ones((CH, CH), F32))
    cumulative = jnp.einsum("sh,st->ht", log_decay, upper, precision=lax.Precision.HIGHEST)
    beta = jax.nn.sigmoid(beta_logit.astype(F32)).T
    rows = jnp.concatenate(
        [cumulative.reshape(-1, PIECE, CH), beta.reshape(-1, PIECE, CH)], axis=1
    )
    masks = level_masks()

    theirs_ma, theirs_loc, theirs_car = block_terms(
        theirs_at, mixed_qkv, rim, conv_weight, rows, masks
    )
    other_ma = swap(theirs_ma, 1)
    mine_ma, mine_loc, mine_car = block_terms(mine_at, mixed_qkv, rim, conv_weight, rows, masks)

    sent = [compose(place, mine_ma, other_ma, offset) for offset in range(CHIPS)]
    pieces = [sent[0]] + [swap(sent[offset], 2 * offset) for offset in range(1, CHIPS)]

    state_shape = jax.ShapeDtypeStruct((PIECE, DH, DH), BF16)
    order_shape = jax.ShapeDtypeStruct((CHIPS, ROWS, WIDE), BF16)
    entering = jnp.zeros((PIECE, DH, DH), BF16)
    for _ in range(lax.axis_size("seq") // (2 * CHIPS) - 1):
        order, leaving = scalar_call(
            gather_kernel, place, [*pieces, entering], [order_shape, state_shape], name="gather"
        )
        entering = shift(leaving, 2 * CHIPS)
    spread = scalar_call(
        spread_kernel,
        place,
        [order, entering],
        [state_shape] * CHIPS,
        [pltpu.VMEM((CHIPS, PIECE, DH, DH), BF16)],
        name="spread",
    )
    starts = [spread[0]] + [swap(spread[offset], 2 * offset) for offset in range(1, CHIPS)]
    states_shape = jax.ShapeDtypeStruct((CHIPS, PIECE, DH, DH), BF16)
    keep, send = scalar_call(
        enter_kernel,
        place,
        [mine_ma, other_ma, *starts],
        [states_shape, states_shape],
        [pltpu.VMEM((CHIPS, PIECE, DH, DH), BF16)],
        name="enter",
    )
    given = swap(send, 1)
    gain = norm_gain[None]
    out = finish(mine_at, mine_loc, mine_car, keep, gate_in, gain, None)
    return finish(theirs_at, theirs_loc, theirs_car, given, gate_in, gain, out)


def solution(mesh):
    spec = P(("groups", "seq"), None)
    return jax.shard_map(
        local,
        mesh=mesh,
        in_specs=(spec, P(), spec, spec, spec, P()),
        out_specs=spec,
        check_vma=False,
    )
```

time: 580 us -> 99.8 us (0.17)
  the two profiles are of different devices: /device:TPU:13 before, /device:TPU:0 now
where the time goes in v1:
time: 99.8 us; the launch traced here: 99.1 us
  Pallas kernels  54.4 us (55%)
  starting transfers between devices  19.6 us (20%)
  waiting for transfers between devices  16.7 us (17%)
  local copies, waits for them, and re-layouts  5.44 us (5%)
  other arithmetic  2.67 us (3%)
    pallas_call x2, Pallas kernels, block_terms(): pl.pallas_call(terms_kernel, out_shape=[jax.ShapeDtypeStruct((pieces, ROW...  26 us
    ppermute x8, waiting for transfers between devices, swap(): lax.ppermute(block, 'seq', [(i, i ^ distance) for i in range(lax.axis_siz...  13.9 us
    ppermute x8, starting transfers between devices, swap(): lax.ppermute(block, 'seq', [(i, i ^ distance) for i in range(lax.axis_siz...  12.6 us
    pallas_call x4, Pallas kernels, compose(): pl.pallas_call(compose_kernel, out_shape=jax.ShapeDtypeStruct((ROWS, WIDE...  10.6 us
    pallas_call x3, Pallas kernels, scalar_call(): pl.pallas_call(kernel, out_shape=out_shape, in_specs=[pl.BlockSpec(memory...  9.46 us
    pallas_call x2, Pallas kernels, finish(): pl.pallas_call(finish_kernel, out_shape=jax.ShapeDtypeStruct(gate_in.shap...  8.41 us
    ppermute x2, starting transfers between devices, shift(): lax.ppermute(block, 'seq', [(i, i + distance) for i in range(count - dist...  7.01 us
    unnamed x22, local copies, waits for them, and re-layouts  3.78 us
  transfers between devices with their start and end apart: 10, of which 5 were waited for; matrix products, arithmetic and copies ran while one was open for 3% of the time, Pallas kernels for 25%

profile of v1, /device:TPU:0, one launch (start us, length us, event | category | flops | bytes accessed | tf_op | source)
XLA Modules:
  0.0 99.1 jit_solution(17064643035691262074)
XLA Ops:
  0.0 0.9 slice.3
  0.9 2.4 %collective-permute-start = (bf16[8,8192]{1,0:T(8,128)(2,1)S(1)}, bf16[8,8192]{1,0:T(8,128)(2,1)S(1)}, u32[]{:S(2)}, u32[]{:S(2)}) collective-permute-start(bf16[8,8192]{1,0:T(8,128)(2,1)S(1)} %slice.3), channel_id=1, source_target_pairs={{0,1},{1,2},{2,3},{3,4},{4,5},{5,6},{6,7},{7,8},{8,9},{9,10},{10,1... | collective-permute-start | bytes 393224 | tf_op jit(solution)/shard_map/ppermute | solution.py:322
  3.3 0.7 add_divide_fusion
  4.9 0.8 fusion.3.masks_ref
  5.7 0.6 copy-done.10
  6.3 13.0 %block_terms.2 = (bf16[4,528,256]{2,1,0:T(8,128)(2,1)}, f32[4,4,128,128]{3,2,1,0:T(8,128)}, bf16[4,4,128,256]{3,2,1,0:T(8,128)(2,1)}) custom-call(s32[1]{0:T(128)} %bitcast.sc_ref, bf16[128,8192]{1,0:T(8,128)(2,1)} %xv.3, bf16[128,8192]{1,0:T(8,128)(2,1)} %xv.3, bf16[128,8192]{1,0:T(8,128)(2,1)} %xv.3, bf16[8,8192]{1,0:T(8,128)(2,1)} %copy-done.10, ...), custom_call_target="tpu_custom_call" | custom-call | flops 2000000000 | bytes 6000000 | tf_op jit(solution)/shard_map/block_terms/pallas_call | solution.py:152
  19.3 2.7 %collective-permute-start.1 = (bf16[4,528,256]{2,1,0:T(8,128)(2,1)}, bf16[4,528,256]{2,1,0:T(8,128)(2,1)S(1)}, u32[]{:S(2)}, u32[]{:S(2)}) collective-permute-start(bf16[4,528,256]{2,1,0:T(8,128)(2,1)} %get-tuple-element.22), channel_id=1, source_target_pairs={{0,1},{1,0},{2,3},{3,2},{4,5},{5,4},{6,7},{7,6},{8,9},{9,8},{10,11... | collective-permute-start | bytes 3244040 | tf_op jit(solution)/shard_map/ppermute | solution.py:326
  22.6 13.0 %block_terms.3 = (bf16[4,528,256]{2,1,0:T(8,128)(2,1)}, f32[4,4,128,128]{3,2,1,0:T(8,128)}, bf16[4,4,128,256]{3,2,1,0:T(8,128)(2,1)}) custom-call(s32[1]{0:T(128)} %bitcast.5.sc_ref, bf16[128,8192]{1,0:T(8,128)(2,1)} %xv.3, bf16[128,8192]{1,0:T(8,128)(2,1)} %xv.3, bf16[128,8192]{1,0:T(8,128)(2,1)} %xv.3, bf16[8,8192]{1,0:T(8,128)(2,1)} %copy-done.10, ...), custom_call_target="tpu_custom_call" | custom-call | flops 2000000000 | bytes 6000000 | tf_op jit(solution)/shard_map/block_terms/pallas_call | solution.py:152
  35.6 1.0 copy-done.1
  36.5 2.6 %compose.5 = bf16[528,256]{1,0:T(8,128)(2,1)} custom-call(s32[2]{0:T(128)} %pad_add_fusion.sc_ref, bf16[4,528,256]{2,1,0:T(8,128)(2,1)} %get-tuple-element.21.mine_ref, bf16[4,528,256]{2,1,0:T(8,128)(2,1)} %copy-done.1), custom_call_target="tpu_custom_call" | custom-call | flops 40000000 | bytes 900000 | tf_op jit(solution)/shard_map/compose/pallas_call | solution.py:203
  39.2 1.9 %collective-permute-start.2 = (bf16[528,256]{1,0:T(8,128)(2,1)}, bf16[528,256]{1,0:T(8,128)(2,1)S(1)}, u32[]{:S(2)}, u32[]{:S(2)}) collective-permute-start(bf16[528,256]{1,0:T(8,128)(2,1)} %compose.5), channel_id=1, source_target_pairs={{0,2},{1,3},{2,0},{3,1},{4,6},{5,7},{6,4},{7,5},{8,10},{9,11},{10,... | collective-permute-start | bytes 811016 | tf_op jit(solution)/shard_map/ppermute | solution.py:326
  41.1 2.7 %compose.6 = bf16[528,256]{1,0:T(8,128)(2,1)} custom-call(s32[2]{0:T(128)} %pad_add_fusion.sc_ref, bf16[4,528,256]{2,1,0:T(8,128)(2,1)} %get-tuple-element.21.mine_ref, bf16[4,528,256]{2,1,0:T(8,128)(2,1)} %copy-done.1), custom_call_target="tpu_custom_call" | custom-call | flops 40000000 | bytes 900000 | tf_op jit(solution)/shard_map/compose/pallas_call | solution.py:203
  43.8 1.6 %collective-permute-start.3 = (bf16[528,256]{1,0:T(8,128)(2,1)}, bf16[528,256]{1,0:T(8,128)(2,1)S(1)}, u32[]{:S(2)}, u32[]{:S(2)}) collective-permute-start(bf16[528,256]{1,0:T(8,128)(2,1)} %compose.6), channel_id=1, source_target_pairs={{0,4},{1,5},{2,6},{3,7},{4,0},{5,1},{6,2},{7,3},{8,12},{9,13},{10,... | collective-permute-start | bytes 811016 | tf_op jit(solution)/shard_map/ppermute | solution.py:326
  45.3 2.6 %compose.7 = bf16[528,256]{1,0:T(8,128)(2,1)} custom-call(s32[2]{0:T(128)} %pad_add_fusion.sc_ref, bf16[4,528,256]{2,1,0:T(8,128)(2,1)} %get-tuple-element.21.mine_ref, bf16[4,528,256]{2,1,0:T(8,128)(2,1)} %copy-done.1), custom_call_target="tpu_custom_call" | custom-call | flops 40000000 | bytes 900000 | tf_op jit(solution)/shard_map/compose/pallas_call | solution.py:203
  48.0 0.8 collective-permute-start.4
  48.8 2.6 %compose.4.p0 = bf16[528,256]{1,0:T(8,128)(2,1)} custom-call(s32[2]{0:T(128)} %pad_add_fusion.sc_ref, bf16[4,528,256]{2,1,0:T(8,128)(2,1)} %get-tuple-element.21.mine_ref, bf16[4,528,256]{2,1,0:T(8,128)(2,1)} %copy-done.1), custom_call_target="tpu_custom_call" | custom-call | flops 40000000 | bytes 900000 | tf_op jit(solution)/shard_map/compose/pallas_call | solution.py:203
  51.5 1.8 %collective-permute-done.3.p2 = bf16[528,256]{1,0:T(8,128)(2,1)S(1)} collective-permute-done((bf16[528,256]{1,0:T(8,128)(2,1)}, bf16[528,256]{1,0:T(8,128)(2,1)S(1)}, u32[]{:S(2)}, u32[]{:S(2)}) %collective-permute-start.3) | collective-permute-done | bytes 270368 | tf_op jit(solution)/shard_map/ppermute | solution.py:326
  53.3 5.7 %collective-permute-done.4.p3 = bf16[528,256]{1,0:T(8,128)(2,1)S(1)} collective-permute-done((bf16[528,256]{1,0:T(8,128)(2,1)}, bf16[528,256]{1,0:T(8,128)(2,1)S(1)}, u32[]{:S(2)}, u32[]{:S(2)}) %collective-permute-start.4) | collective-permute-done | bytes 270368 | tf_op jit(solution)/shard_map/ppermute | solution.py:326
  59.0 0.7 broadcast_in_dim.20.in_ref
  59.8 3.4 %gather.1 = (bf16[4,528,256]{2,1,0:T(8,128)(2,1)}, bf16[4,128,128]{2,1,0:T(8,128)(2,1)}) custom-call(s32[2]{0:T(128)} %pad_add_fusion.sc_ref, bf16[528,256]{1,0:T(8,128)(2,1)} %compose.4.p0, bf16[528,256]{1,0:T(8,128)(2,1)} %copy-done.3, bf16[528,256]{1,0:T(8,128)(2,1)} %copy-done.4, bf16[528,256]{1,0:T(8,128)(2,1)} %copy-done.5, ...), custom_call_target="tpu_custom_call" | custom-call | flops 100000000 | bytes 2000000 | tf_op jit(solution)/shard_map/gather/pallas_call | solution.py:250
  63.2 4.7 %collective-permute-start.5 = (bf16[4,128,128]{2,1,0:T(8,128)(2,1)}, bf16[4,128,128]{2,1,0:T(8,128)(2,1)S(1)}, u32[]{:S(2)}, u32[]{:S(2)}) collective-permute-start(bf16[4,128,128]{2,1,0:T(8,128)(2,1)} %get-tuple-element.24), channel_id=1, source_target_pairs={{0,8},{1,9},{2,10},{3,11},{4,12},{5,13},{6,14},{7,15},{16,24},{17,... | collective-permute-start | bytes 393224 | tf_op jit(solution)/shard_map/ppermute | solution.py:322
  67.9 2.8 %collective-permute-done.5.in_ref = bf16[4,128,128]{2,1,0:T(8,128)(2,1)S(1)} collective-permute-done((bf16[4,128,128]{2,1,0:T(8,128)(2,1)}, bf16[4,128,128]{2,1,0:T(8,128)(2,1)S(1)}, u32[]{:S(2)}, u32[]{:S(2)}) %collective-permute-start.5) | collective-permute-done | bytes 131104 | tf_op jit(solution)/shard_map/ppermute | solution.py:322
  70.7 0.7 copy-done.9
  71.3 2.9 %spread.1 = (bf16[4,128,128]{2,1,0:T(8,128)(2,1)}, bf16[4,128,128]{2,1,0:T(8,128)(2,1)}, bf16[4,128,128]{2,1,0:T(8,128)(2,1)}, bf16[4,128,128]{2,1,0:T(8,128)(2,1)}) custom-call(s32[2]{0:T(128)} %pad_add_fusion.sc_ref, bf16[4,528,256]{2,1,0:T(8,128)(2,1)} %get-tuple-element.23.order_ref, bf16[4,128,128]{2,1,0:T(8,128)(2,1)} %copy-done.9), custom_call_target="tpu_custom_call" | custom-call | flops 100000000 | bytes 2000000 | tf_op jit(solution)/shard_map/spread/pallas_call | solution.py:250
  74.9 4.1 %collective-permute-start.7 = (bf16[4,128,128]{2,1,0:T(8,128)(2,1)}, bf16[4,128,128]{2,1,0:T(8,128)(2,1)S(1)}, u32[]{:S(2)}, u32[]{:S(2)}) collective-permute-start(bf16[4,128,128]{2,1,0:T(8,128)(2,1)} %get-tuple-element.27), channel_id=1, source_target_pairs={{0,4},{1,5},{2,6},{3,7},{4,0},{5,1},{6,2},{7,3},{8,12},{9,13},{10,... | collective-permute-start | bytes 393224 | tf_op jit(solution)/shard_map/ppermute | solution.py:326
  78.9 0.9 collective-permute-start.8
  79.8 3.4 %collective-permute-done.7.p2 = bf16[4,128,128]{2,1,0:T(8,128)(2,1)S(1)} collective-permute-done((bf16[4,128,128]{2,1,0:T(8,128)(2,1)}, bf16[4,128,128]{2,1,0:T(8,128)(2,1)S(1)}, u32[]{:S(2)}, u32[]{:S(2)}) %collective-permute-start.7) | collective-permute-done | bytes 131104 | tf_op jit(solution)/shard_map/ppermute | solution.py:326
  83.2 2.9 %collective-permute-done.8.p3 = bf16[4,128,128]{2,1,0:T(8,128)(2,1)S(1)} collective-permute-done((bf16[4,128,128]{2,1,0:T(8,128)(2,1)}, bf16[4,128,128]{2,1,0:T(8,128)(2,1)S(1)}, u32[]{:S(2)}, u32[]{:S(2)}) %collective-permute-start.8) | collective-permute-done | bytes 131104 | tf_op jit(solution)/shard_map/ppermute | solution.py:326
  86.8 3.1 %enter.1 = (bf16[4,4,128,128]{3,2,1,0:T(8,128)(2,1)}, bf16[4,4,128,128]{3,2,1,0:T(8,128)(2,1)}) custom-call(s32[2]{0:T(128)} %pad_add_fusion.sc_ref, bf16[4,528,256]{2,1,0:T(8,128)(2,1)} %get-tuple-element.21.mine_ref, bf16[4,528,256]{2,1,0:T(8,128)(2,1)} %copy-done.1, bf16[4,128,128]{2,1,0:T(8,128)(2,1)} %get-tuple-element.25.p0, ...), custom_call_target="tpu_custom_call" | custom-call | flops 100000000 | bytes 2000000 | tf_op jit(solution)/shard_map/enter/pallas_call | solution.py:250
  89.9 4.2 %finish.2.refs_0_ = bf16[128,4096]{1,0:T(8,128)(2,1)} custom-call(s32[1]{0:T(128)} %bitcast.5.sc_ref, f32[4,4,128,128]{3,2,1,0:T(8,128)} %get-tuple-element.30.loc_ref, bf16[4,4,128,256]{3,2,1,0:T(8,128)(2,1)} %get-tuple-element.31.car_ref, bf16[4,4,128,128]{3,2,1,0:T(8,128)(2,1)} %get-tuple-element.32.state_ref, bf16[128,4096]{1,0:T(8,128)(2,1)} %gate_ref.3, ...), custom_call_target="tpu_custom_call" | custom-call | flops 300000000 | bytes 4000000 | tf_op jit(solution)/shard_map/finish/pallas_call | solution.py:308
  94.1 0.8 copy-done.2
  94.9 4.2 %finish.3 = bf16[128,4096]{1,0:T(8,128)(2,1)} custom-call(s32[1]{0:T(128)} %bitcast.sc_ref, f32[4,4,128,128]{3,2,1,0:T(8,128)} %get-tuple-element.19.loc_ref, bf16[4,4,128,256]{3,2,1,0:T(8,128)(2,1)} %get-tuple-element.20.car_ref, bf16[4,4,128,128]{3,2,1,0:T(8,128)(2,1)} %copy-done.2, bf16[128,4096]{1,0:T(8,128)(2,1)} %gate_ref.3, ...), custom_call_target="tpu_custom_call", output_to_operand_aliasing={{}: (6, {})} | custom-call | flops 300000000 | bytes 4000000 | tf_op jit(solution)/shard_map/finish/pallas_call | solution.py:308
  (29 shorter events, 2.8 us)
Async XLA Ops:
  0.0 4.0 %copy-start = (f32[128,32]{0,1:T(8,128)S(1)}, f32[128,32]{0,1:T(8,128)}, u32[]{:S(2)}) copy-start(f32[128,32]{0,1:T(8,128)} %param.9) | copy-start | bytes 49156
  0.9 4.7 %collective-permute-start = (bf16[8,8192]{1,0:T(8,128)(2,1)S(1)}, bf16[8,8192]{1,0:T(8,128)(2,1)S(1)}, u32[]{:S(2)}, u32[]{:S(2)}) collective-permute-start(bf16[8,8192]{1,0:T(8,128)(2,1)S(1)} %slice.3), channel_id=1, source_target_pairs={{0,1},{1,2},{2,3},{3,4},{4,5},{5,6},{6,7},{7,8},{8,9},{9,10},{10,1... | collective-permute-start | bytes 393224 | tf_op jit(solution)/shard_map/ppermute | solution.py:322
  5.7 0.6 copy-start.10
  19.3 16.3 %collective-permute-start.1 = (bf16[4,528,256]{2,1,0:T(8,128)(2,1)}, bf16[4,528,256]{2,1,0:T(8,128)(2,1)S(1)}, u32[]{:S(2)}, u32[]{:S(2)}) collective-permute-start(bf16[4,528,256]{2,1,0:T(8,128)(2,1)} %get-tuple-element.22), channel_id=1, source_target_pairs={{0,1},{1,0},{2,3},{3,2},{4,5},{5,4},{6,7},{7,6},{8,9},{9,8},{10,11... | collective-permute-start | bytes 3244040 | tf_op jit(solution)/shard_map/ppermute | solution.py:326
  35.6 1.0 copy-start.1
  39.2 12.3 %collective-permute-start.2 = (bf16[528,256]{1,0:T(8,128)(2,1)}, bf16[528,256]{1,0:T(8,128)(2,1)S(1)}, u32[]{:S(2)}, u32[]{:S(2)}) collective-permute-start(bf16[528,256]{1,0:T(8,128)(2,1)} %compose.5), channel_id=1, source_target_pairs={{0,2},{1,3},{2,0},{3,1},{4,6},{5,7},{6,4},{7,5},{8,10},{9,11},{10,... | collective-permute-start | bytes 811016 | tf_op jit(solution)/shard_map/ppermute | solution.py:326
  43.8 9.5 %collective-permute-start.3 = (bf16[528,256]{1,0:T(8,128)(2,1)}, bf16[528,256]{1,0:T(8,128)(2,1)S(1)}, u32[]{:S(2)}, u32[]{:S(2)}) collective-permute-start(bf16[528,256]{1,0:T(8,128)(2,1)} %compose.6), channel_id=1, source_target_pairs={{0,4},{1,5},{2,6},{3,7},{4,0},{5,1},{6,2},{7,3},{8,12},{9,13},{10,... | collective-permute-start | bytes 811016 | tf_op jit(solution)/shard_map/ppermute | solution.py:326
  48.0 11.0 %collective-permute-start.4 = (bf16[528,256]{1,0:T(8,128)(2,1)}, bf16[528,256]{1,0:T(8,128)(2,1)S(1)}, u32[]{:S(2)}, u32[]{:S(2)}) collective-permute-start(bf16[528,256]{1,0:T(8,128)(2,1)} %compose.7), channel_id=1, source_target_pairs={{0,6},{1,7},{2,4},{3,5},{4,2},{5,3},{6,0},{7,1},{8,14},{9,15},{10,... | collective-permute-start | bytes 811016 | tf_op jit(solution)/shard_map/ppermute | solution.py:326
  51.5 8.3 %copy-start.3 = (bf16[528,256]{1,0:T(8,128)(2,1)}, bf16[528,256]{1,0:T(8,128)(2,1)S(1)}, u32[]{:S(2)}) copy-start(bf16[528,256]{1,0:T(8,128)(2,1)S(1)} %collective-permute-done.2.p1) | copy-start | bytes 811012
  53.3 6.5 %copy-start.4 = (bf16[528,256]{1,0:T(8,128)(2,1)}, bf16[528,256]{1,0:T(8,128)(2,1)S(1)}, u32[]{:S(2)}) copy-start(bf16[528,256]{1,0:T(8,128)(2,1)S(1)} %collective-permute-done.3.p2) | copy-start | bytes 811012
  59.0 0.8 copy-start.5
  63.2 7.5 %collective-permute-start.5 = (bf16[4,128,128]{2,1,0:T(8,128)(2,1)}, bf16[4,128,128]{2,1,0:T(8,128)(2,1)S(1)}, u32[]{:S(2)}, u32[]{:S(2)}) collective-permute-start(bf16[4,128,128]{2,1,0:T(8,128)(2,1)} %get-tuple-element.24), channel_id=1, source_target_pairs={{0,8},{1,9},{2,10},{3,11},{4,12},{5,13},{6,14},{7,15},{16,24},{17,... | collective-permute-start | bytes 393224 | tf_op jit(solution)/shard_map/ppermute | solution.py:322
  70.7 0.7 copy-start.9
  74.3 5.5 %collective-permute-start.6 = (bf16[4,128,128]{2,1,0:T(8,128)(2,1)}, bf16[4,128,128]{2,1,0:T(8,128)(2,1)S(1)}, u32[]{:S(2)}, u32[]{:S(2)}) collective-permute-start(bf16[4,128,128]{2,1,0:T(8,128)(2,1)} %get-tuple-element.26), channel_id=1, source_target_pairs={{0,2},{1,3},{2,0},{3,1},{4,6},{5,7},{6,4},{7,5},{8,10},{9,11},{10,... | collective-permute-start | bytes 393224 | tf_op jit(solution)/shard_map/ppermute | solution.py:326
  74.9 8.3 %collective-permute-start.7 = (bf16[4,128,128]{2,1,0:T(8,128)(2,1)}, bf16[4,128,128]{2,1,0:T(8,128)(2,1)S(1)}, u32[]{:S(2)}, u32[]{:S(2)}) collective-permute-start(bf16[4,128,128]{2,1,0:T(8,128)(2,1)} %get-tuple-element.27), channel_id=1, source_target_pairs={{0,4},{1,5},{2,6},{3,7},{4,0},{5,1},{6,2},{7,3},{8,12},{9,13},{10,... | collective-permute-start | bytes 393224 | tf_op jit(solution)/shard_map/ppermute | solution.py:326
  78.9 7.2 %collective-permute-start.8 = (bf16[4,128,128]{2,1,0:T(8,128)(2,1)}, bf16[4,128,128]{2,1,0:T(8,128)(2,1)S(1)}, u32[]{:S(2)}, u32[]{:S(2)}) collective-permute-start(bf16[4,128,128]{2,1,0:T(8,128)(2,1)} %get-tuple-element.28), channel_id=1, source_target_pairs={{0,6},{1,7},{2,4},{3,5},{4,2},{5,3},{6,0},{7,1},{8,14},{9,15},{10,... | collective-permute-start | bytes 393224 | tf_op jit(solution)/shard_map/ppermute | solution.py:326
  79.8 6.3 %copy-start.6 = (bf16[4,128,128]{2,1,0:T(8,128)(2,1)}, bf16[4,128,128]{2,1,0:T(8,128)(2,1)S(1)}, u32[]{:S(2)}) copy-start(bf16[4,128,128]{2,1,0:T(8,128)(2,1)S(1)} %collective-permute-done.6.p1) | copy-start | bytes 393220
  83.2 2.9 %copy-start.7 = (bf16[4,128,128]{2,1,0:T(8,128)(2,1)}, bf16[4,128,128]{2,1,0:T(8,128)(2,1)S(1)}, u32[]{:S(2)}) copy-start(bf16[4,128,128]{2,1,0:T(8,128)(2,1)S(1)} %collective-permute-done.7.p2) | copy-start | bytes 393220
  86.1 0.6 copy-start.8
  89.9 4.2 %collective-permute-start.9 = (bf16[4,4,128,128]{3,2,1,0:T(8,128)(2,1)}, bf16[4,4,128,128]{3,2,1,0:T(8,128)(2,1)S(1)}, u32[]{:S(2)}, u32[]{:S(2)}) collective-permute-start(bf16[4,4,128,128]{3,2,1,0:T(8,128)(2,1)} %get-tuple-element.29), channel_id=1, source_target_pairs={{0,1},{1,0},{2,3},{3,2},{4,5},{5,4},{6,7},{7,6},{8,9},{9,8},{10,11... | collective-permute-start | bytes 1572872 | tf_op jit(solution)/shard_map/ppermute | solution.py:326
  94.1 0.8 copy-start.2

commit v2 on v0

v2 whole, which is shorter than its diff:
```python
import functools

import jax
import jax.numpy as jnp
import ml_dtypes
import numpy as np
from jax import lax
from jax.experimental import pallas as pl
from jax.experimental.pallas import tpu as pltpu
from jax.sharding import PartitionSpec as P

KH = 16
VH = 32
DH = 128
CH = 128
CHIPS = 4
PIECE = 4
BANDS = ((0, 1),)
WIDE = 2 * DH

F32 = jnp.float32
BF16 = jnp.bfloat16


def dot(a, b):
    return jnp.dot(a, b, preferred_element_type=F32)


def halves(x):
    high = x.astype(BF16)
    return high, (x - high.astype(F32)).astype(BF16)


def decay_rows(decays):
    high, low = halves(decays)
    return jnp.concatenate([high, low], axis=0)


def rows_of(keys):
    return 2 * len(keys) * DH + 16


def decays_of(rows):
    rows = rows.astype(F32)
    return rows[:8] + rows[8:]


def head_slice(h):
    return slice(h * DH, (h + 1) * DH)


def rows_kernel(decay_ref, logit_ref, rows_ref):
    s_at = lax.broadcasted_iota(jnp.int32, (CH, CH), 0)
    t_at = lax.broadcasted_iota(jnp.int32, (CH, CH), 1)
    cumulative = jnp.dot(
        decay_ref[...],
        (s_at <= t_at).astype(F32),
        precision=lax.Precision.HIGHEST,
        preferred_element_type=F32,
    )
    beta = 1.0 / (1.0 + jnp.exp(-logit_ref[...].astype(F32)))
    for g in range(VH // PIECE):
        rows_ref[g, :PIECE] = cumulative[g * PIECE : (g + 1) * PIECE]
        rows_ref[g, PIECE:] = beta[g * PIECE : (g + 1) * PIECE]


def taps(padded, w, height):
    total = padded(0) * w[0:1]
    for tap in range(1, 4):
        total = total + padded(tap) * w[tap : tap + 1]
    return (total / (1.0 + jnp.exp(-total))).astype(BF16)


def conv_kernel(sc_ref, x_ref, w_ref, out_ref, scr):
    scr[...] = x_ref[...].astype(F32)
    w = w_ref[...].astype(F32)
    out_ref[8:] = taps(lambda tap: scr[5 + tap : 5 + tap + CH - 8, :], w, CH - 8)


def early_conv(place, mixed_qkv, conv_weight):
    width = 512
    keys, values = KH // 2 * DH // width, VH // 2 * DH // width

    def at(i, sc):
        owner = 1 - sc[0]
        key_at = KH * DH // width + owner * keys + i
        value_at = 2 * KH * DH // width + owner * values + i - keys
        return (0, jnp.where(i < keys, key_at, value_at))

    tall = pl.BlockSpec((CH, width), at)
    return pl.pallas_call(
        conv_kernel,
        out_shape=jax.ShapeDtypeStruct(mixed_qkv.shape, BF16),
        grid_spec=pltpu.PrefetchScalarGridSpec(
            num_scalar_prefetch=1,
            grid=(keys + values,),
            in_specs=[tall, pl.BlockSpec((conv_weight.shape[0], width), at)],
            out_specs=tall,
            scratch_shapes=[pltpu.VMEM((CH, width), F32)],
        ),
        cost_estimate=pl.CostEstimate(flops=10_000_000, bytes_accessed=2_000_000, transcendentals=0),
        compiler_params=pltpu.CompilerParams(vmem_limit_bytes=8 << 20),
        name="conv",
    )(place, mixed_qkv, conv_weight)


def convolved(x_ref, rim_ref, w_ref, scr, slot, column, width, conv_ref=None):
    cols = pl.ds(pl.multiple_of(column, DH), width)
    w = w_ref[:, cols].astype(F32)
    scr[slot, 0:8, :width] = rim_ref[:, cols].astype(F32)
    if conv_ref is None:
        scr[slot, 8 : 8 + CH, :width] = x_ref[:, cols].astype(F32)
        return taps(lambda tap: scr[slot, 5 + tap : 5 + tap + CH, :width], w, CH).astype(F32)
    scr[slot, 8:16, :width] = x_ref[:8, cols].astype(F32)
    first = taps(lambda tap: scr[slot, 5 + tap : 13 + tap, :width], w, 8)
    rest = conv_ref[:, cols].astype(F32)
    return jnp.concatenate([first.astype(F32), rest[8:]], axis=0)


def inverse_norms(rows, axis):
    return lax.rsqrt(jnp.sum(rows * rows, axis=axis, keepdims=True) + 1e-06)


def decay_pairs(rows, cols, h, lower):
    gap = jnp.minimum(cols[:, h : h + 1] - rows[h : h + 1], 0.0)
    return jnp.where(lower, jnp.exp(gap), 0.0)


def token_order():
    t_at = lax.broadcasted_iota(jnp.int32, (CH, CH), 0)
    s_at = lax.broadcasted_iota(jnp.int32, (CH, CH), 1)
    return t_at, s_at


def terms_kernel(keys, sc_ref, x_ref, rim_ref, w_ref, conv_ref, rows_ref, masks_ref, *refs):
    theirs_refs, mine_refs, scr = refs[:3], refs[3:6], refs[6]
    t_at, s_at = token_order()
    lower, strict = t_at >= s_at, t_at > s_at
    unit = (t_at == s_at).astype(F32)
    pieces = VH // 2 // PIECE
    kd, vd = len(keys) * DH, 2 * len(keys) * DH

    heads = []
    slot = 0
    for own, (ma_ref, solved_ref, key_ref) in enumerate((theirs_refs, mine_refs)):
        owner = sc_ref[0] if own else 1 - sc_ref[0]
        conv = functools.partial(
            convolved, x_ref, rim_ref, w_ref, scr, conv_ref=None if own else conv_ref
        )
        for offset in range(CHIPS):
            piece = owner * pieces + (sc_ref[1] ^ offset)
            key_at = piece * PIECE // 2 + keys[0]
            ck = conv(slot, (KH + key_at) * DH, kd)
            cv = conv(slot + 1, 2 * (KH + key_at) * DH, vd)
            slot += 2
            rows = rows_ref[piece]
            cols = rows.T
            grow_cols = jnp.exp(cols)
            tail_rows = jnp.exp(rows[:, CH - 1 : CH] - rows)
            ma_ref[offset, 2 * kd :, :] = decay_rows(
                jnp.broadcast_to(jnp.exp(rows[:, CH - 1 : CH]), (8, WIDE))
            )
            for g, key in enumerate(keys):
                k_f = ck[:, head_slice(g)]
                k_b = k_f.astype(BF16)
                key_ref[offset, g] = k_b
                k_t = k_f.T
                rk_col, rk_row = inverse_norms(k_f, 1), inverse_norms(k_t, 0)
                key_dot = dot(k_b, k_t.astype(BF16)) * rk_col * rk_row
                for i in range(2):
                    h = 2 * key + i
                    pair = decay_pairs(rows, cols, h, lower)
                    system = jnp.where(strict, key_dot * pair * cols[:, 4 + h : 5 + h], 0.0)
                    heads.append(
                        dict(
                            out=(ma_ref, solved_ref, offset, 2 * g + i),
                            beta=rows[4 + h : 5 + h],
                            system=system.astype(BF16),
                            inv=halves(unit - system * masks_ref[0].astype(F32)),
                            value=cv[:, head_slice(2 * g + i)].astype(BF16),
                            key=(k_f * (grow_cols[:, h : h + 1] * rk_col)).astype(BF16),
                            tail=halves(k_t * (rk_row * tail_rows[h : h + 1])),
                        )
                    )

    for level in range(1, 7):
        mask = masks_ref[level]
        steps = [dot(p["inv"][0], p["system"] * mask).astype(BF16) for p in heads]
        steps = [halves(dot(s, p["inv"][0])) for s, p in zip(steps, heads)]
        for s, p in zip(steps, heads):
            p["inv"] = (p["inv"][0] - s[0], p["inv"][1] - s[1])

    for p in heads:
        inv = halves((p["inv"][0].astype(F32) + p["inv"][1].astype(F32)) * p["beta"])
        right = jnp.concatenate([p["key"], p["value"]], axis=1)
        p["solved"] = dot(
            jnp.concatenate(inv, axis=1), jnp.concatenate([right, right], axis=0)
        ).astype(BF16)
    for p in heads:
        ma_ref, solved_ref, offset, h = p["out"]
        solved = p["solved"]
        solved_ref[offset, h] = solved
        ma_ref[offset, head_slice(h), :] = dot(
            jnp.concatenate(p["tail"], axis=1), jnp.concatenate([solved, solved], axis=0)
        ).astype(BF16)


def local_call(
    kernel, args, out_shape, scratch=(), flops=100_000_000, vmem_mib=12, scalars=1, name=None
):
    vmem = pl.BlockSpec(memory_space=pltpu.VMEM)
    in_specs = [pl.BlockSpec(memory_space=pltpu.SMEM)] * scalars + [vmem] * (len(args) - scalars)
    return pl.pallas_call(
        kernel,
        out_shape=out_shape,
        in_specs=in_specs,
        out_specs=[vmem] * len(out_shape),
        scratch_shapes=list(scratch),
        cost_estimate=pl.CostEstimate(flops=flops, bytes_accessed=2_000_000, transcendentals=0),
        compiler_params=pltpu.CompilerParams(vmem_limit_bytes=vmem_mib << 20),
        name=name,
    )(*args)


def block_terms(keys, place, shared):
    outs = [
        jax.ShapeDtypeStruct((CHIPS, rows_of(keys), WIDE), BF16),
        jax.ShapeDtypeStruct((CHIPS, 2 * len(keys), CH, WIDE), BF16),
        jax.ShapeDtypeStruct((CHIPS, len(keys), CH, DH), BF16),
    ] * 2
    out = local_call(
        functools.partial(terms_kernel, keys),
        [place, *shared],
        outs,
        [pltpu.VMEM((4 * CHIPS, CH + 8, 2 * len(keys) * DH), F32)],
        vmem_mib=40,
        name="terms",
    )
    return out[:3], out[3:]


def compose_kernel(keys, sc_ref, mine_ref, other_ref, first_ref, *sent_refs):
    count = 2 * len(keys)
    is_first = sc_ref[0] == 0
    for offset in range(CHIPS):
        mine_g, theirs_g = decays_at(mine_ref, offset), decays_at(other_ref, offset)
        first_g = jnp.where(is_first, mine_g, theirs_g)
        second_g = jnp.where(is_first, theirs_g, mine_g)
        first_ref[offset, count * DH :, :] = decay_rows(first_g)
        sent_refs[offset][count * DH :, :] = decay_rows(first_g * second_g)
        for h in range(count):
            mine, theirs = mine_ref[offset, head_slice(h)], other_ref[offset, head_slice(h)]
            first = jnp.where(is_first, mine, theirs)
            second = jnp.where(is_first, theirs, mine)
            first_ref[offset, head_slice(h), :] = first
            product = dot(second[:, :DH], first)
            at = 2 * keys[0] + h
            kept = jnp.concatenate(
                [second[:, :DH].astype(F32) * first_g[at : at + 1, :DH], second[:, DH:].astype(F32)],
                axis=1,
            )
            sent_refs[offset][head_slice(h), :] = (
                first.astype(F32) * second_g[at : at + 1] - product + kept
            ).astype(BF16)


def compose(keys, place, mine, other):
    one = jax.ShapeDtypeStruct((rows_of(keys), WIDE), BF16)
    first, *sent = local_call(
        functools.partial(compose_kernel, keys),
        [place, mine, other],
        [jax.ShapeDtypeStruct(mine.shape, BF16)] + [one] * CHIPS,
        vmem_mib=16,
        name="compose",
    )
    return first, sent


def queries_kernel(keys, mine, sc_ref, x_ref, rim_ref, w_ref, rows_ref, solved_ref, key_ref, *refs):
    loc_ref, car_ref, scr = refs
    owner = sc_ref[0] if mine else 1 - sc_ref[0]
    t_at, s_at = token_order()
    heads = []
    for offset in range(CHIPS):
        piece = owner * (VH // 2 // PIECE) + (sc_ref[1] ^ offset)
        kd = len(keys) * DH
        key_at = piece * PIECE // 2 + keys[0]
        cq = convolved(x_ref, rim_ref, w_ref, scr, offset, key_at * DH, kd)
        rows = rows_ref[piece]
        cols = rows.T
        grow_cols = jnp.exp(cols)
        for g, key in enumerate(keys):
            q_f = cq[:, head_slice(g)]
            k_t = key_ref[offset, g].astype(F32).T
            rq_col = inverse_norms(q_f, 1) * DH ** (-0.5)
            query_dot = dot(q_f.astype(BF16), k_t.astype(BF16)) * rq_col * inverse_norms(k_t, 0)
            for i in range(2):
                h = 2 * key + i
                mixing = halves(query_dot * decay_pairs(rows, cols, h, t_at >= s_at))
                query = q_f * (grow_cols[:, h : h + 1] * rq_col)
                heads.append((offset, 2 * g + i, mixing, query))
    for offset, h, mixing, query in heads:
        solved = solved_ref[offset, h]
        both = dot(jnp.concatenate(mixing, axis=1), jnp.concatenate([solved, solved], axis=0))
        loc_ref[offset, h] = both[:, DH:]
        car_ref[offset, h] = jnp.concatenate(halves(query - both[:, :DH]), axis=1)


def block_queries(keys, mine, place, shared, solved, key_rows):
    count = 2 * len(keys)
    return local_call(
        functools.partial(queries_kernel, keys, mine),
        [place, *shared[:3], shared[4], solved, key_rows],
        [
            jax.ShapeDtypeStruct((CHIPS, count, CH, DH), F32),
            jax.ShapeDtypeStruct((CHIPS, count, CH, WIDE), BF16),
        ],
        [pltpu.VMEM((CHIPS, CH + 8, len(keys) * DH), F32)],
        vmem_mib=24,
        name="queries",
    )


def decays_at(ref, slot):
    return decays_of(ref[slot, ref.shape[1] - 16 :])


def advance(keys, ref, slot, h, decays, state):
    mats = ref[slot, head_slice(h)]
    at = 2 * keys[0] + h
    moved = state.astype(F32) * decays[at : at + 1, :DH] - dot(mats[:, :DH], state)
    return (moved + mats[:, DH:].astype(F32)).astype(BF16)


def gather_kernel(keys, sc_ref, p0, p1, p2, p3, in_ref, order_ref, out_ref):
    for offset, piece in enumerate((p0, p1, p2, p3)):
        order_ref[sc_ref[1] ^ offset] = piece[...]
    states = [in_ref[h] for h in range(2 * len(keys))]
    for chip in range(CHIPS):
        decays = decays_at(order_ref, chip)
        states = [advance(keys, order_ref, chip, h, decays, s) for h, s in enumerate(states)]
    for h, state in enumerate(states):
        out_ref[h] = state


def spread_kernel(keys, sc_ref, order_ref, in_ref, o0, o1, o2, o3, scr):
    states = [in_ref[h] for h in range(2 * len(keys))]
    for chip in range(CHIPS):
        for h, state in enumerate(states):
            scr[chip, h] = state
        if chip < CHIPS - 1:
            decays = decays_at(order_ref, chip)
            states = [advance(keys, order_ref, chip, h, decays, s) for h, s in enumerate(states)]
    for offset, out in enumerate((o0, o1, o2, o3)):
        out[...] = scr[sc_ref[1] ^ offset]


def enter_kernel(keys, sc_ref, first_ref, *refs):
    starts, (keep_ref, send_ref) = refs[:CHIPS], refs[CHIPS:]
    is_first = sc_ref[0] == 0
    for offset in range(CHIPS):
        decays = decays_at(first_ref, offset)
        for h in range(2 * len(keys)):
            start = starts[offset][h]
            after = advance(keys, first_ref, offset, h, decays, start)
            keep_ref[offset, h] = jnp.where(is_first, start, after)
            send_ref[offset, h] = jnp.where(is_first, after, start)


def finish_kernel(mine, sc_ref, gate_ref, gain_ref, *refs):
    bands = [refs[3 * b : 3 * b + 3] for b in range(len(BANDS))]
    out_ref, scr, sems = refs[-3:]
    owner = sc_ref[0] if mine else 1 - sc_ref[0]
    copies = []
    for offset in range(CHIPS):
        piece = owner * (VH // 2 // PIECE) + (sc_ref[1] ^ offset)
        cols = pl.ds(pl.multiple_of(piece * PIECE * DH, PIECE * DH), PIECE * DH)
        gates = gate_ref[:, cols].astype(F32)
        gates = gates / (1.0 + jnp.exp(-gates))
        at = 0
        for state_ref, loc_ref, car_ref in bands:
            for h in range(state_ref.shape[1]):
                state = state_ref[offset, h]
                core = loc_ref[offset, h] + dot(
                    car_ref[offset, h], jnp.concatenate([state, state], axis=0)
                )
                mean_sq = jnp.mean(core * core, axis=1, keepdims=True)
                scaled = core * lax.rsqrt(mean_sq + 1e-06) * gain_ref[...] * gates[:, head_slice(at)]
                scr[offset, :, head_slice(at)] = scaled.astype(BF16)
                at += 1
        copy = pltpu.make_async_copy(scr.at[offset], out_ref.at[:, cols], sems.at[offset])
        copy.start()
        copies.append(copy)
    for copy in copies:
        copy.wait()


def finish(mine, place, gate_in, gain, terms, so_far=None):
    vmem = pl.BlockSpec(memory_space=pltpu.VMEM)
    hbm = pl.BlockSpec(memory_space=pl.ANY)
    args = [place, gate_in, gain, *terms]
    in_specs = [pl.BlockSpec(memory_space=pltpu.SMEM)] + [vmem] * (len(args) - 1)
    aliases = {}
    if so_far is not None:
        aliases = {len(args): 0}
        args.append(so_far)
        in_specs.append(hbm)
    return pl.pallas_call(
        functools.partial(finish_kernel, mine),
        out_shape=jax.ShapeDtypeStruct(gate_in.shape, BF16),
        in_specs=in_specs,
        out_specs=hbm,
        scratch_shapes=[
            pltpu.VMEM((CHIPS, CH, PIECE * DH), BF16),
            pltpu.SemaphoreType.DMA((CHIPS,)),
        ],
        input_output_aliases=aliases,
        cost_estimate=pl.CostEstimate(flops=300_000_000, bytes_accessed=4_000_000, transcendentals=0),
        compiler_params=pltpu.CompilerParams(vmem_limit_bytes=16 << 20),
        name="finish",
    )(*args)


def shift(block, distance):
    count = lax.axis_size("seq")
    return lax.ppermute(block, "seq", [(i, i + distance) for i in range(count - distance)])


def swap(block, distance):
    return lax.ppermute(block, "seq", [(i, i ^ distance) for i in range(lax.axis_size("seq"))])


def level_masks():
    t_at, s_at = np.arange(CH)[:, None], np.arange(CH)[None, :]
    return np.stack(
        [(t_at > s_at) & ((t_at ^ s_at) >> level == 1) for level in range(7)]
    ).astype(ml_dtypes.bfloat16)


def local(mixed_qkv, conv_weight, beta_logit, log_decay, gate_in, norm_gain):
    at = lax.axis_index("seq")
    place = jnp.stack([at % 2, (at // 2) % CHIPS])
    rim = shift(mixed_qkv[CH - 8 :], 1)
    (rows,) = local_call(
        rows_kernel,
        [log_decay.T, beta_logit.T],
        [jax.ShapeDtypeStruct((VH // PIECE, 2 * PIECE, CH), F32)],
        scalars=0,
        name="rows",
    )
    conv_out = early_conv(place[:1], mixed_qkv, conv_weight)
    shared = (mixed_qkv, rim, conv_weight, conv_out, rows, jnp.asarray(level_masks()))
    chips = range(CHIPS)
    finals = [[], []]
    for keys in BANDS:
        theirs, mine = block_terms(keys, place, shared)
        other = swap(theirs[0], 1)
        first, sent = compose(keys, place, mine[0], other)
        pieces = [swap(sent[n], 2 * n) if n else sent[0] for n in chips]
        queries = [
            block_queries(keys, own, place, shared, *part[1:])
            for own, part in ((False, theirs), (True, mine))
        ]
        turn, _ = lax.optimization_barrier((place, queries))

        count = 2 * len(keys)
        state_shape = jax.ShapeDtypeStruct((count, DH, DH), BF16)
        order_shape = jax.ShapeDtypeStruct((CHIPS, rows_of(keys), WIDE), BF16)
        entering = jnp.zeros((count, DH, DH), BF16)
        for _ in range(max(lax.axis_size("seq") // (2 * CHIPS) - 1, 1)):
            order, leaving = local_call(
                functools.partial(gather_kernel, keys),
                [turn, *pieces, entering],
                [order_shape, state_shape],
                name="gather",
            )
            entering = shift(leaving, 2 * CHIPS)
        spread = local_call(
            functools.partial(spread_kernel, keys),
            [place, order, entering],
            [state_shape] * CHIPS,
            [pltpu.VMEM((CHIPS, count, DH, DH), BF16)],
            name="spread",
        )
        starts = [swap(spread[n], 2 * n) if n else spread[0] for n in chips]
        states_shape = jax.ShapeDtypeStruct((CHIPS, count, DH, DH), BF16)
        keep, send = local_call(
            functools.partial(enter_kernel, keys),
            [place, first, *starts],
            [states_shape, states_shape],
            name="enter",
        )
        finals[0] += [swap(send, 1), *queries[0]]
        finals[1] += [keep, *queries[1]]
    gain = norm_gain[None]
    out = finish(True, place, gate_in, gain, finals[1])
    return finish(False, place, gate_in, gain, finals[0], out)


def solution(mesh):
    spec = P(("groups", "seq"), None)
    return jax.shard_map(
        local,
        mesh=mesh,
        in_specs=(spec, P(), spec, spec, spec, P()),
        out_specs=spec,
        check_vma=False,
    )
```

time: 580 us -> 67.3 us (0.12)
  the two profiles are of different devices: /device:TPU:13 before, /device:TPU:0 now
where the time goes in v2:
time: 67.3 us; the launch traced here: 66.9 us
  Pallas kernels  26.6 us (40%)
  starting transfers between devices  18.6 us (28%)
  waiting for transfers between devices  17.8 us (26%)
  local copies, waits for them, and re-layouts  3.38 us (5%)
    pallas_call x8, Pallas kernels, local_call(): pl.pallas_call(kernel, out_shape=out_shape, in_specs=in_specs, out_specs=...  20.6 us
    ppermute x8, waiting for transfers between devices, swap(): lax.ppermute(block, 'seq', [(i, i ^ distance) for i in range(lax.axis_siz...  15.3 us
    ppermute x8, starting transfers between devices, swap(): lax.ppermute(block, 'seq', [(i, i ^ distance) for i in range(lax.axis_siz...  11.8 us
    ppermute x2, starting transfers between devices, shift(): lax.ppermute(block, 'seq', [(i, i + distance) for i in range(count - dist...  6.87 us
    pallas_call x2, Pallas kernels, finish(): pl.pallas_call(functools.partial(finish_kernel, mine), out_shape=jax.Shap...  4.08 us
    ppermute x2, waiting for transfers between devices, shift(): lax.ppermute(block, 'seq', [(i, i + distance) for i in range(count - dist...  2.5 us
    unnamed x16, local copies, waits for them, and re-layouts  2.45 us
    pallas_call x1, Pallas kernels, early_conv(): pl.pallas_call(conv_kernel, out_shape=jax.ShapeDtypeStruct(mixed_qkv.shap...  1.97 us
  transfers between devices with their start and end apart: 10, of which 6 were waited for; matrix products, arithmetic and copies ran while one was open for 0% of the time, Pallas kernels for 14%

profile of v2, /device:TPU:0, one launch (start us, length us, event | category | flops | bytes accessed | tf_op | source)
XLA Modules:
  0.0 66.9 jit_solution(14446654890392987730)
XLA Ops:
  0.0 0.9 %slice.3 = bf16[8,8192]{1,0:T(8,128)(2,1)S(1)} slice(bf16[128,8192]{1,0:T(8,128)(2,1)} %x_ref.7), slice={[120:128], [0:8192]} | slice | bytes 262144 | tf_op jit(solution)/shard_map/slice | solution.py:443
  0.9 2.4 %collective-permute-start = (bf16[8,8192]{1,0:T(8,128)(2,1)S(1)}, bf16[8,8192]{1,0:T(8,128)(2,1)S(1)}, u32[]{:S(2)}, u32[]{:S(2)}) collective-permute-start(bf16[8,8192]{1,0:T(8,128)(2,1)S(1)} %slice.3), channel_id=1, source_target_pairs={{0,1},{1,2},{2,3},{3,4},{4,5},{5,6},{6,7},{7,8},{8,9},{9,10},{10,1... | collective-permute-start | bytes 393224 | tf_op jit(solution)/shard_map/ppermute | solution.py:426
  3.3 1.6 %copy-done = bf16[128,8192]{1,0:T(8,128)(2,1)S(1)} copy-done((bf16[128,8192]{1,0:T(8,128)(2,1)S(1)}, bf16[128,8192]{1,0:T(8,128)(2,1)}, u32[]{:S(2)}) %copy-start) | copy-done | bytes 2097176
  4.9 0.8 %copy-done.3 = bf16[4,8192]{1,0:T(4,128)(2,1)S(1)} copy-done((bf16[4,8192]{1,0:T(4,128)(2,1)S(1)}, bf16[4,8192]{1,0:T(4,128)(2,1)}, u32[]{:S(2)}) %copy-start.3) | copy-done | bytes 65560
  5.8 2.0 %conv.1.conv_ref = bf16[128,8192]{1,0:T(8,128)(2,1)S(1)} custom-call(s32[1]{0:T(128)} %bitcast.sc_ref, bf16[128,8192]{1,0:T(8,128)(2,1)S(1)} %copy-done, bf16[4,8192]{1,0:T(4,128)(2,1)S(1)} %copy-done.3), custom_call_target="tpu_custom_call" | custom-call | flops 10000000 | bytes 2000000 | tf_op jit(solution)/shard_map/conv/pallas_call | solution.py:91
  7.8 0.2 rows.1.rows_ref
  7.9 0.1 pad_add_fusion.sc_ref
  8.0 10.5 %terms.1 = (bf16[4,528,256]{2,1,0:T(8,128)(2,1)S(1)}, bf16[4,4,128,256]{3,2,1,0:T(8,128)(2,1)S(1)}, bf16[4,2,128,128]{3,2,1,0:T(8,128)(2,1)S(1)}, bf16[4,528,256...) custom-call(s32[2]{0:T(128)S(1)} %pad_add_fusion.sc_ref, ...), custom_call_target="tpu_custom_call" | custom-call | flops 100000000 | bytes 2000000 | tf_op jit(solution)/shard_map/terms/pallas_call | solution.py:213
  18.6 2.7 %collective-permute-start.1 = (bf16[4,528,256]{2,1,0:T(8,128)(2,1)S(1)}, bf16[4,528,256]{2,1,0:T(8,128)(2,1)S(1)}, u32[]{:S(2)}, u32[]{:S(2)}) collective-permute-start(bf16[4,528,256]{2,1,0:T(8,128)(2,1)S(1)} %get-tuple-element.30), channel_id=1, source_target_pairs={{0,1},{1,0},{2,3},{3,2},{4,5},{5,4},{6,7},{7,6},{8,9},{9,8},{10,11... | collective-permute-start | bytes 3244040 | tf_op jit(solution)/shard_map/ppermute | solution.py:430
  21.2 2.3 %collective-permute-done.1.other_ref = bf16[4,528,256]{2,1,0:T(8,128)(2,1)S(1)} collective-permute-done((bf16[4,528,256]{2,1,0:T(8,128)(2,1)S(1)}, bf16[4,528,256]{2,1,0:T(8,128)(2,1)S(1)}, u32[]{:S(2)}, u32[]{:S(2)}) %collective-permute-start.1) | collective-permute-done | bytes 1081376 | tf_op jit(solution)/shard_map/ppermute | solution.py:430
  23.6 1.3 %compose.1 = (bf16[4,528,256]{2,1,0:T(8,128)(2,1)S(1)}, bf16[528,256]{1,0:T(8,128)(2,1)S(1)}, bf16[528,256]{1,0:T(8,128)(2,1)S(1)}, bf16[528,256]{1,0:T(8,128)(2,1)S(1)}, bf16[528,256]{1,0:T(8,128)(2,1)S(1)}) custom-call(s32[2]{0:T(128)S(1)} %pad_add_fusion.sc_ref, bf16[4,528,256]{2,1,0:T(8,128)(2,1)S(1)} %get-tuple-element.29.mine_ref, ...), custom_call_target="tpu_custom_call" | custom-call | flops 100000000 | bytes 2000000 | tf_op jit(solution)/shard_map/compose/pallas_call | solution.py:213
  24.9 1.6 %collective-permute-start.2 = (bf16[528,256]{1,0:T(8,128)(2,1)S(1)}, bf16[528,256]{1,0:T(8,128)(2,1)S(1)}, u32[]{:S(2)}, u32[]{:S(2)}) collective-permute-start(bf16[528,256]{1,0:T(8,128)(2,1)S(1)} %get-tuple-element.42), channel_id=1, source_target_pairs={{0,2},{1,3},{2,0},{3,1},{4,6},{5,7},{6,4},{7,5},{8,10},{9,11},{10,... | collective-permute-start | bytes 811016 | tf_op jit(solution)/shard_map/ppermute | solution.py:430
  26.5 1.6 %collective-permute-start.3 = (bf16[528,256]{1,0:T(8,128)(2,1)S(1)}, bf16[528,256]{1,0:T(8,128)(2,1)S(1)}, u32[]{:S(2)}, u32[]{:S(2)}) collective-permute-start(bf16[528,256]{1,0:T(8,128)(2,1)S(1)} %get-tuple-element.43), channel_id=1, source_target_pairs={{0,4},{1,5},{2,6},{3,7},{4,0},{5,1},{6,2},{7,3},{8,12},{9,13},{10,... | collective-permute-start | bytes 811016 | tf_op jit(solution)/shard_map/ppermute | solution.py:430
  28.0 0.4 collective-permute-start.4
  28.4 2.7 %queries.2 = (f32[4,4,128,128]{3,2,1,0:T(8,128)S(1)}, bf16[4,4,128,256]{3,2,1,0:T(8,128)(2,1)S(1)}) custom-call(s32[2]{0:T(128)S(1)} %pad_add_fusion.sc_ref, bf16[128,8192]{1,0:T(8,128)(2,1)S(1)} %copy-done.1, bf16[8,8192]{1,0:T(8,128)(2,1)S(1)} %collective-permute-done.rim_ref, bf16[4,8192]{1,0:T(4,128)(2,1)S(1)} %copy-done.3, ...), custom_call_target="tpu_custom_call" | custom-call | flops 100000000 | bytes 2000000 | tf_op jit(solution)/shard_map/queries/pallas_call | solution.py:213
  31.1 2.5 %queries.3 = (f32[4,4,128,128]{3,2,1,0:T(8,128)S(1)}, bf16[4,4,128,256]{3,2,1,0:T(8,128)(2,1)S(1)}) custom-call(s32[2]{0:T(128)S(1)} %pad_add_fusion.sc_ref, bf16[128,8192]{1,0:T(8,128)(2,1)S(1)} %copy-done.1, bf16[8,8192]{1,0:T(8,128)(2,1)S(1)} %collective-permute-done.rim_ref, bf16[4,8192]{1,0:T(4,128)(2,1)S(1)} %copy-done.3, ...), custom_call_target="tpu_custom_call" | custom-call | flops 100000000 | bytes 2000000 | tf_op jit(solution)/shard_map/queries/pallas_call | solution.py:213
  33.6 0.1 collective-permute-done.2.p1
  33.7 2.1 %collective-permute-done.3.p2 = bf16[528,256]{1,0:T(8,128)(2,1)S(1)} collective-permute-done((bf16[528,256]{1,0:T(8,128)(2,1)S(1)}, bf16[528,256]{1,0:T(8,128)(2,1)S(1)}, u32[]{:S(2)}, u32[]{:S(2)}) %collective-permute-start.3) | collective-permute-done | bytes 270368 | tf_op jit(solution)/shard_map/ppermute | solution.py:430
  35.8 4.9 %collective-permute-done.4.p3 = bf16[528,256]{1,0:T(8,128)(2,1)S(1)} collective-permute-done((bf16[528,256]{1,0:T(8,128)(2,1)S(1)}, bf16[528,256]{1,0:T(8,128)(2,1)S(1)}, u32[]{:S(2)}, u32[]{:S(2)}) %collective-permute-start.4) | collective-permute-done | bytes 270368 | tf_op jit(solution)/shard_map/ppermute | solution.py:430
  40.7 1.2 %gather.1 = (bf16[4,528,256]{2,1,0:T(8,128)(2,1)S(1)}, bf16[4,128,128]{2,1,0:T(8,128)(2,1)S(1)}) custom-call(s32[2]{0:T(128)S(1)} %pad_add_fusion.sc_ref, bf16[528,256]{1,0:T(8,128)(2,1)S(1)} %get-tuple-element.41.p0, bf16[528,256]{1,0:T(8,128)(2,1)S(1)} %collective-permute-done.2.p1, bf16[528,256]{1,0:T(8,128)(2,1)S(1)} %collective-permute-done.3.p2, ...), custom_call_target="tpu_custom_call" | custom-call | flops 100000000 | bytes 2000000 | tf_op jit(solution)/shard_map/gather/pallas_call | solution.py:213
  41.9 4.5 %collective-permute-start.5 = (bf16[4,128,128]{2,1,0:T(8,128)(2,1)S(1)}, bf16[4,128,128]{2,1,0:T(8,128)(2,1)S(1)}, u32[]{:S(2)}, u32[]{:S(2)}) collective-permute-start(bf16[4,128,128]{2,1,0:T(8,128)(2,1)S(1)} %get-tuple-element.46), channel_id=1, source_target_pairs={{0,8},{1,9},{2,10},{3,11},{4,12},{5,13},{6,14},{7,15},{16,24},{17,... | collective-permute-start | bytes 393224 | tf_op jit(solution)/shard_map/ppermute | solution.py:426
  46.4 2.5 %collective-permute-done.5.in_ref = bf16[4,128,128]{2,1,0:T(8,128)(2,1)S(1)} collective-permute-done((bf16[4,128,128]{2,1,0:T(8,128)(2,1)S(1)}, bf16[4,128,128]{2,1,0:T(8,128)(2,1)S(1)}, u32[]{:S(2)}, u32[]{:S(2)}) %collective-permute-start.5) | collective-permute-done | bytes 131104 | tf_op jit(solution)/shard_map/ppermute | solution.py:426
  48.9 1.1 %spread.1 = (bf16[4,128,128]{2,1,0:T(8,128)(2,1)S(1)}, bf16[4,128,128]{2,1,0:T(8,128)(2,1)S(1)}, bf16[4,128,128]{2,1,0:T(8,128)(2,1)S(1)}, bf16[4,128,128]{2,1,0:T(8,128)(2,1)S(1)}) custom-call(s32[2]{0:T(128)S(1)} %pad_add_fusion.sc_ref, bf16[4,528,256]{2,1,0:T(8,128)(2,1)S(1)} %get-tuple-element.45.order_ref, ...), custom_call_target="tpu_custom_call" | custom-call | flops 100000000 | bytes 2000000 | tf_op jit(solution)/shard_map/spread/pallas_call | solution.py:213
  50.0 1.6 %collective-permute-start.6 = (bf16[4,128,128]{2,1,0:T(8,128)(2,1)S(1)}, bf16[4,128,128]{2,1,0:T(8,128)(2,1)S(1)}, u32[]{:S(2)}, u32[]{:S(2)}) collective-permute-start(bf16[4,128,128]{2,1,0:T(8,128)(2,1)S(1)} %get-tuple-element.48), channel_id=1, source_target_pairs={{0,2},{1,3},{2,0},{3,1},{4,6},{5,7},{6,4},{7,5},{8,10},{9,11},{10,... | collective-permute-start | bytes 393224 | tf_op jit(solution)/shard_map/ppermute | solution.py:430
  51.6 3.0 %collective-permute-start.7 = (bf16[4,128,128]{2,1,0:T(8,128)(2,1)S(1)}, bf16[4,128,128]{2,1,0:T(8,128)(2,1)S(1)}, u32[]{:S(2)}, u32[]{:S(2)}) collective-permute-start(bf16[4,128,128]{2,1,0:T(8,128)(2,1)S(1)} %get-tuple-element.49), channel_id=1, source_target_pairs={{0,4},{1,5},{2,6},{3,7},{4,0},{5,1},{6,2},{7,3},{8,12},{9,13},{10,... | collective-permute-start | bytes 393224 | tf_op jit(solution)/shard_map/ppermute | solution.py:430
  54.6 0.9 %collective-permute-start.8 = (bf16[4,128,128]{2,1,0:T(8,128)(2,1)S(1)}, bf16[4,128,128]{2,1,0:T(8,128)(2,1)S(1)}, u32[]{:S(2)}, u32[]{:S(2)}) collective-permute-start(bf16[4,128,128]{2,1,0:T(8,128)(2,1)S(1)} %get-tuple-element.50), channel_id=1, source_target_pairs={{0,6},{1,7},{2,4},{3,5},{4,2},{5,3},{6,0},{7,1},{8,14},{9,15},{10,... | collective-permute-start | bytes 393224 | tf_op jit(solution)/shard_map/ppermute | solution.py:430
  55.5 2.7 %collective-permute-done.7.refs_2_ = bf16[4,128,128]{2,1,0:T(8,128)(2,1)S(1)} collective-permute-done((bf16[4,128,128]{2,1,0:T(8,128)(2,1)S(1)}, bf16[4,128,128]{2,1,0:T(8,128)(2,1)S(1)}, u32[]{:S(2)}, u32[]{:S(2)}) %collective-permute-start.7) | collective-permute-done | bytes 131104 | tf_op jit(solution)/shard_map/ppermute | solution.py:430
  58.2 3.2 %collective-permute-done.8.refs_3_ = bf16[4,128,128]{2,1,0:T(8,128)(2,1)S(1)} collective-permute-done((bf16[4,128,128]{2,1,0:T(8,128)(2,1)S(1)}, bf16[4,128,128]{2,1,0:T(8,128)(2,1)S(1)}, u32[]{:S(2)}, u32[]{:S(2)}) %collective-permute-start.8) | collective-permute-done | bytes 131104 | tf_op jit(solution)/shard_map/ppermute | solution.py:430
  61.4 1.1 %enter.1 = (bf16[4,4,128,128]{3,2,1,0:T(8,128)(2,1)S(1)}, bf16[4,4,128,128]{3,2,1,0:T(8,128)(2,1)S(1)}) custom-call(s32[2]{0:T(128)S(1)} %pad_add_fusion.sc_ref, bf16[4,528,256]{2,1,0:T(8,128)(2,1)S(1)} %get-tuple-element.31.first_ref, bf16[4,128,128]{2,1,0:T(8,128)(2,1)S(1)} %get-tuple-element.47.refs_0_, ...), custom_call_target="tpu_custom_call" | custom-call | flops 100000000 | bytes 2000000 | tf_op jit(solution)/shard_map/enter/pallas_call | solution.py:213
  62.6 0.1 collective-permute-start.9
  62.7 2.0 %finish.2.refs_3_ = bf16[128,4096]{1,0:T(8,128)(2,1)} custom-call(s32[2]{0:T(128)S(1)} %pad_add_fusion.sc_ref, bf16[128,4096]{1,0:T(8,128)(2,1)S(1)} %copy-done.2, f32[1,128]{1,0:T(1,128)S(1)} %bitcast.5, bf16[4,4,128,128]{3,2,1,0:T(8,128)(2,1)S(1)} %get-tuple-element.52.refs_0_, f32[4,4,128,128]{3,2,1,0:T(8,128)S(1)} %get-tuple-element.38.refs_1_, ...), custom_call_target="tpu_custom_call" | custom-call | flops 300000000 | bytes 4000000 | tf_op jit(solution)/shard_map/finish/pallas_call | solution.py:408
  64.7 2.0 %finish.3 = bf16[128,4096]{1,0:T(8,128)(2,1)} custom-call(s32[2]{0:T(128)S(1)} %pad_add_fusion.sc_ref, bf16[128,4096]{1,0:T(8,128)(2,1)S(1)} %copy-done.2, f32[1,128]{1,0:T(1,128)S(1)} %bitcast.6, bf16[4,4,128,128]{3,2,1,0:T(8,128)(2,1)S(1)} %collective-permute-done.9.refs_0_, ...), custom_call_target="tpu_custom_call", output_to_operand_aliasing={{}: (6, {})} | custom-call | flops 300000000 | bytes 4000000 | tf_op jit(solution)/shard_map/finish/pallas_call | solution.py:408
  (18 shorter events, 0.1 us)
Async XLA Ops:
  0.9 7.1 %collective-permute-start = (bf16[8,8192]{1,0:T(8,128)(2,1)S(1)}, bf16[8,8192]{1,0:T(8,128)(2,1)S(1)}, u32[]{:S(2)}, u32[]{:S(2)}) collective-permute-start(bf16[8,8192]{1,0:T(8,128)(2,1)S(1)} %slice.3), channel_id=1, source_target_pairs={{0,1},{1,2},{2,3},{3,4},{4,5},{5,6},{6,7},{7,8},{8,9},{9,10},{10,1... | collective-permute-start | bytes 393224 | tf_op jit(solution)/shard_map/ppermute | solution.py:426
  3.3 1.6 %copy-start = (bf16[128,8192]{1,0:T(8,128)(2,1)S(1)}, bf16[128,8192]{1,0:T(8,128)(2,1)}, u32[]{:S(2)}) copy-start(bf16[128,8192]{1,0:T(8,128)(2,1)} %x_ref.7) | copy-start | bytes 6291460
  4.9 0.8 %copy-start.3 = (bf16[4,8192]{1,0:T(4,128)(2,1)S(1)}, bf16[4,8192]{1,0:T(4,128)(2,1)}, u32[]{:S(2)}) copy-start(bf16[4,8192]{1,0:T(4,128)(2,1)} %w_ref.7) | copy-start | bytes 196612
  5.8 2.0 %copy-start.6 = (f32[128,32]{0,1:T(8,128)S(1)}, f32[128,32]{0,1:T(8,128)}, u32[]{:S(2)}) copy-start(f32[128,32]{0,1:T(8,128)} %param.10) | copy-start | bytes 49156
  5.8 2.0 %copy-start.7 = (bf16[128,32]{0,1:T(8,128)(2,1)S(1)}, bf16[128,32]{0,1:T(8,128)(2,1)}, u32[]{:S(2)}) copy-start(bf16[128,32]{0,1:T(8,128)(2,1)} %param.9) | copy-start | bytes 24580
  5.8 2.3 %copy-start.1 = (bf16[128,8192]{1,0:T(8,128)(2,1)S(1)}, bf16[128,8192]{1,0:T(8,128)(2,1)}, u32[]{:S(2)}) copy-start(bf16[128,8192]{1,0:T(8,128)(2,1)} %x_ref.7) | copy-start | bytes 6291460
  5.8 2.3 %copy-start.4 = (bf16[7,128,128]{2,1,0:T(8,128)(2,1)S(1)}, bf16[7,128,128]{2,1,0:T(8,128)(2,1)}, u32[]{:S(2)}) copy-start(bf16[7,128,128]{2,1,0:T(8,128)(2,1)} %constant.42.clone.masks_ref) | copy-start | bytes 688132
  18.6 5.0 %collective-permute-start.1 = (bf16[4,528,256]{2,1,0:T(8,128)(2,1)S(1)}, bf16[4,528,256]{2,1,0:T(8,128)(2,1)S(1)}, u32[]{:S(2)}, u32[]{:S(2)}) collective-permute-start(bf16[4,528,256]{2,1,0:T(8,128)(2,1)S(1)} %get-tuple-element.30), channel_id=1, source_target_pairs={{0,1},{1,0},{2,3},{3,2},{4,5},{5,4},{6,7},{7,6},{8,9},{9,8},{10,11... | collective-permute-start | bytes 3244040 | tf_op jit(solution)/shard_map/ppermute | solution.py:430
  24.9 8.8 %collective-permute-start.2 = (bf16[528,256]{1,0:T(8,128)(2,1)S(1)}, bf16[528,256]{1,0:T(8,128)(2,1)S(1)}, u32[]{:S(2)}, u32[]{:S(2)}) collective-permute-start(bf16[528,256]{1,0:T(8,128)(2,1)S(1)} %get-tuple-element.42), channel_id=1, source_target_pairs={{0,2},{1,3},{2,0},{3,1},{4,6},{5,7},{6,4},{7,5},{8,10},{9,11},{10,... | collective-permute-start | bytes 811016 | tf_op jit(solution)/shard_map/ppermute | solution.py:430
  26.5 9.3 %collective-permute-start.3 = (bf16[528,256]{1,0:T(8,128)(2,1)S(1)}, bf16[528,256]{1,0:T(8,128)(2,1)S(1)}, u32[]{:S(2)}, u32[]{:S(2)}) collective-permute-start(bf16[528,256]{1,0:T(8,128)(2,1)S(1)} %get-tuple-element.43), channel_id=1, source_target_pairs={{0,4},{1,5},{2,6},{3,7},{4,0},{5,1},{6,2},{7,3},{8,12},{9,13},{10,... | collective-permute-start | bytes 811016 | tf_op jit(solution)/shard_map/ppermute | solution.py:430
  28.0 12.6 %collective-permute-start.4 = (bf16[528,256]{1,0:T(8,128)(2,1)S(1)}, bf16[528,256]{1,0:T(8,128)(2,1)S(1)}, u32[]{:S(2)}, u32[]{:S(2)}) collective-permute-start(bf16[528,256]{1,0:T(8,128)(2,1)S(1)} %get-tuple-element.44), channel_id=1, source_target_pairs={{0,6},{1,7},{2,4},{3,5},{4,2},{5,3},{6,0},{7,1},{8,14},{9,15},{10,... | collective-permute-start | bytes 811016 | tf_op jit(solution)/shard_map/ppermute | solution.py:430
  41.9 7.0 %collective-permute-start.5 = (bf16[4,128,128]{2,1,0:T(8,128)(2,1)S(1)}, bf16[4,128,128]{2,1,0:T(8,128)(2,1)S(1)}, u32[]{:S(2)}, u32[]{:S(2)}) collective-permute-start(bf16[4,128,128]{2,1,0:T(8,128)(2,1)S(1)} %get-tuple-element.46), channel_id=1, source_target_pairs={{0,8},{1,9},{2,10},{3,11},{4,12},{5,13},{6,14},{7,15},{16,24},{17,... | collective-permute-start | bytes 393224 | tf_op jit(solution)/shard_map/ppermute | solution.py:426
  50.0 12.6 %copy-start.2 = (bf16[128,4096]{1,0:T(8,128)(2,1)S(1)}, bf16[128,4096]{1,0:T(8,128)(2,1)}, u32[]{:S(2)}) copy-start(bf16[128,4096]{1,0:T(8,128)(2,1)} %gate_ref.3) | copy-start | bytes 3145732
  50.0 12.6 %copy-start.5 = (f32[128]{0:T(128)S(1)}, f32[128]{0:T(128)}, u32[]{:S(2)}) copy-start(f32[128]{0:T(128)} %param.12) | copy-start | bytes 1540
  50.0 5.4 %collective-permute-start.6 = (bf16[4,128,128]{2,1,0:T(8,128)(2,1)S(1)}, bf16[4,128,128]{2,1,0:T(8,128)(2,1)S(1)}, u32[]{:S(2)}, u32[]{:S(2)}) collective-permute-start(bf16[4,128,128]{2,1,0:T(8,128)(2,1)S(1)} %get-tuple-element.48), channel_id=1, source_target_pairs={{0,2},{1,3},{2,0},{3,1},{4,6},{5,7},{6,4},{7,5},{8,10},{9,11},{10,... | collective-permute-start | bytes 393224 | tf_op jit(solution)/shard_map/ppermute | solution.py:430
  51.6 6.6 %collective-permute-start.7 = (bf16[4,128,128]{2,1,0:T(8,128)(2,1)S(1)}, bf16[4,128,128]{2,1,0:T(8,128)(2,1)S(1)}, u32[]{:S(2)}, u32[]{:S(2)}) collective-permute-start(bf16[4,128,128]{2,1,0:T(8,128)(2,1)S(1)} %get-tuple-element.49), channel_id=1, source_target_pairs={{0,4},{1,5},{2,6},{3,7},{4,0},{5,1},{6,2},{7,3},{8,12},{9,13},{10,... | collective-permute-start | bytes 393224 | tf_op jit(solution)/shard_map/ppermute | solution.py:430
  54.6 6.8 %collective-permute-start.8 = (bf16[4,128,128]{2,1,0:T(8,128)(2,1)S(1)}, bf16[4,128,128]{2,1,0:T(8,128)(2,1)S(1)}, u32[]{:S(2)}, u32[]{:S(2)}) collective-permute-start(bf16[4,128,128]{2,1,0:T(8,128)(2,1)S(1)} %get-tuple-element.50), channel_id=1, source_target_pairs={{0,6},{1,7},{2,4},{3,5},{4,2},{5,3},{6,0},{7,1},{8,14},{9,15},{10,... | collective-permute-start | bytes 393224 | tf_op jit(solution)/shard_map/ppermute | solution.py:430
  62.6 2.1 %collective-permute-start.9 = (bf16[4,4,128,128]{3,2,1,0:T(8,128)(2,1)S(1)}, bf16[4,4,128,128]{3,2,1,0:T(8,128)(2,1)S(1)}, u32[]{:S(2)}, u32[]{:S(2)}) collective-permute-start(bf16[4,4,128,128]{3,2,1,0:T(8,128)(2,1)S(1)} %get-tuple-element.51), channel_id=1, source_target_pairs={{0,1},{1,0},{2,3},{3,2},{4,5},{5,4},{6,7},{7,6},{8,9},{9,8},{10,11... | collective-permute-start | bytes 1572872 | tf_op jit(solution)/shard_map/ppermute | solution.py:430

commit v3 on v2

--- a/solution.py
+++ b/solution.py
@@ -15,7 +15,7 @@
 CH = 128
 CHIPS = 4
 PIECE = 4
-BANDS = ((0, 1),)
+BANDS = ((0,), (1,))
 WIDE = 2 * DH
 
 F32 = jnp.float32
@@ -71,43 +71,68 @@
     return (total / (1.0 + jnp.exp(-total))).astype(BF16)
 
 
+def load_kernel(x_ref, w_ref, x_out, w_out, rim_out, sems):
+    copies = [
+        pltpu.make_async_copy(x_ref.at[CH - 4 :], rim_out, sems.at[0]),
+        pltpu.make_async_copy(w_ref, w_out, sems.at[1]),
+    ]
+    step = CH // 4
+    for i in range(4):
+        part = pl.ds(i * step, step)
+        copies.append(pltpu.make_async_copy(x_ref.at[part], x_out.at[part], sems.at[2 + i]))
+    for copy in copies:
+        copy.start()
+    for copy in copies:
+        copy.wait()
+
+
+def load(mixed_qkv, conv_weight):
+    vmem = pl.BlockSpec(memory_space=pltpu.VMEM)
+    return pl.pallas_call(
+        load_kernel,
+        out_shape=[
+            jax.ShapeDtypeStruct(mixed_qkv.shape, BF16),
+            jax.ShapeDtypeStruct(conv_weight.shape, BF16),
+            jax.ShapeDtypeStruct((4, mixed_qkv.shape[1]), BF16),
+        ],
+        in_specs=[pl.BlockSpec(memory_space=pl.ANY)] * 2,
+        out_specs=[vmem] * 3,
+        scratch_shapes=[pltpu.SemaphoreType.DMA((6,))],
+        cost_estimate=pl.CostEstimate(flops=100, bytes_accessed=100, transcendentals=0),
+        compiler_params=pltpu.CompilerParams(vmem_limit_bytes=4 << 20),
+        name="load",
+    )(*(pltpu.with_memory_space_constraint(a, pltpu.HBM) for a in (mixed_qkv, conv_weight)))
+
+
 def conv_kernel(sc_ref, x_ref, w_ref, out_ref, scr):
-    scr[...] = x_ref[...].astype(F32)
-    w = w_ref[...].astype(F32)
-    out_ref[8:] = taps(lambda tap: scr[5 + tap : 5 + tap + CH - 8, :], w, CH - 8)
-
-
-def early_conv(place, mixed_qkv, conv_weight):
-    width = 512
+    owner = 1 - sc_ref[0]
+    width = scr.shape[2]
     keys, values = KH // 2 * DH // width, VH // 2 * DH // width
-
-    def at(i, sc):
-        owner = 1 - sc[0]
-        key_at = KH * DH // width + owner * keys + i
-        value_at = 2 * KH * DH // width + owner * values + i - keys
-        return (0, jnp.where(i < keys, key_at, value_at))
-
-    tall = pl.BlockSpec((CH, width), at)
-    return pl.pallas_call(
+    starts = [KH * DH + (owner * keys + i) * width for i in range(keys)]
+    starts += [2 * KH * DH + (owner * values + i) * width for i in range(values)]
+    for i, start in enumerate(starts):
+        cols = pl.ds(pl.multiple_of(start, width), width)
+        scr[i % 2] = x_ref[:, cols].astype(F32)
+        w = w_ref[:, cols].astype(F32)
+        out_ref[8:, cols] = taps(lambda tap: scr[i % 2, 5 + tap : 5 + tap + CH - 8, :], w, CH - 8)
+
+
+def early_conv(place, x, conv_weight):
+    return local_call(
         conv_kernel,
-        out_shape=jax.ShapeDtypeStruct(mixed_qkv.shape, BF16),
-        grid_spec=pltpu.PrefetchScalarGridSpec(
-            num_scalar_prefetch=1,
-            grid=(keys + values,),
-            in_specs=[tall, pl.BlockSpec((conv_weight.shape[0], width), at)],
-            out_specs=tall,
-            scratch_shapes=[pltpu.VMEM((CH, width), F32)],
-        ),
-        cost_estimate=pl.CostEstimate(flops=10_000_000, bytes_accessed=2_000_000, transcendentals=0),
-        compiler_params=pltpu.CompilerParams(vmem_limit_bytes=8 << 20),
+        [place, x, conv_weight],
+        [jax.ShapeDtypeStruct(x.shape, BF16)],
+        [pltpu.VMEM((2, CH, 512), F32)],
+        flops=10_000_000,
+        vmem_mib=4,
         name="conv",
-    )(place, mixed_qkv, conv_weight)
+    )[0]
 
 
 def convolved(x_ref, rim_ref, w_ref, scr, slot, column, width, conv_ref=None):
     cols = pl.ds(pl.multiple_of(column, DH), width)
     w = w_ref[:, cols].astype(F32)
-    scr[slot, 0:8, :width] = rim_ref[:, cols].astype(F32)
+    scr[slot, 4:8, :width] = rim_ref[:, cols].astype(F32)
     if conv_ref is None:
         scr[slot, 8 : 8 + CH, :width] = x_ref[:, cols].astype(F32)
         return taps(lambda tap: scr[slot, 5 + tap : 5 + tap + CH, :width], w, CH).astype(F32)
@@ -121,9 +146,8 @@
     return lax.rsqrt(jnp.sum(rows * rows, axis=axis, keepdims=True) + 1e-06)
 
 
-def decay_pairs(rows, cols, h, lower):
-    gap = jnp.minimum(cols[:, h : h + 1] - rows[h : h + 1], 0.0)
-    return jnp.where(lower, jnp.exp(gap), 0.0)
+def decay_pairs(rows, cols, h):
+    return jnp.exp(jnp.minimum(cols[:, h : h + 1] - rows[h : h + 1], 0.0))
 
 
 def token_order():
@@ -135,8 +159,8 @@
 def terms_kernel(keys, sc_ref, x_ref, rim_ref, w_ref, conv_ref, rows_ref, masks_ref, *refs):
     theirs_refs, mine_refs, scr = refs[:3], refs[3:6], refs[6]
     t_at, s_at = token_order()
-    lower, strict = t_at >= s_at, t_at > s_at
-    unit = (t_at == s_at).astype(F32)
+    strict = t_at > s_at
+    unit = (t_at == s_at).astype(F32).astype(BF16)
     pieces = VH // 2 // PIECE
     kd, vd = len(keys) * DH, 2 * len(keys) * DH
 
@@ -169,40 +193,41 @@
                 key_dot = dot(k_b, k_t.astype(BF16)) * rk_col * rk_row
                 for i in range(2):
                     h = 2 * key + i
-                    pair = decay_pairs(rows, cols, h, lower)
-                    system = jnp.where(strict, key_dot * pair * cols[:, 4 + h : 5 + h], 0.0)
+                    system = key_dot * decay_pairs(rows, cols, h)
+                    system = jnp.where(strict, system, 0.0).astype(BF16)
+                    beta_row = rows[4 + h : 5 + h]
+                    gains = (cols[:, 4 + h : 5 + h] * beta_row).astype(BF16)
+                    high, low = halves(jnp.broadcast_to(beta_row, (CH, CH)))
                     heads.append(
                         dict(
                             out=(ma_ref, solved_ref, offset, 2 * g + i),
-                            beta=rows[4 + h : 5 + h],
-                            system=system.astype(BF16),
-                            inv=halves(unit - system * masks_ref[0].astype(F32)),
+                            system=system,
+                            inv=unit * high - system * masks_ref[0] * gains,
+                            inv_low=unit * low,
                             value=cv[:, head_slice(2 * g + i)].astype(BF16),
                             key=(k_f * (grow_cols[:, h : h + 1] * rk_col)).astype(BF16),
-                            tail=halves(k_t * (rk_row * tail_rows[h : h + 1])),
+                            tail=(k_t * (rk_row * tail_rows[h : h + 1])).astype(BF16),
                         )
                     )
 
     for level in range(1, 7):
         mask = masks_ref[level]
-        steps = [dot(p["inv"][0], p["system"] * mask).astype(BF16) for p in heads]
-        steps = [halves(dot(s, p["inv"][0])) for s, p in zip(steps, heads)]
+        steps = [dot(p["inv"], p["system"] * mask).astype(BF16) for p in heads]
+        steps = [dot(s, p["inv"]).astype(BF16) for s, p in zip(steps, heads)]
         for s, p in zip(steps, heads):
-            p["inv"] = (p["inv"][0] - s[0], p["inv"][1] - s[1])
+            p["inv"] = p["inv"] - s
 
     for p in heads:
-        inv = halves((p["inv"][0].astype(F32) + p["inv"][1].astype(F32)) * p["beta"])
         right = jnp.concatenate([p["key"], p["value"]], axis=1)
         p["solved"] = dot(
-            jnp.concatenate(inv, axis=1), jnp.concatenate([right, right], axis=0)
+            jnp.concatenate([p["inv"], p["inv_low"]], axis=1),
+            jnp.concatenate([right, right], axis=0),
         ).astype(BF16)
     for p in heads:
         ma_ref, solved_ref, offset, h = p["out"]
         solved = p["solved"]
         solved_ref[offset, h] = solved
-        ma_ref[offset, head_slice(h), :] = dot(
-            jnp.concatenate(p["tail"], axis=1), jnp.concatenate([solved, solved], axis=0)
-        ).astype(BF16)
+        ma_ref[offset, head_slice(h), :] = dot(p["tail"], solved).astype(BF16)
 
 
 def local_call(
@@ -216,7 +241,7 @@
         in_specs=in_specs,
         out_specs=[vmem] * len(out_shape),
         scratch_shapes=list(scratch),
-        cost_estimate=pl.CostEstimate(flops=flops, bytes_accessed=2_000_000, transcendentals=0),
+        cost_estimate=pl.CostEstimate(flops=100, bytes_accessed=100, transcendentals=0),
         compiler_params=pltpu.CompilerParams(vmem_limit_bytes=vmem_mib << 20),
         name=name,
     )(*args)
@@ -296,14 +321,15 @@
             query_dot = dot(q_f.astype(BF16), k_t.astype(BF16)) * rq_col * inverse_norms(k_t, 0)
             for i in range(2):
                 h = 2 * key + i
-                mixing = halves(query_dot * decay_pairs(rows, cols, h, t_at >= s_at))
+                mixing = query_dot * decay_pairs(rows, cols, h)
+                mixing = halves(jnp.where(t_at >= s_at, mixing, 0.0))
                 query = q_f * (grow_cols[:, h : h + 1] * rq_col)
                 heads.append((offset, 2 * g + i, mixing, query))
     for offset, h, mixing, query in heads:
         solved = solved_ref[offset, h]
         both = dot(jnp.concatenate(mixing, axis=1), jnp.concatenate([solved, solved], axis=0))
         loc_ref[offset, h] = both[:, DH:]
-        car_ref[offset, h] = jnp.concatenate(halves(query - both[:, :DH]), axis=1)
+        car_ref[offset, h] = (query - both[:, :DH]).astype(BF16)
 
 
 def block_queries(keys, mine, place, shared, solved, key_rows):
@@ -313,7 +339,7 @@
         [place, *shared[:3], shared[4], solved, key_rows],
         [
             jax.ShapeDtypeStruct((CHIPS, count, CH, DH), F32),
-            jax.ShapeDtypeStruct((CHIPS, count, CH, WIDE), BF16),
+            jax.ShapeDtypeStruct((CHIPS, count, CH, DH), BF16),
         ],
         [pltpu.VMEM((CHIPS, CH + 8, len(keys) * DH), F32)],
         vmem_mib=24,
@@ -367,57 +393,76 @@
             send_ref[offset, h] = jnp.where(is_first, after, start)
 
 
-def finish_kernel(mine, sc_ref, gate_ref, gain_ref, *refs):
+def piece_columns(own, sc_ref, offset):
+    owner = sc_ref[0] if own else 1 - sc_ref[0]
+    piece = owner * (VH // 2 // PIECE) + (sc_ref[1] ^ offset)
+    return pl.ds(pl.multiple_of(piece * PIECE * DH, PIECE * DH), PIECE * DH)
+
+
+def finish_piece(own, offset, sc_ref, gate_ref, gain_ref, bands, out_ref):
+    gates = gate_ref[:, piece_columns(own, sc_ref, offset)].astype(F32)
+    gates = gates / (1.0 + jnp.exp(-gates))
+    for keys, (state_ref, loc_ref, car_ref) in zip(BANDS, bands):
+        for h in range(2 * len(keys)):
+            core = loc_ref[offset, h] + dot(car_ref[offset, h], state_ref[offset, h])
+            mean_sq = jnp.mean(core * core, axis=1, keepdims=True)
+            cols = head_slice(2 * keys[0] + h)
+            scaled = core * lax.rsqrt(mean_sq + 1e-06) * gain_ref[...] * gates[:, cols]
+            out_ref[offset, :, cols] = scaled.astype(BF16)
+
+
+def finish_kernel(sc_ref, gate_ref, gain_ref, *refs):
+    bands = [refs[3 * b : 3 * b + 3] for b in range(len(BANDS))]
+    for offset in range(CHIPS):
+        finish_piece(1, offset, sc_ref, gate_ref, gain_ref, bands, refs[-1])
+
+
+def finish(place, gate_in, gain, terms):
+    return local_call(
+        finish_kernel,
+        [place, gate_in, gain, *terms],
+        [jax.ShapeDtypeStruct((CHIPS, CH, PIECE * DH), BF16)],
+        vmem_mib=4,
+        name="finish",
+    )[0]
+
+
+def last_kernel(sc_ref, gate_ref, gain_ref, done_ref, *refs):
     bands = [refs[3 * b : 3 * b + 3] for b in range(len(BANDS))]
     out_ref, scr, sems = refs[-3:]
-    owner = sc_ref[0] if mine else 1 - sc_ref[0]
     copies = []
+
+    def send(own, source_ref, offset):
+        cols = piece_columns(own, sc_ref, offset)
+        copies.append(
+            pltpu.make_async_copy(source_ref.at[offset], out_ref.at[:, cols], sems.at[len(copies)])
+        )
+        copies[-1].start()
+
     for offset in range(CHIPS):
-        piece = owner * (VH // 2 // PIECE) + (sc_ref[1] ^ offset)
-        cols = pl.ds(pl.multiple_of(piece * PIECE * DH, PIECE * DH), PIECE * DH)
-        gates = gate_ref[:, cols].astype(F32)
-        gates = gates / (1.0 + jnp.exp(-gates))
-        at = 0
-        for state_ref, loc_ref, car_ref in bands:
-            for h in range(state_ref.shape[1]):
-                state = state_ref[offset, h]
-                core = loc_ref[offset, h] + dot(
-                    car_ref[offset, h], jnp.concatenate([state, state], axis=0)
-                )
-                mean_sq = jnp.mean(core * core, axis=1, keepdims=True)
-                scaled = core * lax.rsqrt(mean_sq + 1e-06) * gain_ref[...] * gates[:, head_slice(at)]
-                scr[offset, :, head_slice(at)] = scaled.astype(BF16)
-                at += 1
-        copy = pltpu.make_async_copy(scr.at[offset], out_ref.at[:, cols], sems.at[offset])
-        copy.start()
-        copies.append(copy)
+        send(1, done_ref, offset)
+    for offset in range(CHIPS):
+        finish_piece(0, offset, sc_ref, gate_ref, gain_ref, bands, scr)
+        send(0, scr, offset)
     for copy in copies:
         copy.wait()
 
 
-def finish(mine, place, gate_in, gain, terms, so_far=None):
+def finish_last(place, gate_in, gain, done, terms):
     vmem = pl.BlockSpec(memory_space=pltpu.VMEM)
-    hbm = pl.BlockSpec(memory_space=pl.ANY)
-    args = [place, gate_in, gain, *terms]
-    in_specs = [pl.BlockSpec(memory_space=pltpu.SMEM)] + [vmem] * (len(args) - 1)
-    aliases = {}
-    if so_far is not None:
-        aliases = {len(args): 0}
-        args.append(so_far)
-        in_specs.append(hbm)
+    args = [place, gate_in, gain, done, *terms]
     return pl.pallas_call(
-        functools.partial(finish_kernel, mine),
+        last_kernel,
         out_shape=jax.ShapeDtypeStruct(gate_in.shape, BF16),
-        in_specs=in_specs,
-        out_specs=hbm,
+        in_specs=[pl.BlockSpec(memory_space=pltpu.SMEM)] + [vmem] * (len(args) - 1),
+        out_specs=pl.BlockSpec(memory_space=pl.ANY),
         scratch_shapes=[
             pltpu.VMEM((CHIPS, CH, PIECE * DH), BF16),
-            pltpu.SemaphoreType.DMA((CHIPS,)),
+            pltpu.SemaphoreType.DMA((2 * CHIPS,)),
         ],
-        input_output_aliases=aliases,
-        cost_estimate=pl.CostEstimate(flops=300_000_000, bytes_accessed=4_000_000, transcendentals=0),
-        compiler_params=pltpu.CompilerParams(vmem_limit_bytes=16 << 20),
-        name="finish",
+        cost_estimate=pl.CostEstimate(flops=100, bytes_accessed=100, transcendentals=0),
+        compiler_params=pltpu.CompilerParams(vmem_limit_bytes=4 << 20),
+        name="finish_last",
     )(*args)
 
 
@@ -440,7 +485,8 @@
 def local(mixed_qkv, conv_weight, beta_logit, log_decay, gate_in, norm_gain):
     at = lax.axis_index("seq")
     place = jnp.stack([at % 2, (at // 2) % CHIPS])
-    rim = shift(mixed_qkv[CH - 8 :], 1)
+    x, weight, last_rows = load(mixed_qkv, conv_weight)
+    rim = shift(last_rows, 1)
     (rows,) = local_call(
         rows_kernel,
         [log_decay.T, beta_logit.T],
@@ -448,18 +494,18 @@
         scalars=0,
         name="rows",
     )
-    conv_out = early_conv(place[:1], mixed_qkv, conv_weight)
-    shared = (mixed_qkv, rim, conv_weight, conv_out, rows, jnp.asarray(level_masks()))
+    conv_out = early_conv(place, x, weight)
+    shared = (x, rim, weight, conv_out, rows, jnp.asarray(level_masks()))
     chips = range(CHIPS)
     finals = [[], []]
     for keys in BANDS:
         theirs, mine = block_terms(keys, place, shared)
         other = swap(theirs[0], 1)
         first, sent = compose(keys, place, mine[0], other)
-        pieces = [swap(sent[n], 2 * n) if n else sent[0] for n in chips]
+        pieces = [swap(sent[n], 2 * n) if n else sent[0] for n in range(CHIPS)]
         queries = [
             block_queries(keys, own, place, shared, *part[1:])
-            for own, part in ((False, theirs), (True, mine))
+            for own, part in enumerate((theirs, mine))
         ]
         turn, _ = lax.optimization_barrier((place, queries))
 
@@ -482,7 +528,7 @@
             [pltpu.VMEM((CHIPS, count, DH, DH), BF16)],
             name="spread",
         )
-        starts = [swap(spread[n], 2 * n) if n else spread[0] for n in chips]
+        starts = [swap(spread[n], 2 * n) if n else spread[0] for n in range(CHIPS)]
         states_shape = jax.ShapeDtypeStruct((CHIPS, count, DH, DH), BF16)
         keep, send = local_call(
             functools.partial(enter_kernel, keys),
@@ -490,11 +536,11 @@
             [states_shape, states_shape],
             name="enter",
         )
-        finals[0] += [swap(send, 1), *queries[0]]
-        finals[1] += [keep, *queries[1]]
+        for own, state in enumerate((swap(send, 1), keep)):
+            finals[own] += [state, *queries[own]]
     gain = norm_gain[None]
-    out = finish(True, place, gate_in, gain, finals[1])
-    return finish(False, place, gate_in, gain, finals[0], out)
+    done = finish(place, gate_in, gain, finals[1])
+    return finish_last(place, gate_in, gain, done, finals[0])
 
 
 def solution(mesh):

time: 67.3 us -> 61.6 us (0.915)
  waiting for transfers between devices: 17.8 us -> 3.3 us
  starting transfers between devices: 18.6 us -> 26.3 us
  Pallas kernels: 26.6 us -> 31.1 us
  local copies, waits for them, and re-layouts: 3.38 us -> 0.03 us
    ppermute x8 -> x16, waiting for transfers between devices: 15.3 us -> 3.29 us  [swap(): lax.ppermute(block, 'seq', [(i, i ^ distance) for i in range(lax.axis_siz...]
    pallas_call x8 -> x17, Pallas kernels: 20.6 us -> 27.5 us  [local_call(): pl.pallas_call(kernel, out_shape=out_shape, in_specs=in_specs, out_specs=...]
    ppermute x8 -> x16, starting transfers between devices: 11.8 us -> 17.8 us  [swap(): lax.ppermute(block, 'seq', [(i, i ^ distance) for i in range(lax.axis_siz...]
    ppermute x2 -> x3, waiting for transfers between devices: 2.5 us -> 0.01 us  [shift(): lax.ppermute(block, 'seq', [(i, i + distance) for i in range(count - dist...]
    unnamed x16 -> x10, local copies, waits for them, and re-layouts: 2.45 us -> 0.02 us
    pallas_call x3 -> x2, Pallas kernels: 6.05 us -> 3.67 us  [the longest x1 2.01 us: finish_last(): pl.pallas_call(last_kernel, out_shape=jax.ShapeDtypeStruct(gate_in.shape,...]
    ppermute x2 -> x3, starting transfers between devices: 6.87 us -> 8.59 us  [shift(): lax.ppermute(block, 'seq', [(i, i + distance) for i in range(count - dist...]
    slice x1 -> x0, local copies, waits for them, and re-layouts: 0.91 us -> none  [local(): rim = shift(mixed_qkv[CH - 8:], 1)]
  transfers between devices with their start and end apart: 10 -> 19, of which waited for: 6 -> 4; matrix products, arithmetic and copies ran while one was open for 0% -> 0% of each run, Pallas kernels for 14% -> 36%
where the time goes in v3:
time: 61.6 us; the launch traced here: 61.4 us
  Pallas kernels  31.1 us (50%)
  starting transfers between devices  26.3 us (43%)
  waiting for transfers between devices  3.3 us (5%)
    pallas_call x17, Pallas kernels, local_call(): pl.pallas_call(kernel, out_shape=out_shape, in_specs=in_specs, out_specs=...  27.5 us
    ppermute x16, starting transfers between devices, swap(): lax.ppermute(block, 'seq', [(i, i ^ distance) for i in range(lax.axis_siz...  17.8 us
    ppermute x3, starting transfers between devices, shift(): lax.ppermute(block, 'seq', [(i, i + distance) for i in range(count - dist...  8.59 us
    ppermute x16, waiting for transfers between devices, swap(): lax.ppermute(block, 'seq', [(i, i ^ distance) for i in range(lax.axis_siz...  3.29 us
    pallas_call x1, Pallas kernels, finish_last(): pl.pallas_call(last_kernel, out_shape=jax.ShapeDtypeStruct(gate_in.shape,...  2.01 us
    pallas_call x1, Pallas kernels, load(): pl.pallas_call(load_kernel, out_shape=[jax.ShapeDtypeStruct(mixed_qkv.sha...  1.66 us
  transfers between devices with their start and end apart: 19, of which 4 were waited for; matrix products, arithmetic and copies ran while one was open for 0% of the time, Pallas kernels for 36%

profile of v3, /device:TPU:0, one launch (start us, length us, event | category | flops | bytes accessed | tf_op | source)
XLA Modules:
  0.0 61.4 jit_solution(13332231342783526244)
XLA Ops:
  0.0 1.7 %load.1 = (bf16[128,8192]{1,0:T(8,128)(2,1)S(1)}, bf16[4,8192]{1,0:T(4,128)(2,1)S(1)}, bf16[4,8192]{1,0:T(4,128)(2,1)S(1)}) custom-call(bf16[128,8192]{1,0:T(8,128)(2,1)} %x_ref.1, bf16[4,8192]{1,0:T(4,128)(2,1)} %w_ref.1), custom_call_target="tpu_custom_call" | custom-call | flops 100 | bytes 100 | tf_op jit(solution)/shard_map/load/pallas_call | solution.py:91
  1.7 2.4 %collective-permute-start = (bf16[4,8192]{1,0:T(4,128)(2,1)S(1)}, bf16[4,8192]{1,0:T(4,128)(2,1)S(1)}, u32[]{:S(2)}, u32[]{:S(2)}) collective-permute-start(bf16[4,8192]{1,0:T(4,128)(2,1)S(1)} %get-tuple-element.57), channel_id=1, source_target_pairs={{0,1},{1,2},{2,3},{3,4},{4,5},{5,6},{6,7},{7,8},{8,9},{9,10},{10,1... | collective-permute-start | bytes 196616 | tf_op jit(solution)/shard_map/ppermute | solution.py:471
  4.3 2.1 %conv.1.conv_ref = bf16[128,8192]{1,0:T(8,128)(2,1)S(1)} custom-call(s32[2]{0:T(128)S(1)} %pad_add_fusion.sc_ref, bf16[128,8192]{1,0:T(8,128)(2,1)S(1)} %get-tuple-element.56.x_ref, bf16[4,8192]{1,0:T(4,128)(2,1)S(1)} %get-tuple-element.58.w_ref), custom_call_target="tpu_custom_call" | custom-call | flops 100 | bytes 100 | tf_op jit(solution)/shard_map/conv/pallas_call | solution.py:238
  6.5 5.2 %terms.3 = (bf16[4,272,256]{2,1,0:T(8,128)(2,1)S(1)}, bf16[4,2,128,256]{3,2,1,0:T(8,128)(2,1)S(1)}, bf16[4,1,128,128]{3,2,1,0:T(8,128)(2,1)S(1)}, bf16[4,272,256...) custom-call(s32[2]{0:T(128)S(1)} %pad_add_fusion.sc_ref, ...), custom_call_target="tpu_custom_call" | custom-call | flops 100 | bytes 100 | tf_op jit(solution)/shard_map/terms/pallas_call | solution.py:238
  11.7 2.7 %collective-permute-start.9 = (bf16[4,272,256]{2,1,0:T(8,128)(2,1)S(1)}, bf16[4,272,256]{2,1,0:T(8,128)(2,1)S(1)}, u32[]{:S(2)}, u32[]{:S(2)}) collective-permute-start(bf16[4,272,256]{2,1,0:T(8,128)(2,1)S(1)} %get-tuple-element.83), channel_id=1, source_target_pairs={{0,1},{1,0},{2,3},{3,2},{4,5},{5,4},{6,7},{7,6},{8,9},{9,8},{10,11... | collective-permute-start | bytes 1671176 | tf_op jit(solution)/shard_map/ppermute | solution.py:475
  14.4 5.2 %terms.2 = (bf16[4,272,256]{2,1,0:T(8,128)(2,1)S(1)}, bf16[4,2,128,256]{3,2,1,0:T(8,128)(2,1)S(1)}, bf16[4,1,128,128]{3,2,1,0:T(8,128)(2,1)S(1)}, bf16[4,272,256...) custom-call(s32[2]{0:T(128)S(1)} %pad_add_fusion.sc_ref, ...), custom_call_target="tpu_custom_call" | custom-call | flops 100 | bytes 100 | tf_op jit(solution)/shard_map/terms/pallas_call | solution.py:238
  19.8 0.9 %compose.3 = (bf16[4,272,256]{2,1,0:T(8,128)(2,1)S(1)}, bf16[272,256]{1,0:T(8,128)(2,1)S(1)}, bf16[272,256]{1,0:T(8,128)(2,1)S(1)}, bf16[272,256]{1,0:T(8,128)(2,1)S(1)}, bf16[272,256]{1,0:T(8,128)(2,1)S(1)}) custom-call(s32[2]{0:T(128)S(1)} %pad_add_fusion.sc_ref, bf16[4,272,256]{2,1,0:T(8,128)(2,1)S(1)} %get-tuple-element.82.mine_ref, ...), custom_call_target="tpu_custom_call" | custom-call | flops 100 | bytes 100 | tf_op jit(solution)/shard_map/compose/pallas_call | solution.py:238
  20.7 1.6 %collective-permute-start.10 = (bf16[272,256]{1,0:T(8,128)(2,1)S(1)}, bf16[272,256]{1,0:T(8,128)(2,1)S(1)}, u32[]{:S(2)}, u32[]{:S(2)}) collective-permute-start(bf16[272,256]{1,0:T(8,128)(2,1)S(1)} %get-tuple-element.95), channel_id=1, source_target_pairs={{0,2},{1,3},{2,0},{3,1},{4,6},{5,7},{6,4},{7,5},{8,10},{9,11},{10,... | collective-permute-start | bytes 417800 | tf_op jit(solution)/shard_map/ppermute | solution.py:475
  22.3 1.6 %collective-permute-start.11 = (bf16[272,256]{1,0:T(8,128)(2,1)S(1)}, bf16[272,256]{1,0:T(8,128)(2,1)S(1)}, u32[]{:S(2)}, u32[]{:S(2)}) collective-permute-start(bf16[272,256]{1,0:T(8,128)(2,1)S(1)} %get-tuple-element.96), channel_id=1, source_target_pairs={{0,4},{1,5},{2,6},{3,7},{4,0},{5,1},{6,2},{7,3},{8,12},{9,13},{10,... | collective-permute-start | bytes 417800 | tf_op jit(solution)/shard_map/ppermute | solution.py:475
  23.9 0.9 %collective-permute-start.12 = (bf16[272,256]{1,0:T(8,128)(2,1)S(1)}, bf16[272,256]{1,0:T(8,128)(2,1)S(1)}, u32[]{:S(2)}, u32[]{:S(2)}) collective-permute-start(bf16[272,256]{1,0:T(8,128)(2,1)S(1)} %get-tuple-element.97), channel_id=1, source_target_pairs={{0,6},{1,7},{2,4},{3,5},{4,2},{5,3},{6,0},{7,1},{8,14},{9,15},{10,... | collective-permute-start | bytes 417800 | tf_op jit(solution)/shard_map/ppermute | solution.py:475
  24.8 0.9 %compose.2 = (bf16[4,272,256]{2,1,0:T(8,128)(2,1)S(1)}, bf16[272,256]{1,0:T(8,128)(2,1)S(1)}, bf16[272,256]{1,0:T(8,128)(2,1)S(1)}, bf16[272,256]{1,0:T(8,128)(2,1)S(1)}, bf16[272,256]{1,0:T(8,128)(2,1)S(1)}) custom-call(s32[2]{0:T(128)S(1)} %pad_add_fusion.sc_ref, bf16[4,272,256]{2,1,0:T(8,128)(2,1)S(1)} %get-tuple-element.59.mine_ref, ...), custom_call_target="tpu_custom_call" | custom-call | flops 100 | bytes 100 | tf_op jit(solution)/shard_map/compose/pallas_call | solution.py:238
  25.7 1.1 %collective-permute-start.2 = (bf16[272,256]{1,0:T(8,128)(2,1)S(1)}, bf16[272,256]{1,0:T(8,128)(2,1)S(1)}, u32[]{:S(2)}, u32[]{:S(2)}) collective-permute-start(bf16[272,256]{1,0:T(8,128)(2,1)S(1)} %get-tuple-element.72), channel_id=1, source_target_pairs={{0,2},{1,3},{2,0},{3,1},{4,6},{5,7},{6,4},{7,5},{8,10},{9,11},{10,... | collective-permute-start | bytes 417800 | tf_op jit(solution)/shard_map/ppermute | solution.py:475
  26.8 1.6 %collective-permute-start.3 = (bf16[272,256]{1,0:T(8,128)(2,1)S(1)}, bf16[272,256]{1,0:T(8,128)(2,1)S(1)}, u32[]{:S(2)}, u32[]{:S(2)}) collective-permute-start(bf16[272,256]{1,0:T(8,128)(2,1)S(1)} %get-tuple-element.73), channel_id=1, source_target_pairs={{0,4},{1,5},{2,6},{3,7},{4,0},{5,1},{6,2},{7,3},{8,12},{9,13},{10,... | collective-permute-start | bytes 417800 | tf_op jit(solution)/shard_map/ppermute | solution.py:475
  28.4 1.0 %collective-permute-start.4 = (bf16[272,256]{1,0:T(8,128)(2,1)S(1)}, bf16[272,256]{1,0:T(8,128)(2,1)S(1)}, u32[]{:S(2)}, u32[]{:S(2)}) collective-permute-start(bf16[272,256]{1,0:T(8,128)(2,1)S(1)} %get-tuple-element.74), channel_id=1, source_target_pairs={{0,6},{1,7},{2,4},{3,5},{4,2},{5,3},{6,0},{7,1},{8,14},{9,15},{10,... | collective-permute-start | bytes 417800 | tf_op jit(solution)/shard_map/ppermute | solution.py:475
  29.4 1.4 %queries.7 = (f32[4,2,128,128]{3,2,1,0:T(8,128)S(1)}, bf16[4,2,128,128]{3,2,1,0:T(8,128)(2,1)S(1)}) custom-call(s32[2]{0:T(128)S(1)} %pad_add_fusion.sc_ref, bf16[128,8192]{1,0:T(8,128)(2,1)S(1)} %get-tuple-element.56.x_ref, bf16[4,8192]{1,0:T(4,128)(2,1)S(1)} %collective-permute-done.rim_ref, bf16[4,8192]{1,0:T(4,128)(2,1)S(1)} %get-tuple-element.58.w_ref, ...), custom_call_target="tpu_custom_call" | custom-call | flops 100 | bytes 100 | tf_op jit(solution)/shard_map/queries/pallas_call | solution.py:238
  30.8 1.4 %queries.6 = (f32[4,2,128,128]{3,2,1,0:T(8,128)S(1)}, bf16[4,2,128,128]{3,2,1,0:T(8,128)(2,1)S(1)}) custom-call(s32[2]{0:T(128)S(1)} %pad_add_fusion.sc_ref, bf16[128,8192]{1,0:T(8,128)(2,1)S(1)} %get-tuple-element.56.x_ref, bf16[4,8192]{1,0:T(4,128)(2,1)S(1)} %collective-permute-done.rim_ref, bf16[4,8192]{1,0:T(4,128)(2,1)S(1)} %get-tuple-element.58.w_ref, ...), custom_call_target="tpu_custom_call" | custom-call | flops 100 | bytes 100 | tf_op jit(solution)/shard_map/queries/pallas_call | solution.py:238
  32.3 1.2 %gather.3 = (bf16[4,272,256]{2,1,0:T(8,128)(2,1)S(1)}, bf16[2,128,128]{2,1,0:T(8,128)(2,1)S(1)}) custom-call(s32[2]{0:T(128)S(1)} %pad_add_fusion.sc_ref, bf16[272,256]{1,0:T(8,128)(2,1)S(1)} %get-tuple-element.94.p0, bf16[272,256]{1,0:T(8,128)(2,1)S(1)} %collective-permute-done.10.p1, bf16[272,256]{1,0:T(8,128)(2,1)S(1)} %collective-permute-done.11.p2, ...), custom_call_target="tpu_custom_call" | custom-call | flops 100 | bytes 100 | tf_op jit(solution)/shard_map/gather/pallas_call | solution.py:238
  33.5 4.9 %collective-permute-start.13 = (bf16[2,128,128]{2,1,0:T(8,128)(2,1)S(1)}, bf16[2,128,128]{2,1,0:T(8,128)(2,1)S(1)}, u32[]{:S(2)}, u32[]{:S(2)}) collective-permute-start(bf16[2,128,128]{2,1,0:T(8,128)(2,1)S(1)} %get-tuple-element.99), channel_id=1, source_target_pairs={{0,8},{1,9},{2,10},{3,11},{4,12},{5,13},{6,14},{7,15},{16,24},{17,... | collective-permute-start | bytes 196616 | tf_op jit(solution)/shard_map/ppermute | solution.py:471
  38.4 1.4 %queries.5 = (f32[4,2,128,128]{3,2,1,0:T(8,128)S(1)}, bf16[4,2,128,128]{3,2,1,0:T(8,128)(2,1)S(1)}) custom-call(s32[2]{0:T(128)S(1)} %pad_add_fusion.sc_ref, bf16[128,8192]{1,0:T(8,128)(2,1)S(1)} %get-tuple-element.56.x_ref, bf16[4,8192]{1,0:T(4,128)(2,1)S(1)} %collective-permute-done.rim_ref, bf16[4,8192]{1,0:T(4,128)(2,1)S(1)} %get-tuple-element.58.w_ref, ...), custom_call_target="tpu_custom_call" | custom-call | flops 100 | bytes 100 | tf_op jit(solution)/shard_map/queries/pallas_call | solution.py:238
  39.8 1.4 %queries.4 = (f32[4,2,128,128]{3,2,1,0:T(8,128)S(1)}, bf16[4,2,128,128]{3,2,1,0:T(8,128)(2,1)S(1)}) custom-call(s32[2]{0:T(128)S(1)} %pad_add_fusion.sc_ref, bf16[128,8192]{1,0:T(8,128)(2,1)S(1)} %get-tuple-element.56.x_ref, bf16[4,8192]{1,0:T(4,128)(2,1)S(1)} %collective-permute-done.rim_ref, bf16[4,8192]{1,0:T(4,128)(2,1)S(1)} %get-tuple-element.58.w_ref, ...), custom_call_target="tpu_custom_call" | custom-call | flops 100 | bytes 100 | tf_op jit(solution)/shard_map/queries/pallas_call | solution.py:238
  41.3 1.2 %gather.2 = (bf16[4,272,256]{2,1,0:T(8,128)(2,1)S(1)}, bf16[2,128,128]{2,1,0:T(8,128)(2,1)S(1)}) custom-call(s32[2]{0:T(128)S(1)} %pad_add_fusion.sc_ref, bf16[272,256]{1,0:T(8,128)(2,1)S(1)} %get-tuple-element.71.p0, bf16[272,256]{1,0:T(8,128)(2,1)S(1)} %collective-permute-done.2.p1, bf16[272,256]{1,0:T(8,128)(2,1)S(1)} %collective-permute-done.3.p2, ...), custom_call_target="tpu_custom_call" | custom-call | flops 100 | bytes 100 | tf_op jit(solution)/shard_map/gather/pallas_call | solution.py:238
  42.4 1.3 %collective-permute-start.5 = (bf16[2,128,128]{2,1,0:T(8,128)(2,1)S(1)}, bf16[2,128,128]{2,1,0:T(8,128)(2,1)S(1)}, u32[]{:S(2)}, u32[]{:S(2)}) collective-permute-start(bf16[2,128,128]{2,1,0:T(8,128)(2,1)S(1)} %get-tuple-element.76), channel_id=1, source_target_pairs={{0,8},{1,9},{2,10},{3,11},{4,12},{5,13},{6,14},{7,15},{16,24},{17,... | collective-permute-start | bytes 196616 | tf_op jit(solution)/shard_map/ppermute | solution.py:471
  43.7 1.0 %spread.3 = (bf16[2,128,128]{2,1,0:T(8,128)(2,1)S(1)}, bf16[2,128,128]{2,1,0:T(8,128)(2,1)S(1)}, bf16[2,128,128]{2,1,0:T(8,128)(2,1)S(1)}, bf16[2,128,128]{2,1,0:T(8,128)(2,1)S(1)}) custom-call(s32[2]{0:T(128)S(1)} %pad_add_fusion.sc_ref, bf16[4,272,256]{2,1,0:T(8,128)(2,1)S(1)} %get-tuple-element.98.order_ref, ...), custom_call_target="tpu_custom_call" | custom-call | flops 100 | bytes 100 | tf_op jit(solution)/shard_map/spread/pallas_call | solution.py:238
  45.4 1.6 %collective-permute-start.15 = (bf16[2,128,128]{2,1,0:T(8,128)(2,1)S(1)}, bf16[2,128,128]{2,1,0:T(8,128)(2,1)S(1)}, u32[]{:S(2)}, u32[]{:S(2)}) collective-permute-start(bf16[2,128,128]{2,1,0:T(8,128)(2,1)S(1)} %get-tuple-element.102), channel_id=1, source_target_pairs={{0,4},{1,5},{2,6},{3,7},{4,0},{5,1},{6,2},{7,3},{8,12},{9,13},{10,... | collective-permute-start | bytes 196616 | tf_op jit(solution)/shard_map/ppermute | solution.py:475
  47.0 1.3 %collective-permute-start.16 = (bf16[2,128,128]{2,1,0:T(8,128)(2,1)S(1)}, bf16[2,128,128]{2,1,0:T(8,128)(2,1)S(1)}, u32[]{:S(2)}, u32[]{:S(2)}) collective-permute-start(bf16[2,128,128]{2,1,0:T(8,128)(2,1)S(1)} %get-tuple-element.103), channel_id=1, source_target_pairs={{0,6},{1,7},{2,4},{3,5},{4,2},{5,3},{6,0},{7,1},{8,14},{9,15},{10,... | collective-permute-start | bytes 196616 | tf_op jit(solution)/shard_map/ppermute | solution.py:475
  48.3 1.0 %spread.2 = (bf16[2,128,128]{2,1,0:T(8,128)(2,1)S(1)}, bf16[2,128,128]{2,1,0:T(8,128)(2,1)S(1)}, bf16[2,128,128]{2,1,0:T(8,128)(2,1)S(1)}, bf16[2,128,128]{2,1,0:T(8,128)(2,1)S(1)}) custom-call(s32[2]{0:T(128)S(1)} %pad_add_fusion.sc_ref, bf16[4,272,256]{2,1,0:T(8,128)(2,1)S(1)} %get-tuple-element.75.order_ref, ...), custom_call_target="tpu_custom_call" | custom-call | flops 100 | bytes 100 | tf_op jit(solution)/shard_map/spread/pallas_call | solution.py:238
  50.0 1.6 %collective-permute-start.7 = (bf16[2,128,128]{2,1,0:T(8,128)(2,1)S(1)}, bf16[2,128,128]{2,1,0:T(8,128)(2,1)S(1)}, u32[]{:S(2)}, u32[]{:S(2)}) collective-permute-start(bf16[2,128,128]{2,1,0:T(8,128)(2,1)S(1)} %get-tuple-element.79), channel_id=1, source_target_pairs={{0,4},{1,5},{2,6},{3,7},{4,0},{5,1},{6,2},{7,3},{8,12},{9,13},{10,... | collective-permute-start | bytes 196616 | tf_op jit(solution)/shard_map/ppermute | solution.py:475
  51.6 1.3 %collective-permute-start.8 = (bf16[2,128,128]{2,1,0:T(8,128)(2,1)S(1)}, bf16[2,128,128]{2,1,0:T(8,128)(2,1)S(1)}, u32[]{:S(2)}, u32[]{:S(2)}) collective-permute-start(bf16[2,128,128]{2,1,0:T(8,128)(2,1)S(1)} %get-tuple-element.80), channel_id=1, source_target_pairs={{0,6},{1,7},{2,4},{3,5},{4,2},{5,3},{6,0},{7,1},{8,14},{9,15},{10,... | collective-permute-start | bytes 196616 | tf_op jit(solution)/shard_map/ppermute | solution.py:475
  52.9 0.8 %enter.3 = (bf16[4,2,128,128]{3,2,1,0:T(8,128)(2,1)S(1)}, bf16[4,2,128,128]{3,2,1,0:T(8,128)(2,1)S(1)}) custom-call(s32[2]{0:T(128)S(1)} %pad_add_fusion.sc_ref, bf16[4,272,256]{2,1,0:T(8,128)(2,1)S(1)} %get-tuple-element.84.first_ref, bf16[2,128,128]{2,1,0:T(8,128)(2,1)S(1)} %get-tuple-element.100.refs_0_, ...), custom_call_target="tpu_custom_call" | custom-call | flops 100 | bytes 100 | tf_op jit(solution)/shard_map/enter/pallas_call | solution.py:238
  54.3 2.5 %collective-permute-done.8.refs_3_ = bf16[2,128,128]{2,1,0:T(8,128)(2,1)S(1)} collective-permute-done((bf16[2,128,128]{2,1,0:T(8,128)(2,1)S(1)}, bf16[2,128,128]{2,1,0:T(8,128)(2,1)S(1)}, u32[]{:S(2)}, u32[]{:S(2)}) %collective-permute-start.8) | collective-permute-done | bytes 65568 | tf_op jit(solution)/shard_map/ppermute | solution.py:475
  57.7 1.3 %finish.1.done_ref = bf16[4,128,512]{2,1,0:T(8,128)(2,1)S(1)} custom-call(s32[2]{0:T(128)S(1)} %pad_add_fusion.sc_ref, bf16[128,4096]{1,0:T(8,128)(2,1)S(1)} %copy-done, f32[1,128]{1,0:T(1,128)S(1)} %bitcast.7, bf16[4,2,128,128]{3,2,1,0:T(8,128)(2,1)S(1)} %get-tuple-element.81.refs_0_, f32[4,2,128,128]{3,2,1,0:T(8,128)S(1)} %get-tuple-element.68.refs_1_, ...), custom_call_target="tpu_custom_call" | custom-call | flops 100 | bytes 100 | tf_op jit(solution)/shard_map/finish/pallas_call | solution.py:238
  59.2 2.0 %finish_last.1 = bf16[128,4096]{1,0:T(8,128)(2,1)} custom-call(s32[2]{0:T(128)S(1)} %pad_add_fusion.sc_ref, bf16[128,4096]{1,0:T(8,128)(2,1)S(1)} %copy-done, f32[1,128]{1,0:T(1,128)S(1)} %bitcast.8, bf16[4,128,512]{2,1,0:T(8,128)(2,1)S(1)} %finish.1.done_ref, bf16[4,2,128,128]{3,2,1,0:T(8,128)(2,1)S(1)} %collective-permute-done.17.refs_0_, ...), custom_call_target="tpu_custom_call" | custom-call | flops 100 | bytes 100 | tf_op jit(solution)/shard_map/finish_last/pallas_call | solution.py:454
  (37 shorter events, 3.5 us)
Async XLA Ops:
  0.0 4.1 %copy-start.2 = (f32[128,32]{0,1:T(8,128)S(1)}, f32[128,32]{0,1:T(8,128)}, u32[]{:S(2)}) copy-start(f32[128,32]{0,1:T(8,128)} %param.10) | copy-start | bytes 49156
  0.0 4.1 %copy-start.3 = (bf16[128,32]{0,1:T(8,128)(2,1)S(1)}, bf16[128,32]{0,1:T(8,128)(2,1)}, u32[]{:S(2)}) copy-start(bf16[128,32]{0,1:T(8,128)(2,1)} %param.9) | copy-start | bytes 24580
  1.7 4.8 %collective-permute-start = (bf16[4,8192]{1,0:T(4,128)(2,1)S(1)}, bf16[4,8192]{1,0:T(4,128)(2,1)S(1)}, u32[]{:S(2)}, u32[]{:S(2)}) collective-permute-start(bf16[4,8192]{1,0:T(4,128)(2,1)S(1)} %get-tuple-element.57), channel_id=1, source_target_pairs={{0,1},{1,2},{2,3},{3,4},{4,5},{5,6},{6,7},{7,8},{8,9},{9,10},{10,1... | collective-permute-start | bytes 196616 | tf_op jit(solution)/shard_map/ppermute | solution.py:471
  4.3 2.1 %copy-start.1 = (bf16[7,128,128]{2,1,0:T(8,128)(2,1)S(1)}, bf16[7,128,128]{2,1,0:T(8,128)(2,1)}, u32[]{:S(2)}) copy-start(bf16[7,128,128]{2,1,0:T(8,128)(2,1)} %constant.42.clone.masks_ref) | copy-start | bytes 688132
  11.7 8.0 %collective-permute-start.9 = (bf16[4,272,256]{2,1,0:T(8,128)(2,1)S(1)}, bf16[4,272,256]{2,1,0:T(8,128)(2,1)S(1)}, u32[]{:S(2)}, u32[]{:S(2)}) collective-permute-start(bf16[4,272,256]{2,1,0:T(8,128)(2,1)S(1)} %get-tuple-element.83), channel_id=1, source_target_pairs={{0,1},{1,0},{2,3},{3,2},{4,5},{5,4},{6,7},{7,6},{8,9},{9,8},{10,11... | collective-permute-start | bytes 1671176 | tf_op jit(solution)/shard_map/ppermute | solution.py:475
  19.7 5.1 %collective-permute-start.1 = (bf16[4,272,256]{2,1,0:T(8,128)(2,1)S(1)}, bf16[4,272,256]{2,1,0:T(8,128)(2,1)S(1)}, u32[]{:S(2)}, u32[]{:S(2)}) collective-permute-start(bf16[4,272,256]{2,1,0:T(8,128)(2,1)S(1)} %get-tuple-element.60), channel_id=1, source_target_pairs={{0,1},{1,0},{2,3},{3,2},{4,5},{5,4},{6,7},{7,6},{8,9},{9,8},{10,11... | collective-permute-start | bytes 1671176 | tf_op jit(solution)/shard_map/ppermute | solution.py:475
  20.7 7.7 %collective-permute-start.10 = (bf16[272,256]{1,0:T(8,128)(2,1)S(1)}, bf16[272,256]{1,0:T(8,128)(2,1)S(1)}, u32[]{:S(2)}, u32[]{:S(2)}) collective-permute-start(bf16[272,256]{1,0:T(8,128)(2,1)S(1)} %get-tuple-element.95), channel_id=1, source_target_pairs={{0,2},{1,3},{2,0},{3,1},{4,6},{5,7},{6,4},{7,5},{8,10},{9,11},{10,... | collective-permute-start | bytes 417800 | tf_op jit(solution)/shard_map/ppermute | solution.py:475
  22.3 9.8 %collective-permute-start.11 = (bf16[272,256]{1,0:T(8,128)(2,1)S(1)}, bf16[272,256]{1,0:T(8,128)(2,1)S(1)}, u32[]{:S(2)}, u32[]{:S(2)}) collective-permute-start(bf16[272,256]{1,0:T(8,128)(2,1)S(1)} %get-tuple-element.96), channel_id=1, source_target_pairs={{0,4},{1,5},{2,6},{3,7},{4,0},{5,1},{6,2},{7,3},{8,12},{9,13},{10,... | collective-permute-start | bytes 417800 | tf_op jit(solution)/shard_map/ppermute | solution.py:475
  23.9 8.4 %collective-permute-start.12 = (bf16[272,256]{1,0:T(8,128)(2,1)S(1)}, bf16[272,256]{1,0:T(8,128)(2,1)S(1)}, u32[]{:S(2)}, u32[]{:S(2)}) collective-permute-start(bf16[272,256]{1,0:T(8,128)(2,1)S(1)} %get-tuple-element.97), channel_id=1, source_target_pairs={{0,6},{1,7},{2,4},{3,5},{4,2},{5,3},{6,0},{7,1},{8,14},{9,15},{10,... | collective-permute-start | bytes 417800 | tf_op jit(solution)/shard_map/ppermute | solution.py:475
  25.7 15.5 %collective-permute-start.2 = (bf16[272,256]{1,0:T(8,128)(2,1)S(1)}, bf16[272,256]{1,0:T(8,128)(2,1)S(1)}, u32[]{:S(2)}, u32[]{:S(2)}) collective-permute-start(bf16[272,256]{1,0:T(8,128)(2,1)S(1)} %get-tuple-element.72), channel_id=1, source_target_pairs={{0,2},{1,3},{2,0},{3,1},{4,6},{5,7},{6,4},{7,5},{8,10},{9,11},{10,... | collective-permute-start | bytes 417800 | tf_op jit(solution)/shard_map/ppermute | solution.py:475
  26.8 14.4 %collective-permute-start.3 = (bf16[272,256]{1,0:T(8,128)(2,1)S(1)}, bf16[272,256]{1,0:T(8,128)(2,1)S(1)}, u32[]{:S(2)}, u32[]{:S(2)}) collective-permute-start(bf16[272,256]{1,0:T(8,128)(2,1)S(1)} %get-tuple-element.73), channel_id=1, source_target_pairs={{0,4},{1,5},{2,6},{3,7},{4,0},{5,1},{6,2},{7,3},{8,12},{9,13},{10,... | collective-permute-start | bytes 417800 | tf_op jit(solution)/shard_map/ppermute | solution.py:475
  28.4 12.8 %collective-permute-start.4 = (bf16[272,256]{1,0:T(8,128)(2,1)S(1)}, bf16[272,256]{1,0:T(8,128)(2,1)S(1)}, u32[]{:S(2)}, u32[]{:S(2)}) collective-permute-start(bf16[272,256]{1,0:T(8,128)(2,1)S(1)} %get-tuple-element.74), channel_id=1, source_target_pairs={{0,6},{1,7},{2,4},{3,5},{4,2},{5,3},{6,0},{7,1},{8,14},{9,15},{10,... | collective-permute-start | bytes 417800 | tf_op jit(solution)/shard_map/ppermute | solution.py:475
  33.5 10.2 %collective-permute-start.13 = (bf16[2,128,128]{2,1,0:T(8,128)(2,1)S(1)}, bf16[2,128,128]{2,1,0:T(8,128)(2,1)S(1)}, u32[]{:S(2)}, u32[]{:S(2)}) collective-permute-start(bf16[2,128,128]{2,1,0:T(8,128)(2,1)S(1)} %get-tuple-element.99), channel_id=1, source_target_pairs={{0,8},{1,9},{2,10},{3,11},{4,12},{5,13},{6,14},{7,15},{16,24},{17,... | collective-permute-start | bytes 196616 | tf_op jit(solution)/shard_map/ppermute | solution.py:471
  41.2 16.5 %copy-start = (bf16[128,4096]{1,0:T(8,128)(2,1)S(1)}, bf16[128,4096]{1,0:T(8,128)(2,1)}, u32[]{:S(2)}) copy-start(bf16[128,4096]{1,0:T(8,128)(2,1)} %gate_ref.3) | copy-start | bytes 3145732
  41.2 16.5 %copy-start.4 = (f32[128]{0:T(128)S(1)}, f32[128]{0:T(128)}, u32[]{:S(2)}) copy-start(f32[128]{0:T(128)} %param.12) | copy-start | bytes 1540
  42.4 5.9 %collective-permute-start.5 = (bf16[2,128,128]{2,1,0:T(8,128)(2,1)S(1)}, bf16[2,128,128]{2,1,0:T(8,128)(2,1)S(1)}, u32[]{:S(2)}, u32[]{:S(2)}) collective-permute-start(bf16[2,128,128]{2,1,0:T(8,128)(2,1)S(1)} %get-tuple-element.76), channel_id=1, source_target_pairs={{0,8},{1,9},{2,10},{3,11},{4,12},{5,13},{6,14},{7,15},{16,24},{17,... | collective-permute-start | bytes 196616 | tf_op jit(solution)/shard_map/ppermute | solution.py:471
  44.8 6.8 %collective-permute-start.14 = (bf16[2,128,128]{2,1,0:T(8,128)(2,1)S(1)}, bf16[2,128,128]{2,1,0:T(8,128)(2,1)S(1)}, u32[]{:S(2)}, u32[]{:S(2)}) collective-permute-start(bf16[2,128,128]{2,1,0:T(8,128)(2,1)S(1)} %get-tuple-element.101), channel_id=1, source_target_pairs={{0,2},{1,3},{2,0},{3,1},{4,6},{5,7},{6,4},{7,5},{8,10},{9,11},{10,... | collective-permute-start | bytes 196616 | tf_op jit(solution)/shard_map/ppermute | solution.py:475
  45.4 7.5 %collective-permute-start.15 = (bf16[2,128,128]{2,1,0:T(8,128)(2,1)S(1)}, bf16[2,128,128]{2,1,0:T(8,128)(2,1)S(1)}, u32[]{:S(2)}, u32[]{:S(2)}) collective-permute-start(bf16[2,128,128]{2,1,0:T(8,128)(2,1)S(1)} %get-tuple-element.102), channel_id=1, source_target_pairs={{0,4},{1,5},{2,6},{3,7},{4,0},{5,1},{6,2},{7,3},{8,12},{9,13},{10,... | collective-permute-start | bytes 196616 | tf_op jit(solution)/shard_map/ppermute | solution.py:475
  47.0 5.9 %collective-permute-start.16 = (bf16[2,128,128]{2,1,0:T(8,128)(2,1)S(1)}, bf16[2,128,128]{2,1,0:T(8,128)(2,1)S(1)}, u32[]{:S(2)}, u32[]{:S(2)}) collective-permute-start(bf16[2,128,128]{2,1,0:T(8,128)(2,1)S(1)} %get-tuple-element.103), channel_id=1, source_target_pairs={{0,6},{1,7},{2,4},{3,5},{4,2},{5,3},{6,0},{7,1},{8,14},{9,15},{10,... | collective-permute-start | bytes 196616 | tf_op jit(solution)/shard_map/ppermute | solution.py:475
  49.3 4.5 %collective-permute-start.6 = (bf16[2,128,128]{2,1,0:T(8,128)(2,1)S(1)}, bf16[2,128,128]{2,1,0:T(8,128)(2,1)S(1)}, u32[]{:S(2)}, u32[]{:S(2)}) collective-permute-start(bf16[2,128,128]{2,1,0:T(8,128)(2,1)S(1)} %get-tuple-element.78), channel_id=1, source_target_pairs={{0,2},{1,3},{2,0},{3,1},{4,6},{5,7},{6,4},{7,5},{8,10},{9,11},{10,... | collective-permute-start | bytes 196616 | tf_op jit(solution)/shard_map/ppermute | solution.py:475
  50.0 4.3 %collective-permute-start.7 = (bf16[2,128,128]{2,1,0:T(8,128)(2,1)S(1)}, bf16[2,128,128]{2,1,0:T(8,128)(2,1)S(1)}, u32[]{:S(2)}, u32[]{:S(2)}) collective-permute-start(bf16[2,128,128]{2,1,0:T(8,128)(2,1)S(1)} %get-tuple-element.79), channel_id=1, source_target_pairs={{0,4},{1,5},{2,6},{3,7},{4,0},{5,1},{6,2},{7,3},{8,12},{9,13},{10,... | collective-permute-start | bytes 196616 | tf_op jit(solution)/shard_map/ppermute | solution.py:475
  51.6 5.2 %collective-permute-start.8 = (bf16[2,128,128]{2,1,0:T(8,128)(2,1)S(1)}, bf16[2,128,128]{2,1,0:T(8,128)(2,1)S(1)}, u32[]{:S(2)}, u32[]{:S(2)}) collective-permute-start(bf16[2,128,128]{2,1,0:T(8,128)(2,1)S(1)} %get-tuple-element.80), channel_id=1, source_target_pairs={{0,6},{1,7},{2,4},{3,5},{4,2},{5,3},{6,0},{7,1},{8,14},{9,15},{10,... | collective-permute-start | bytes 196616 | tf_op jit(solution)/shard_map/ppermute | solution.py:475
  53.7 5.3 %collective-permute-start.18 = (bf16[4,2,128,128]{3,2,1,0:T(8,128)(2,1)S(1)}, bf16[4,2,128,128]{3,2,1,0:T(8,128)(2,1)S(1)}, u32[]{:S(2)}, u32[]{:S(2)}) collective-permute-start(bf16[4,2,128,128]{3,2,1,0:T(8,128)(2,1)S(1)} %get-tuple-element.106), channel_id=1, source_target_pairs={{0,1},{1,0},{2,3},{3,2},{4,5},{5,4},{6,7},{7,6},{8,9},{9,8},{10,11... | collective-permute-start | bytes 786440 | tf_op jit(solution)/shard_map/ppermute | solution.py:475
  57.6 1.6 %collective-permute-start.17 = (bf16[4,2,128,128]{3,2,1,0:T(8,128)(2,1)S(1)}, bf16[4,2,128,128]{3,2,1,0:T(8,128)(2,1)S(1)}, u32[]{:S(2)}, u32[]{:S(2)}) collective-permute-start(bf16[4,2,128,128]{3,2,1,0:T(8,128)(2,1)S(1)} %get-tuple-element.105), channel_id=1, source_target_pairs={{0,1},{1,0},{2,3},{3,2},{4,5},{5,4},{6,7},{7,6},{8,9},{9,8},{10,11... | collective-permute-start | bytes 786440 | tf_op jit(solution)/shard_map/ppermute | solution.py:475

commit v4 on v3

--- a/solution.py
+++ b/solution.py
@@ -178,6 +178,7 @@
             cv = conv(slot + 1, 2 * (KH + key_at) * DH, vd)
             slot += 2
             rows = rows_ref[piece]
+            following = pltpu.roll(rows, CH - 1, axis=1)
             cols = rows.T
             grow_cols = jnp.exp(cols)
             tail_rows = jnp.exp(rows[:, CH - 1 : CH] - rows)
@@ -196,7 +197,7 @@
                     system = key_dot * decay_pairs(rows, cols, h)
                     system = jnp.where(strict, system, 0.0).astype(BF16)
                     beta_row = rows[4 + h : 5 + h]
-                    gains = (cols[:, 4 + h : 5 + h] * beta_row).astype(BF16)
+                    gains = jnp.broadcast_to(beta_row * following[4 + h : 5 + h], (CH, CH)).astype(BF16)
                     high, low = halves(jnp.broadcast_to(beta_row, (CH, CH)))
                     heads.append(
                         dict(
@@ -301,50 +302,53 @@
     return first, sent
 
 
-def queries_kernel(keys, mine, sc_ref, x_ref, rim_ref, w_ref, rows_ref, solved_ref, key_ref, *refs):
-    loc_ref, car_ref, scr = refs
-    owner = sc_ref[0] if mine else 1 - sc_ref[0]
+def queries_kernel(keys, sc_ref, x_ref, rim_ref, w_ref, rows_ref, *refs):
+    ins, outs, scr = (refs[0:2], refs[2:4]), (refs[4:6], refs[6:8]), refs[8]
     t_at, s_at = token_order()
     heads = []
-    for offset in range(CHIPS):
-        piece = owner * (VH // 2 // PIECE) + (sc_ref[1] ^ offset)
-        kd = len(keys) * DH
-        key_at = piece * PIECE // 2 + keys[0]
-        cq = convolved(x_ref, rim_ref, w_ref, scr, offset, key_at * DH, kd)
-        rows = rows_ref[piece]
-        cols = rows.T
-        grow_cols = jnp.exp(cols)
-        for g, key in enumerate(keys):
-            q_f = cq[:, head_slice(g)]
-            k_t = key_ref[offset, g].astype(F32).T
-            rq_col = inverse_norms(q_f, 1) * DH ** (-0.5)
-            query_dot = dot(q_f.astype(BF16), k_t.astype(BF16)) * rq_col * inverse_norms(k_t, 0)
-            for i in range(2):
-                h = 2 * key + i
-                mixing = query_dot * decay_pairs(rows, cols, h)
-                mixing = halves(jnp.where(t_at >= s_at, mixing, 0.0))
-                query = q_f * (grow_cols[:, h : h + 1] * rq_col)
-                heads.append((offset, 2 * g + i, mixing, query))
-    for offset, h, mixing, query in heads:
+    for own, ((solved_ref, key_ref), out) in enumerate(zip(ins, outs)):
+        owner = sc_ref[0] if own else 1 - sc_ref[0]
+        for offset in range(CHIPS):
+            piece = owner * (VH // 2 // PIECE) + (sc_ref[1] ^ offset)
+            kd = len(keys) * DH
+            key_at = piece * PIECE // 2 + keys[0]
+            cq = convolved(x_ref, rim_ref, w_ref, scr, own * CHIPS + offset, key_at * DH, kd)
+            rows = rows_ref[piece]
+            cols = rows.T
+            grow_cols = jnp.exp(cols)
+            for g, key in enumerate(keys):
+                q_f = cq[:, head_slice(g)]
+                k_t = key_ref[offset, g].astype(F32).T
+                rq_col = inverse_norms(q_f, 1) * DH ** (-0.5)
+                query_dot = dot(q_f.astype(BF16), k_t.astype(BF16)) * rq_col * inverse_norms(k_t, 0)
+                for i in range(2):
+                    h = 2 * key + i
+                    mixing = query_dot * decay_pairs(rows, cols, h)
+                    mixing = halves(jnp.where(t_at >= s_at, mixing, 0.0))
+                    query = q_f * (grow_cols[:, h : h + 1] * rq_col)
+                    heads.append((solved_ref, out, offset, 2 * g + i, mixing, query))
+    for solved_ref, (loc_ref, car_ref), offset, h, mixing, query in heads:
         solved = solved_ref[offset, h]
         both = dot(jnp.concatenate(mixing, axis=1), jnp.concatenate([solved, solved], axis=0))
         loc_ref[offset, h] = both[:, DH:]
         car_ref[offset, h] = (query - both[:, :DH]).astype(BF16)
 
 
-def block_queries(keys, mine, place, shared, solved, key_rows):
+def block_queries(keys, place, shared, theirs, mine):
     count = 2 * len(keys)
-    return local_call(
-        functools.partial(queries_kernel, keys, mine),
-        [place, *shared[:3], shared[4], solved, key_rows],
+    out = local_call(
+        functools.partial(queries_kernel, keys),
+        [place, *shared[:3], shared[4], *theirs, *mine],
         [
             jax.ShapeDtypeStruct((CHIPS, count, CH, DH), F32),
             jax.ShapeDtypeStruct((CHIPS, count, CH, DH), BF16),
-        ],
-        [pltpu.VMEM((CHIPS, CH + 8, len(keys) * DH), F32)],
+        ]
+        * 2,
+        [pltpu.VMEM((2 * CHIPS, CH + 8, len(keys) * DH), F32)],
         vmem_mib=24,
         name="queries",
     )
+    return out[:2], out[2:]
 
 
 def decays_at(ref, slot):
@@ -361,12 +365,19 @@
 def gather_kernel(keys, sc_ref, p0, p1, p2, p3, in_ref, order_ref, out_ref):
     for offset, piece in enumerate((p0, p1, p2, p3)):
         order_ref[sc_ref[1] ^ offset] = piece[...]
-    states = [in_ref[h] for h in range(2 * len(keys))]
-    for chip in range(CHIPS):
-        decays = decays_at(order_ref, chip)
-        states = [advance(keys, order_ref, chip, h, decays, s) for h, s in enumerate(states)]
-    for h, state in enumerate(states):
-        out_ref[h] = state
+
+    @pl.when(sc_ref[2] == 0)
+    def _():
+        states = [in_ref[h] for h in range(2 * len(keys))]
+        for chip in range(CHIPS):
+            decays = decays_at(order_ref, chip)
+            states = [advance(keys, order_ref, chip, h, decays, s) for h, s in enumerate(states)]
+        for h, state in enumerate(states):
+            out_ref[h] = state
+
+    @pl.when(sc_ref[2] == 1)
+    def _():
+        out_ref[...] = jnp.zeros_like(out_ref)
 
 
 def spread_kernel(keys, sc_ref, order_ref, in_ref, o0, o1, o2, o3, scr):
@@ -393,41 +404,47 @@
             send_ref[offset, h] = jnp.where(is_first, after, start)
 
 
+def gates_kernel(gate_ref, gain_ref, out_ref):
+    gates = gate_ref[...].astype(F32)
+    gates = gates / (1.0 + jnp.exp(-gates))
+    for h in range(VH):
+        out_ref[:, head_slice(h)] = gates[:, head_slice(h)] * gain_ref[...]
+
+
 def piece_columns(own, sc_ref, offset):
     owner = sc_ref[0] if own else 1 - sc_ref[0]
     piece = owner * (VH // 2 // PIECE) + (sc_ref[1] ^ offset)
     return pl.ds(pl.multiple_of(piece * PIECE * DH, PIECE * DH), PIECE * DH)
 
 
-def finish_piece(own, offset, sc_ref, gate_ref, gain_ref, bands, out_ref):
-    gates = gate_ref[:, piece_columns(own, sc_ref, offset)].astype(F32)
-    gates = gates / (1.0 + jnp.exp(-gates))
+def finish_piece(own, offset, sc_ref, gate_ref, bands, out_ref):
+    gates = gate_ref[:, piece_columns(own, sc_ref, offset)]
     for keys, (state_ref, loc_ref, car_ref) in zip(BANDS, bands):
         for h in range(2 * len(keys)):
             core = loc_ref[offset, h] + dot(car_ref[offset, h], state_ref[offset, h])
             mean_sq = jnp.mean(core * core, axis=1, keepdims=True)
             cols = head_slice(2 * keys[0] + h)
-            scaled = core * lax.rsqrt(mean_sq + 1e-06) * gain_ref[...] * gates[:, cols]
+            scaled = core * lax.rsqrt(mean_sq + 1e-06) * gates[:, cols]
             out_ref[offset, :, cols] = scaled.astype(BF16)
 
 
-def finish_kernel(sc_ref, gate_ref, gain_ref, *refs):
+def finish_kernel(sc_ref, gate_ref, *refs):
     bands = [refs[3 * b : 3 * b + 3] for b in range(len(BANDS))]
     for offset in range(CHIPS):
-        finish_piece(1, offset, sc_ref, gate_ref, gain_ref, bands, refs[-1])
-
-
-def finish(place, gate_in, gain, terms):
+        finish_piece(1, offset, sc_ref, gate_ref, bands, refs[-1])
+
+
+def finish(place, gates, terms):
     return local_call(
         finish_kernel,
-        [place, gate_in, gain, *terms],
+        [place, gates, *terms],
         [jax.ShapeDtypeStruct((CHIPS, CH, PIECE * DH), BF16)],
         vmem_mib=4,
         name="finish",
     )[0]
 
 
-def last_kernel(sc_ref, gate_ref, gain_ref, done_ref, *refs):
+def last_kernel(sc_ref, gate_ref, done_ref, *refs):
     bands = [refs[3 * b : 3 * b + 3] for b in range(len(BANDS))]
     out_ref, scr, sems = refs[-3:]
     copies = []
@@ -442,18 +459,18 @@
     for offset in range(CHIPS):
         send(1, done_ref, offset)
     for offset in range(CHIPS):
-        finish_piece(0, offset, sc_ref, gate_ref, gain_ref, bands, scr)
+        finish_piece(0, offset, sc_ref, gate_ref, bands, scr)
         send(0, scr, offset)
     for copy in copies:
         copy.wait()
 
 
-def finish_last(place, gate_in, gain, done, terms):
+def finish_last(place, gates, done, terms):
     vmem = pl.BlockSpec(memory_space=pltpu.VMEM)
-    args = [place, gate_in, gain, done, *terms]
+    args = [place, gates, done, *terms]
     return pl.pallas_call(
         last_kernel,
-        out_shape=jax.ShapeDtypeStruct(gate_in.shape, BF16),
+        out_shape=jax.ShapeDtypeStruct(gates.shape, BF16),
         in_specs=[pl.BlockSpec(memory_space=pltpu.SMEM)] + [vmem] * (len(args) - 1),
         out_specs=pl.BlockSpec(memory_space=pl.ANY),
         scratch_shapes=[
@@ -484,7 +501,8 @@
 
 def local(mixed_qkv, conv_weight, beta_logit, log_decay, gate_in, norm_gain):
     at = lax.axis_index("seq")
-    place = jnp.stack([at % 2, (at // 2) % CHIPS])
+    last = at // (2 * CHIPS) == lax.axis_size("seq") // (2 * CHIPS) - 1
+    place = jnp.stack([at % 2, (at // 2) % CHIPS, last.astype(at.dtype)])
     x, weight, last_rows = load(mixed_qkv, conv_weight)
     rim = shift(last_rows, 1)
     (rows,) = local_call(
@@ -498,15 +516,20 @@
     shared = (x, rim, weight, conv_out, rows, jnp.asarray(level_masks()))
     chips = range(CHIPS)
     finals = [[], []]
+    (gates,) = local_call(
+        gates_kernel,
+        [gate_in, norm_gain[None]],
+        [jax.ShapeDtypeStruct(gate_in.shape, F32)],
+        scalars=0,
+        vmem_mib=4,
+        name="gates",
+    )
     for keys in BANDS:
         theirs, mine = block_terms(keys, place, shared)
         other = swap(theirs[0], 1)
         first, sent = compose(keys, place, mine[0], other)
         pieces = [swap(sent[n], 2 * n) if n else sent[0] for n in range(CHIPS)]
-        queries = [
-            block_queries(keys, own, place, shared, *part[1:])
-            for own, part in enumerate((theirs, mine))
-        ]
+        queries = block_queries(keys, place, shared, theirs[1:], mine[1:])
         turn, _ = lax.optimization_barrier((place, queries))
 
         count = 2 * len(keys)
@@ -532,15 +555,14 @@
         states_shape = jax.ShapeDtypeStruct((CHIPS, count, DH, DH), BF16)
         keep, send = local_call(
             functools.partial(enter_kernel, keys),
-            [place, first, *starts],
+            [turn if keys == BANDS[0] else lax.optimization_barrier((turn, gates))[0], first, *starts],
             [states_shape, states_shape],
             name="enter",
         )
         for own, state in enumerate((swap(send, 1), keep)):
             finals[own] += [state, *queries[own]]
-    gain = norm_gain[None]
-    done = finish(place, gate_in, gain, finals[1])
-    return finish_last(place, gate_in, gain, done, finals[0])
+    done = finish(place, gates, finals[1])
+    return finish_last(place, gates, done, finals[0])
 
 
 def solution(mesh):

time: 61.6 us -> 59.5 us (0.966)
  Pallas kernels: 31.1 us -> 29 us
    pallas_call x17 -> x16, Pallas kernels: 27.5 us -> 25.6 us  [local_call(): pl.pallas_call(kernel, out_shape=out_shape, in_specs=in_specs, out_specs=...]
  transfers between devices with their start and end apart: 19 -> 19, of which waited for: 4 -> 4; matrix products, arithmetic and copies ran while one was open for 0% -> 0% of each run, Pallas kernels for 36% -> 35%
where the time goes in v4:
time: 59.5 us; the launch traced here: 59.3 us
  Pallas kernels  29 us (49%)
  starting transfers between devices  26.2 us (44%)
  waiting for transfers between devices  3.51 us (6%)
    pallas_call x16, Pallas kernels, local_call(): pl.pallas_call(kernel, out_shape=out_shape, in_specs=in_specs, out_specs=...  25.6 us
    ppermute x16, starting transfers between devices, swap(): lax.ppermute(block, 'seq', [(i, i ^ distance) for i in range(lax.axis_siz...  18 us
    ppermute x3, starting transfers between devices, shift(): lax.ppermute(block, 'seq', [(i, i + distance) for i in range(count - dist...  8.13 us
    ppermute x16, waiting for transfers between devices, swap(): lax.ppermute(block, 'seq', [(i, i ^ distance) for i in range(lax.axis_siz...  3.5 us
    pallas_call x1, Pallas kernels, finish_last(): pl.pallas_call(last_kernel, out_shape=jax.ShapeDtypeStruct(gates.shape, B...  1.82 us
    pallas_call x1, Pallas kernels, load(): pl.pallas_call(load_kernel, out_shape=[jax.ShapeDtypeStruct(mixed_qkv.sha...  1.66 us
  transfers between devices with their start and end apart: 19, of which 4 were waited for; matrix products, arithmetic and copies ran while one was open for 0% of the time, Pallas kernels for 35%

profile of v4, /device:TPU:0, one launch (start us, length us, event | category | flops | bytes accessed | tf_op | source)
XLA Modules:
  0.0 59.3 jit_solution(6312136658158333356)
XLA Ops:
  0.0 1.7 %load.1 = (bf16[128,8192]{1,0:T(8,128)(2,1)S(1)}, bf16[4,8192]{1,0:T(4,128)(2,1)S(1)}, bf16[4,8192]{1,0:T(4,128)(2,1)S(1)}) custom-call(bf16[128,8192]{1,0:T(8,128)(2,1)} %x_ref.1, bf16[4,8192]{1,0:T(4,128)(2,1)} %w_ref.1), custom_call_target="tpu_custom_call" | custom-call | flops 100 | bytes 100 | tf_op jit(solution)/shard_map/load/pallas_call | solution.py:91
  1.7 2.4 %collective-permute-start = (bf16[4,8192]{1,0:T(4,128)(2,1)S(1)}, bf16[4,8192]{1,0:T(4,128)(2,1)S(1)}, u32[]{:S(2)}, u32[]{:S(2)}) collective-permute-start(bf16[4,8192]{1,0:T(4,128)(2,1)S(1)} %get-tuple-element.58), channel_id=1, source_target_pairs={{0,1},{1,2},{2,3},{3,4},{4,5},{5,6},{6,7},{7,8},{8,9},{9,10},{10,1... | collective-permute-start | bytes 196616 | tf_op jit(solution)/shard_map/ppermute | solution.py:488
  4.3 2.1 %conv.1.conv_ref = bf16[128,8192]{1,0:T(8,128)(2,1)S(1)} custom-call(s32[3]{0:T(128)S(1)} %pad_add_fusion.sc_ref, bf16[128,8192]{1,0:T(8,128)(2,1)S(1)} %get-tuple-element.57.x_ref, bf16[4,8192]{1,0:T(4,128)(2,1)S(1)} %get-tuple-element.59.w_ref), custom_call_target="tpu_custom_call" | custom-call | flops 100 | bytes 100 | tf_op jit(solution)/shard_map/conv/pallas_call | solution.py:239
  6.5 4.7 %terms.3 = (bf16[4,272,256]{2,1,0:T(8,128)(2,1)S(1)}, bf16[4,2,128,256]{3,2,1,0:T(8,128)(2,1)S(1)}, bf16[4,1,128,128]{3,2,1,0:T(8,128)(2,1)S(1)}, bf16[4,272,256...) custom-call(s32[3]{0:T(128)S(1)} %pad_add_fusion.sc_ref, ...), custom_call_target="tpu_custom_call" | custom-call | flops 100 | bytes 100 | tf_op jit(solution)/shard_map/terms/pallas_call | solution.py:239
  11.2 2.7 %collective-permute-start.9 = (bf16[4,272,256]{2,1,0:T(8,128)(2,1)S(1)}, bf16[4,272,256]{2,1,0:T(8,128)(2,1)S(1)}, u32[]{:S(2)}, u32[]{:S(2)}) collective-permute-start(bf16[4,272,256]{2,1,0:T(8,128)(2,1)S(1)} %get-tuple-element.94), channel_id=1, source_target_pairs={{0,1},{1,0},{2,3},{3,2},{4,5},{5,4},{6,7},{7,6},{8,9},{9,8},{10,11... | collective-permute-start | bytes 1671176 | tf_op jit(solution)/shard_map/ppermute | solution.py:492
  13.9 4.7 %terms.2 = (bf16[4,272,256]{2,1,0:T(8,128)(2,1)S(1)}, bf16[4,2,128,256]{3,2,1,0:T(8,128)(2,1)S(1)}, bf16[4,1,128,128]{3,2,1,0:T(8,128)(2,1)S(1)}, bf16[4,272,256...) custom-call(s32[3]{0:T(128)S(1)} %pad_add_fusion.sc_ref, ...), custom_call_target="tpu_custom_call" | custom-call | flops 100 | bytes 100 | tf_op jit(solution)/shard_map/terms/pallas_call | solution.py:239
  18.7 0.9 %compose.3 = (bf16[4,272,256]{2,1,0:T(8,128)(2,1)S(1)}, bf16[272,256]{1,0:T(8,128)(2,1)S(1)}, bf16[272,256]{1,0:T(8,128)(2,1)S(1)}, bf16[272,256]{1,0:T(8,128)(2,1)S(1)}, bf16[272,256]{1,0:T(8,128)(2,1)S(1)}) custom-call(s32[3]{0:T(128)S(1)} %pad_add_fusion.sc_ref, bf16[4,272,256]{2,1,0:T(8,128)(2,1)S(1)} %get-tuple-element.93.mine_ref, ...), custom_call_target="tpu_custom_call" | custom-call | flops 100 | bytes 100 | tf_op jit(solution)/shard_map/compose/pallas_call | solution.py:239
  19.7 1.7 %collective-permute-start.10 = (bf16[272,256]{1,0:T(8,128)(2,1)S(1)}, bf16[272,256]{1,0:T(8,128)(2,1)S(1)}, u32[]{:S(2)}, u32[]{:S(2)}) collective-permute-start(bf16[272,256]{1,0:T(8,128)(2,1)S(1)} %get-tuple-element.97), channel_id=1, source_target_pairs={{0,2},{1,3},{2,0},{3,1},{4,6},{5,7},{6,4},{7,5},{8,10},{9,11},{10,... | collective-permute-start | bytes 417800 | tf_op jit(solution)/shard_map/ppermute | solution.py:492
  21.3 1.6 %collective-permute-start.11 = (bf16[272,256]{1,0:T(8,128)(2,1)S(1)}, bf16[272,256]{1,0:T(8,128)(2,1)S(1)}, u32[]{:S(2)}, u32[]{:S(2)}) collective-permute-start(bf16[272,256]{1,0:T(8,128)(2,1)S(1)} %get-tuple-element.98), channel_id=1, source_target_pairs={{0,4},{1,5},{2,6},{3,7},{4,0},{5,1},{6,2},{7,3},{8,12},{9,13},{10,... | collective-permute-start | bytes 417800 | tf_op jit(solution)/shard_map/ppermute | solution.py:492
  23.8 0.9 %compose.2 = (bf16[4,272,256]{2,1,0:T(8,128)(2,1)S(1)}, bf16[272,256]{1,0:T(8,128)(2,1)S(1)}, bf16[272,256]{1,0:T(8,128)(2,1)S(1)}, bf16[272,256]{1,0:T(8,128)(2,1)S(1)}, bf16[272,256]{1,0:T(8,128)(2,1)S(1)}) custom-call(s32[3]{0:T(128)S(1)} %pad_add_fusion.sc_ref, bf16[4,272,256]{2,1,0:T(8,128)(2,1)S(1)} %get-tuple-element.69.mine_ref, ...), custom_call_target="tpu_custom_call" | custom-call | flops 100 | bytes 100 | tf_op jit(solution)/shard_map/compose/pallas_call | solution.py:239
  24.7 1.1 %collective-permute-start.2 = (bf16[272,256]{1,0:T(8,128)(2,1)S(1)}, bf16[272,256]{1,0:T(8,128)(2,1)S(1)}, u32[]{:S(2)}, u32[]{:S(2)}) collective-permute-start(bf16[272,256]{1,0:T(8,128)(2,1)S(1)} %get-tuple-element.73), channel_id=1, source_target_pairs={{0,2},{1,3},{2,0},{3,1},{4,6},{5,7},{6,4},{7,5},{8,10},{9,11},{10,... | collective-permute-start | bytes 417800 | tf_op jit(solution)/shard_map/ppermute | solution.py:492
  25.8 1.6 %collective-permute-start.3 = (bf16[272,256]{1,0:T(8,128)(2,1)S(1)}, bf16[272,256]{1,0:T(8,128)(2,1)S(1)}, u32[]{:S(2)}, u32[]{:S(2)}) collective-permute-start(bf16[272,256]{1,0:T(8,128)(2,1)S(1)} %get-tuple-element.74), channel_id=1, source_target_pairs={{0,4},{1,5},{2,6},{3,7},{4,0},{5,1},{6,2},{7,3},{8,12},{9,13},{10,... | collective-permute-start | bytes 417800 | tf_op jit(solution)/shard_map/ppermute | solution.py:492
  27.4 1.0 %collective-permute-start.4 = (bf16[272,256]{1,0:T(8,128)(2,1)S(1)}, bf16[272,256]{1,0:T(8,128)(2,1)S(1)}, u32[]{:S(2)}, u32[]{:S(2)}) collective-permute-start(bf16[272,256]{1,0:T(8,128)(2,1)S(1)} %get-tuple-element.75), channel_id=1, source_target_pairs={{0,6},{1,7},{2,4},{3,5},{4,2},{5,3},{6,0},{7,1},{8,14},{9,15},{10,... | collective-permute-start | bytes 417800 | tf_op jit(solution)/shard_map/ppermute | solution.py:492
  28.4 2.2 %queries.3 = (f32[4,2,128,128]{3,2,1,0:T(8,128)S(1)}, bf16[4,2,128,128]{3,2,1,0:T(8,128)(2,1)S(1)}, f32[4,2,128,128]{3,2,1,0:T(8,128)S(1)}, bf16[4,2,128,128]{3,2,1,0:T(8,128)(2,1)S(1)}) custom-call(s32[3]{0:T(128)S(1)} %pad_add_fusion.sc_ref, bf16[128,8192]{1,0:T(8,128)(2,1)S(1)} %get-tuple-element.57.x_ref, ...), custom_call_target="tpu_custom_call" | custom-call | flops 100 | bytes 100 | tf_op jit(solution)/shard_map/queries/pallas_call | solution.py:239
  31.3 1.2 %gather.3 = (bf16[4,272,256]{2,1,0:T(8,128)(2,1)S(1)}, bf16[2,128,128]{2,1,0:T(8,128)(2,1)S(1)}) custom-call(s32[3]{0:T(128)S(1)} %pad_add_fusion.sc_ref, bf16[272,256]{1,0:T(8,128)(2,1)S(1)} %get-tuple-element.96.p0, bf16[272,256]{1,0:T(8,128)(2,1)S(1)} %collective-permute-done.10.p1, bf16[272,256]{1,0:T(8,128)(2,1)S(1)} %collective-permute-done.11.p2, ...), custom_call_target="tpu_custom_call" | custom-call | flops 100 | bytes 100 | tf_op jit(solution)/shard_map/gather/pallas_call | solution.py:239
  32.5 4.4 %collective-permute-start.13 = (bf16[2,128,128]{2,1,0:T(8,128)(2,1)S(1)}, bf16[2,128,128]{2,1,0:T(8,128)(2,1)S(1)}, u32[]{:S(2)}, u32[]{:S(2)}) collective-permute-start(bf16[2,128,128]{2,1,0:T(8,128)(2,1)S(1)} %get-tuple-element.101), channel_id=1, source_target_pairs={{0,8},{1,9},{2,10},{3,11},{4,12},{5,13},{6,14},{7,15},{16,24},{17,... | collective-permute-start | bytes 196616 | tf_op jit(solution)/shard_map/ppermute | solution.py:488
  36.9 2.0 %queries.2 = (f32[4,2,128,128]{3,2,1,0:T(8,128)S(1)}, bf16[4,2,128,128]{3,2,1,0:T(8,128)(2,1)S(1)}, f32[4,2,128,128]{3,2,1,0:T(8,128)S(1)}, bf16[4,2,128,128]{3,2,1,0:T(8,128)(2,1)S(1)}) custom-call(s32[3]{0:T(128)S(1)} %pad_add_fusion.sc_ref, bf16[128,8192]{1,0:T(8,128)(2,1)S(1)} %get-tuple-element.57.x_ref, ...), custom_call_target="tpu_custom_call" | custom-call | flops 100 | bytes 100 | tf_op jit(solution)/shard_map/queries/pallas_call | solution.py:239
  38.9 1.2 %gather.2 = (bf16[4,272,256]{2,1,0:T(8,128)(2,1)S(1)}, bf16[2,128,128]{2,1,0:T(8,128)(2,1)S(1)}) custom-call(s32[3]{0:T(128)S(1)} %pad_add_fusion.sc_ref, bf16[272,256]{1,0:T(8,128)(2,1)S(1)} %get-tuple-element.72.p0, bf16[272,256]{1,0:T(8,128)(2,1)S(1)} %collective-permute-done.2.p1, bf16[272,256]{1,0:T(8,128)(2,1)S(1)} %collective-permute-done.3.p2, ...), custom_call_target="tpu_custom_call" | custom-call | flops 100 | bytes 100 | tf_op jit(solution)/shard_map/gather/pallas_call | solution.py:239
  40.1 1.4 %collective-permute-start.5 = (bf16[2,128,128]{2,1,0:T(8,128)(2,1)S(1)}, bf16[2,128,128]{2,1,0:T(8,128)(2,1)S(1)}, u32[]{:S(2)}, u32[]{:S(2)}) collective-permute-start(bf16[2,128,128]{2,1,0:T(8,128)(2,1)S(1)} %get-tuple-element.77), channel_id=1, source_target_pairs={{0,8},{1,9},{2,10},{3,11},{4,12},{5,13},{6,14},{7,15},{16,24},{17,... | collective-permute-start | bytes 196616 | tf_op jit(solution)/shard_map/ppermute | solution.py:488
  41.6 1.0 %spread.3 = (bf16[2,128,128]{2,1,0:T(8,128)(2,1)S(1)}, bf16[2,128,128]{2,1,0:T(8,128)(2,1)S(1)}, bf16[2,128,128]{2,1,0:T(8,128)(2,1)S(1)}, bf16[2,128,128]{2,1,0:T(8,128)(2,1)S(1)}) custom-call(s32[3]{0:T(128)S(1)} %pad_add_fusion.sc_ref, bf16[4,272,256]{2,1,0:T(8,128)(2,1)S(1)} %get-tuple-element.100.order_ref, ...), custom_call_target="tpu_custom_call" | custom-call | flops 100 | bytes 100 | tf_op jit(solution)/shard_map/spread/pallas_call | solution.py:239
  42.6 1.2 %collective-permute-start.14 = (bf16[2,128,128]{2,1,0:T(8,128)(2,1)S(1)}, bf16[2,128,128]{2,1,0:T(8,128)(2,1)S(1)}, u32[]{:S(2)}, u32[]{:S(2)}) collective-permute-start(bf16[2,128,128]{2,1,0:T(8,128)(2,1)S(1)} %get-tuple-element.103), channel_id=1, source_target_pairs={{0,2},{1,3},{2,0},{3,1},{4,6},{5,7},{6,4},{7,5},{8,10},{9,11},{10,... | collective-permute-start | bytes 196616 | tf_op jit(solution)/shard_map/ppermute | solution.py:492
  43.7 1.4 %collective-permute-start.15 = (bf16[2,128,128]{2,1,0:T(8,128)(2,1)S(1)}, bf16[2,128,128]{2,1,0:T(8,128)(2,1)S(1)}, u32[]{:S(2)}, u32[]{:S(2)}) collective-permute-start(bf16[2,128,128]{2,1,0:T(8,128)(2,1)S(1)} %get-tuple-element.104), channel_id=1, source_target_pairs={{0,4},{1,5},{2,6},{3,7},{4,0},{5,1},{6,2},{7,3},{8,12},{9,13},{10,... | collective-permute-start | bytes 196616 | tf_op jit(solution)/shard_map/ppermute | solution.py:492
  45.1 1.3 %collective-permute-start.16 = (bf16[2,128,128]{2,1,0:T(8,128)(2,1)S(1)}, bf16[2,128,128]{2,1,0:T(8,128)(2,1)S(1)}, u32[]{:S(2)}, u32[]{:S(2)}) collective-permute-start(bf16[2,128,128]{2,1,0:T(8,128)(2,1)S(1)} %get-tuple-element.105), channel_id=1, source_target_pairs={{0,6},{1,7},{2,4},{3,5},{4,2},{5,3},{6,0},{7,1},{8,14},{9,15},{10,... | collective-permute-start | bytes 196616 | tf_op jit(solution)/shard_map/ppermute | solution.py:492
  46.4 1.0 %spread.2 = (bf16[2,128,128]{2,1,0:T(8,128)(2,1)S(1)}, bf16[2,128,128]{2,1,0:T(8,128)(2,1)S(1)}, bf16[2,128,128]{2,1,0:T(8,128)(2,1)S(1)}, bf16[2,128,128]{2,1,0:T(8,128)(2,1)S(1)}) custom-call(s32[3]{0:T(128)S(1)} %pad_add_fusion.sc_ref, bf16[4,272,256]{2,1,0:T(8,128)(2,1)S(1)} %get-tuple-element.76.order_ref, ...), custom_call_target="tpu_custom_call" | custom-call | flops 100 | bytes 100 | tf_op jit(solution)/shard_map/spread/pallas_call | solution.py:239
  47.4 0.9 %collective-permute-start.6 = (bf16[2,128,128]{2,1,0:T(8,128)(2,1)S(1)}, bf16[2,128,128]{2,1,0:T(8,128)(2,1)S(1)}, u32[]{:S(2)}, u32[]{:S(2)}) collective-permute-start(bf16[2,128,128]{2,1,0:T(8,128)(2,1)S(1)} %get-tuple-element.79), channel_id=1, source_target_pairs={{0,2},{1,3},{2,0},{3,1},{4,6},{5,7},{6,4},{7,5},{8,10},{9,11},{10,... | collective-permute-start | bytes 196616 | tf_op jit(solution)/shard_map/ppermute | solution.py:492
  48.3 1.4 %collective-permute-start.7 = (bf16[2,128,128]{2,1,0:T(8,128)(2,1)S(1)}, bf16[2,128,128]{2,1,0:T(8,128)(2,1)S(1)}, u32[]{:S(2)}, u32[]{:S(2)}) collective-permute-start(bf16[2,128,128]{2,1,0:T(8,128)(2,1)S(1)} %get-tuple-element.80), channel_id=1, source_target_pairs={{0,4},{1,5},{2,6},{3,7},{4,0},{5,1},{6,2},{7,3},{8,12},{9,13},{10,... | collective-permute-start | bytes 196616 | tf_op jit(solution)/shard_map/ppermute | solution.py:492
  49.7 1.2 %collective-permute-start.8 = (bf16[2,128,128]{2,1,0:T(8,128)(2,1)S(1)}, bf16[2,128,128]{2,1,0:T(8,128)(2,1)S(1)}, u32[]{:S(2)}, u32[]{:S(2)}) collective-permute-start(bf16[2,128,128]{2,1,0:T(8,128)(2,1)S(1)} %get-tuple-element.81), channel_id=1, source_target_pairs={{0,6},{1,7},{2,4},{3,5},{4,2},{5,3},{6,0},{7,1},{8,14},{9,15},{10,... | collective-permute-start | bytes 196616 | tf_op jit(solution)/shard_map/ppermute | solution.py:492
  51.6 0.8 %enter.3 = (bf16[4,2,128,128]{3,2,1,0:T(8,128)(2,1)S(1)}, bf16[4,2,128,128]{3,2,1,0:T(8,128)(2,1)S(1)}) custom-call(s32[3]{0:T(128)S(1)} %pad_add_fusion.sc_ref, bf16[4,272,256]{2,1,0:T(8,128)(2,1)S(1)} %get-tuple-element.95.first_ref, bf16[2,128,128]{2,1,0:T(8,128)(2,1)S(1)} %get-tuple-element.102.refs_0_, ...), custom_call_target="tpu_custom_call" | custom-call | flops 100 | bytes 100 | tf_op jit(solution)/shard_map/enter/pallas_call | solution.py:239
  52.6 2.3 %collective-permute-done.8.refs_3_ = bf16[2,128,128]{2,1,0:T(8,128)(2,1)S(1)} collective-permute-done((bf16[2,128,128]{2,1,0:T(8,128)(2,1)S(1)}, bf16[2,128,128]{2,1,0:T(8,128)(2,1)S(1)}, u32[]{:S(2)}, u32[]{:S(2)}) %collective-permute-start.8) | collective-permute-done | bytes 65568 | tf_op jit(solution)/shard_map/ppermute | solution.py:492
  54.9 0.8 %enter.2 = (bf16[4,2,128,128]{3,2,1,0:T(8,128)(2,1)S(1)}, bf16[4,2,128,128]{3,2,1,0:T(8,128)(2,1)S(1)}) custom-call(s32[3]{0:T(128)S(1)} %pad_add_fusion.sc_ref, bf16[4,272,256]{2,1,0:T(8,128)(2,1)S(1)} %get-tuple-element.71.first_ref, bf16[2,128,128]{2,1,0:T(8,128)(2,1)S(1)} %get-tuple-element.78.refs_0_, ...), custom_call_target="tpu_custom_call" | custom-call | flops 100 | bytes 100 | tf_op jit(solution)/shard_map/enter/pallas_call | solution.py:239
  55.8 1.1 %finish.1.done_ref = bf16[4,128,512]{2,1,0:T(8,128)(2,1)S(1)} custom-call(s32[3]{0:T(128)S(1)} %pad_add_fusion.sc_ref, f32[128,4096]{1,0:T(8,128)S(1)} %gates.1.gate_ref, bf16[4,2,128,128]{3,2,1,0:T(8,128)(2,1)S(1)} %get-tuple-element.82.refs_0_, f32[4,2,128,128]{3,2,1,0:T(8,128)S(1)} %get-tuple-element.66.refs_1_, ...), custom_call_target="tpu_custom_call" | custom-call | flops 100 | bytes 100 | tf_op jit(solution)/shard_map/finish/pallas_call | solution.py:239
  57.3 1.8 %finish_last.1 = bf16[128,4096]{1,0:T(8,128)(2,1)} custom-call(s32[3]{0:T(128)S(1)} %pad_add_fusion.sc_ref, f32[128,4096]{1,0:T(8,128)S(1)} %gates.1.gate_ref, bf16[4,128,512]{2,1,0:T(8,128)(2,1)S(1)} %finish.1.done_ref, bf16[4,2,128,128]{3,2,1,0:T(8,128)(2,1)S(1)} %collective-permute-done.17.refs_0_, f32[4,2,128,128]{3,2,1,0:T(8,128)S(1)} %get-tuple-element.64.refs_1_, ...), custom_call_target="tpu_custom_call" | custom-call | flops 100 | bytes 100 | tf_op jit(solution)/shard_map/finish_last/pallas_call | solution.py:471
  (36 shorter events, 3.1 us)
Async XLA Ops:
  0.0 4.1 %copy-start.2 = (f32[128,32]{0,1:T(8,128)S(1)}, f32[128,32]{0,1:T(8,128)}, u32[]{:S(2)}) copy-start(f32[128,32]{0,1:T(8,128)} %param.10) | copy-start | bytes 49156
  0.0 4.1 %copy-start.3 = (bf16[128,32]{0,1:T(8,128)(2,1)S(1)}, bf16[128,32]{0,1:T(8,128)(2,1)}, u32[]{:S(2)}) copy-start(bf16[128,32]{0,1:T(8,128)(2,1)} %param.9) | copy-start | bytes 24580
  1.7 4.8 %collective-permute-start = (bf16[4,8192]{1,0:T(4,128)(2,1)S(1)}, bf16[4,8192]{1,0:T(4,128)(2,1)S(1)}, u32[]{:S(2)}, u32[]{:S(2)}) collective-permute-start(bf16[4,8192]{1,0:T(4,128)(2,1)S(1)} %get-tuple-element.58), channel_id=1, source_target_pairs={{0,1},{1,2},{2,3},{3,4},{4,5},{5,6},{6,7},{7,8},{8,9},{9,10},{10,1... | collective-permute-start | bytes 196616 | tf_op jit(solution)/shard_map/ppermute | solution.py:488
  4.3 2.1 %copy-start.1 = (bf16[7,128,128]{2,1,0:T(8,128)(2,1)S(1)}, bf16[7,128,128]{2,1,0:T(8,128)(2,1)}, u32[]{:S(2)}) copy-start(bf16[7,128,128]{2,1,0:T(8,128)(2,1)} %constant.53.clone.masks_ref) | copy-start | bytes 688132
  11.2 7.5 %collective-permute-start.9 = (bf16[4,272,256]{2,1,0:T(8,128)(2,1)S(1)}, bf16[4,272,256]{2,1,0:T(8,128)(2,1)S(1)}, u32[]{:S(2)}, u32[]{:S(2)}) collective-permute-start(bf16[4,272,256]{2,1,0:T(8,128)(2,1)S(1)} %get-tuple-element.94), channel_id=1, source_target_pairs={{0,1},{1,0},{2,3},{3,2},{4,5},{5,4},{6,7},{7,6},{8,9},{9,8},{10,11... | collective-permute-start | bytes 1671176 | tf_op jit(solution)/shard_map/ppermute | solution.py:492
  18.7 5.1 %collective-permute-start.1 = (bf16[4,272,256]{2,1,0:T(8,128)(2,1)S(1)}, bf16[4,272,256]{2,1,0:T(8,128)(2,1)S(1)}, u32[]{:S(2)}, u32[]{:S(2)}) collective-permute-start(bf16[4,272,256]{2,1,0:T(8,128)(2,1)S(1)} %get-tuple-element.70), channel_id=1, source_target_pairs={{0,1},{1,0},{2,3},{3,2},{4,5},{5,4},{6,7},{7,6},{8,9},{9,8},{10,11... | collective-permute-start | bytes 1671176 | tf_op jit(solution)/shard_map/ppermute | solution.py:492
  19.7 7.7 %collective-permute-start.10 = (bf16[272,256]{1,0:T(8,128)(2,1)S(1)}, bf16[272,256]{1,0:T(8,128)(2,1)S(1)}, u32[]{:S(2)}, u32[]{:S(2)}) collective-permute-start(bf16[272,256]{1,0:T(8,128)(2,1)S(1)} %get-tuple-element.97), channel_id=1, source_target_pairs={{0,2},{1,3},{2,0},{3,1},{4,6},{5,7},{6,4},{7,5},{8,10},{9,11},{10,... | collective-permute-start | bytes 417800 | tf_op jit(solution)/shard_map/ppermute | solution.py:492
  21.3 9.3 %collective-permute-start.11 = (bf16[272,256]{1,0:T(8,128)(2,1)S(1)}, bf16[272,256]{1,0:T(8,128)(2,1)S(1)}, u32[]{:S(2)}, u32[]{:S(2)}) collective-permute-start(bf16[272,256]{1,0:T(8,128)(2,1)S(1)} %get-tuple-element.98), channel_id=1, source_target_pairs={{0,4},{1,5},{2,6},{3,7},{4,0},{5,1},{6,2},{7,3},{8,12},{9,13},{10,... | collective-permute-start | bytes 417800 | tf_op jit(solution)/shard_map/ppermute | solution.py:492
  22.9 8.4 %collective-permute-start.12 = (bf16[272,256]{1,0:T(8,128)(2,1)S(1)}, bf16[272,256]{1,0:T(8,128)(2,1)S(1)}, u32[]{:S(2)}, u32[]{:S(2)}) collective-permute-start(bf16[272,256]{1,0:T(8,128)(2,1)S(1)} %get-tuple-element.99), channel_id=1, source_target_pairs={{0,6},{1,7},{2,4},{3,5},{4,2},{5,3},{6,0},{7,1},{8,14},{9,15},{10,... | collective-permute-start | bytes 417800 | tf_op jit(solution)/shard_map/ppermute | solution.py:492
  24.7 14.2 %collective-permute-start.2 = (bf16[272,256]{1,0:T(8,128)(2,1)S(1)}, bf16[272,256]{1,0:T(8,128)(2,1)S(1)}, u32[]{:S(2)}, u32[]{:S(2)}) collective-permute-start(bf16[272,256]{1,0:T(8,128)(2,1)S(1)} %get-tuple-element.73), channel_id=1, source_target_pairs={{0,2},{1,3},{2,0},{3,1},{4,6},{5,7},{6,4},{7,5},{8,10},{9,11},{10,... | collective-permute-start | bytes 417800 | tf_op jit(solution)/shard_map/ppermute | solution.py:492
  25.8 13.1 %collective-permute-start.3 = (bf16[272,256]{1,0:T(8,128)(2,1)S(1)}, bf16[272,256]{1,0:T(8,128)(2,1)S(1)}, u32[]{:S(2)}, u32[]{:S(2)}) collective-permute-start(bf16[272,256]{1,0:T(8,128)(2,1)S(1)} %get-tuple-element.74), channel_id=1, source_target_pairs={{0,4},{1,5},{2,6},{3,7},{4,0},{5,1},{6,2},{7,3},{8,12},{9,13},{10,... | collective-permute-start | bytes 417800 | tf_op jit(solution)/shard_map/ppermute | solution.py:492
  27.4 11.5 %collective-permute-start.4 = (bf16[272,256]{1,0:T(8,128)(2,1)S(1)}, bf16[272,256]{1,0:T(8,128)(2,1)S(1)}, u32[]{:S(2)}, u32[]{:S(2)}) collective-permute-start(bf16[272,256]{1,0:T(8,128)(2,1)S(1)} %get-tuple-element.75), channel_id=1, source_target_pairs={{0,6},{1,7},{2,4},{3,5},{4,2},{5,3},{6,0},{7,1},{8,14},{9,15},{10,... | collective-permute-start | bytes 417800 | tf_op jit(solution)/shard_map/ppermute | solution.py:492
  32.5 9.1 %collective-permute-start.13 = (bf16[2,128,128]{2,1,0:T(8,128)(2,1)S(1)}, bf16[2,128,128]{2,1,0:T(8,128)(2,1)S(1)}, u32[]{:S(2)}, u32[]{:S(2)}) collective-permute-start(bf16[2,128,128]{2,1,0:T(8,128)(2,1)S(1)} %get-tuple-element.101), channel_id=1, source_target_pairs={{0,8},{1,9},{2,10},{3,11},{4,12},{5,13},{6,14},{7,15},{16,24},{17,... | collective-permute-start | bytes 196616 | tf_op jit(solution)/shard_map/ppermute | solution.py:488
  36.8 14.1 %copy-start = (bf16[128,4096]{1,0:T(8,128)(2,1)S(1)}, bf16[128,4096]{1,0:T(8,128)(2,1)}, u32[]{:S(2)}) copy-start(bf16[128,4096]{1,0:T(8,128)(2,1)} %gate_ref.1) | copy-start | bytes 3145732
  36.9 14.1 %copy-start.4 = (f32[128]{0:T(128)S(1)}, f32[128]{0:T(128)}, u32[]{:S(2)}) copy-start(f32[128]{0:T(128)} %param.12) | copy-start | bytes 1540
  40.1 6.3 %collective-permute-start.5 = (bf16[2,128,128]{2,1,0:T(8,128)(2,1)S(1)}, bf16[2,128,128]{2,1,0:T(8,128)(2,1)S(1)}, u32[]{:S(2)}, u32[]{:S(2)}) collective-permute-start(bf16[2,128,128]{2,1,0:T(8,128)(2,1)S(1)} %get-tuple-element.77), channel_id=1, source_target_pairs={{0,8},{1,9},{2,10},{3,11},{4,12},{5,13},{6,14},{7,15},{16,24},{17,... | collective-permute-start | bytes 196616 | tf_op jit(solution)/shard_map/ppermute | solution.py:488
  42.6 7.1 %collective-permute-start.14 = (bf16[2,128,128]{2,1,0:T(8,128)(2,1)S(1)}, bf16[2,128,128]{2,1,0:T(8,128)(2,1)S(1)}, u32[]{:S(2)}, u32[]{:S(2)}) collective-permute-start(bf16[2,128,128]{2,1,0:T(8,128)(2,1)S(1)} %get-tuple-element.103), channel_id=1, source_target_pairs={{0,2},{1,3},{2,0},{3,1},{4,6},{5,7},{6,4},{7,5},{8,10},{9,11},{10,... | collective-permute-start | bytes 196616 | tf_op jit(solution)/shard_map/ppermute | solution.py:492
  43.7 7.8 %collective-permute-start.15 = (bf16[2,128,128]{2,1,0:T(8,128)(2,1)S(1)}, bf16[2,128,128]{2,1,0:T(8,128)(2,1)S(1)}, u32[]{:S(2)}, u32[]{:S(2)}) collective-permute-start(bf16[2,128,128]{2,1,0:T(8,128)(2,1)S(1)} %get-tuple-element.104), channel_id=1, source_target_pairs={{0,4},{1,5},{2,6},{3,7},{4,0},{5,1},{6,2},{7,3},{8,12},{9,13},{10,... | collective-permute-start | bytes 196616 | tf_op jit(solution)/shard_map/ppermute | solution.py:492
  45.1 6.4 %collective-permute-start.16 = (bf16[2,128,128]{2,1,0:T(8,128)(2,1)S(1)}, bf16[2,128,128]{2,1,0:T(8,128)(2,1)S(1)}, u32[]{:S(2)}, u32[]{:S(2)}) collective-permute-start(bf16[2,128,128]{2,1,0:T(8,128)(2,1)S(1)} %get-tuple-element.105), channel_id=1, source_target_pairs={{0,6},{1,7},{2,4},{3,5},{4,2},{5,3},{6,0},{7,1},{8,14},{9,15},{10,... | collective-permute-start | bytes 196616 | tf_op jit(solution)/shard_map/ppermute | solution.py:492
  47.4 5.1 %collective-permute-start.6 = (bf16[2,128,128]{2,1,0:T(8,128)(2,1)S(1)}, bf16[2,128,128]{2,1,0:T(8,128)(2,1)S(1)}, u32[]{:S(2)}, u32[]{:S(2)}) collective-permute-start(bf16[2,128,128]{2,1,0:T(8,128)(2,1)S(1)} %get-tuple-element.79), channel_id=1, source_target_pairs={{0,2},{1,3},{2,0},{3,1},{4,6},{5,7},{6,4},{7,5},{8,10},{9,11},{10,... | collective-permute-start | bytes 196616 | tf_op jit(solution)/shard_map/ppermute | solution.py:492
  48.3 4.3 %collective-permute-start.7 = (bf16[2,128,128]{2,1,0:T(8,128)(2,1)S(1)}, bf16[2,128,128]{2,1,0:T(8,128)(2,1)S(1)}, u32[]{:S(2)}, u32[]{:S(2)}) collective-permute-start(bf16[2,128,128]{2,1,0:T(8,128)(2,1)S(1)} %get-tuple-element.80), channel_id=1, source_target_pairs={{0,4},{1,5},{2,6},{3,7},{4,0},{5,1},{6,2},{7,3},{8,12},{9,13},{10,... | collective-permute-start | bytes 196616 | tf_op jit(solution)/shard_map/ppermute | solution.py:492
  49.7 5.2 %collective-permute-start.8 = (bf16[2,128,128]{2,1,0:T(8,128)(2,1)S(1)}, bf16[2,128,128]{2,1,0:T(8,128)(2,1)S(1)}, u32[]{:S(2)}, u32[]{:S(2)}) collective-permute-start(bf16[2,128,128]{2,1,0:T(8,128)(2,1)S(1)} %get-tuple-element.81), channel_id=1, source_target_pairs={{0,6},{1,7},{2,4},{3,5},{4,2},{5,3},{6,0},{7,1},{8,14},{9,15},{10,... | collective-permute-start | bytes 196616 | tf_op jit(solution)/shard_map/ppermute | solution.py:492
  52.4 4.5 %collective-permute-start.18 = (bf16[4,2,128,128]{3,2,1,0:T(8,128)(2,1)S(1)}, bf16[4,2,128,128]{3,2,1,0:T(8,128)(2,1)S(1)}, u32[]{:S(2)}, u32[]{:S(2)}) collective-permute-start(bf16[4,2,128,128]{3,2,1,0:T(8,128)(2,1)S(1)} %get-tuple-element.108), channel_id=1, source_target_pairs={{0,1},{1,0},{2,3},{3,2},{4,5},{5,4},{6,7},{7,6},{8,9},{9,8},{10,11... | collective-permute-start | bytes 786440 | tf_op jit(solution)/shard_map/ppermute | solution.py:492
  55.7 1.6 %collective-permute-start.17 = (bf16[4,2,128,128]{3,2,1,0:T(8,128)(2,1)S(1)}, bf16[4,2,128,128]{3,2,1,0:T(8,128)(2,1)S(1)}, u32[]{:S(2)}, u32[]{:S(2)}) collective-permute-start(bf16[4,2,128,128]{3,2,1,0:T(8,128)(2,1)S(1)} %get-tuple-element.107), channel_id=1, source_target_pairs={{0,1},{1,0},{2,3},{3,2},{4,5},{5,4},{6,7},{7,6},{8,9},{9,8},{10,11... | collective-permute-start | bytes 786440 | tf_op jit(solution)/shard_map/ppermute | solution.py:492

commit v5 on v4

--- a/solution.py
+++ b/solution.py
@@ -381,7 +381,8 @@
 
 
 def spread_kernel(keys, sc_ref, order_ref, in_ref, o0, o1, o2, o3, scr):
-    states = [in_ref[h] for h in range(2 * len(keys))]
+    keep = (1 - sc_ref[3]).astype(BF16)
+    states = [in_ref[h] * keep for h in range(2 * len(keys))]
     for chip in range(CHIPS):
         for h, state in enumerate(states):
             scr[chip, h] = state
@@ -411,71 +412,70 @@
         out_ref[:, head_slice(h)] = gates[:, head_slice(h)] * gain_ref[...]
 
 
-def piece_columns(own, sc_ref, offset):
+def piece_columns(keys, own, sc_ref, offset):
     owner = sc_ref[0] if own else 1 - sc_ref[0]
     piece = owner * (VH // 2 // PIECE) + (sc_ref[1] ^ offset)
-    return pl.ds(pl.multiple_of(piece * PIECE * DH, PIECE * DH), PIECE * DH)
-
-
-def finish_piece(own, offset, sc_ref, gate_ref, bands, out_ref):
-    gates = gate_ref[:, piece_columns(own, sc_ref, offset)]
-    for keys, (state_ref, loc_ref, car_ref) in zip(BANDS, bands):
-        for h in range(2 * len(keys)):
-            core = loc_ref[offset, h] + dot(car_ref[offset, h], state_ref[offset, h])
-            mean_sq = jnp.mean(core * core, axis=1, keepdims=True)
-            cols = head_slice(2 * keys[0] + h)
-            scaled = core * lax.rsqrt(mean_sq + 1e-06) * gates[:, cols]
-            out_ref[offset, :, cols] = scaled.astype(BF16)
-
-
-def finish_kernel(sc_ref, gate_ref, *refs):
-    bands = [refs[3 * b : 3 * b + 3] for b in range(len(BANDS))]
-    for offset in range(CHIPS):
-        finish_piece(1, offset, sc_ref, gate_ref, bands, refs[-1])
-
-
-def finish(place, gates, terms):
+    start = (piece * PIECE + 2 * keys[0]) * DH
+    return pl.ds(pl.multiple_of(start, 2 * DH), 2 * len(keys) * DH)
+
+
+def finish_piece(keys, own, offset, sc_ref, gate_ref, state_ref, loc_ref, car_ref, out_ref):
+    gates = gate_ref[:, piece_columns(keys, own, sc_ref, offset)]
+    for h in range(2 * len(keys)):
+        core = loc_ref[offset, h] + dot(car_ref[offset, h], state_ref[offset, h])
+        mean_sq = jnp.mean(core * core, axis=1, keepdims=True)
+        cols = head_slice(h)
+        scaled = core * lax.rsqrt(mean_sq + 1e-06) * gates[:, cols]
+        out_ref[offset, :, cols] = scaled.astype(BF16)
+
+
+def finish_kernel(parts, sc_ref, gate_ref, *refs):
+    for n, (keys, own) in enumerate(parts):
+        for offset in range(CHIPS):
+            ins = refs[3 * n : 3 * n + 3]
+            finish_piece(keys, own, offset, sc_ref, gate_ref, *ins, refs[3 * len(parts) + n])
+
+
+def finish(parts, place, gates, terms):
     return local_call(
-        finish_kernel,
-        [place, gates, *terms],
-        [jax.ShapeDtypeStruct((CHIPS, CH, PIECE * DH), BF16)],
+        functools.partial(finish_kernel, parts),
+        [place, gates, *sum(terms, [])],
+        [jax.ShapeDtypeStruct((CHIPS, CH, 2 * len(keys) * DH), BF16) for keys, _ in parts],
         vmem_mib=4,
         name="finish",
-    )[0]
-
-
-def last_kernel(sc_ref, gate_ref, done_ref, *refs):
-    bands = [refs[3 * b : 3 * b + 3] for b in range(len(BANDS))]
-    out_ref, scr, sems = refs[-3:]
+    )
+
+
+def last_kernel(earlier, keys, own, sc_ref, gate_ref, state_ref, loc_ref, car_ref, *refs):
+    done_refs, (out_ref, scr, sems) = refs[: len(earlier)], refs[len(earlier) :]
     copies = []
 
-    def send(own, source_ref, offset):
-        cols = piece_columns(own, sc_ref, offset)
-        copies.append(
-            pltpu.make_async_copy(source_ref.at[offset], out_ref.at[:, cols], sems.at[len(copies)])
-        )
+    def send(source, cols):
+        copies.append(pltpu.make_async_copy(source, out_ref.at[:, cols], sems.at[len(copies)]))
         copies[-1].start()
 
+    for part, done_ref in zip(earlier, done_refs):
+        for offset in range(CHIPS):
+            send(done_ref.at[offset], piece_columns(*part, sc_ref, offset))
     for offset in range(CHIPS):
-        send(1, done_ref, offset)
-    for offset in range(CHIPS):
-        finish_piece(0, offset, sc_ref, gate_ref, bands, scr)
-        send(0, scr, offset)
+        finish_piece(keys, own, offset, sc_ref, gate_ref, state_ref, loc_ref, car_ref, scr)
+        send(scr.at[offset], piece_columns(keys, own, sc_ref, offset))
     for copy in copies:
         copy.wait()
 
 
-def finish_last(place, gates, done, terms):
+def finish_last(earlier, part, place, gates, done, terms):
+    keys, own = part
     vmem = pl.BlockSpec(memory_space=pltpu.VMEM)
-    args = [place, gates, done, *terms]
+    args = [place, gates, *terms, *done]
     return pl.pallas_call(
-        last_kernel,
+        functools.partial(last_kernel, earlier, keys, own),
         out_shape=jax.ShapeDtypeStruct(gates.shape, BF16),
         in_specs=[pl.BlockSpec(memory_space=pltpu.SMEM)] + [vmem] * (len(args) - 1),
         out_specs=pl.BlockSpec(memory_space=pl.ANY),
         scratch_shapes=[
-            pltpu.VMEM((CHIPS, CH, PIECE * DH), BF16),
-            pltpu.SemaphoreType.DMA((2 * CHIPS,)),
+            pltpu.VMEM((CHIPS, CH, 2 * len(keys) * DH), BF16),
+            pltpu.SemaphoreType.DMA((CHIPS * (len(earlier) + 1),)),
         ],
         cost_estimate=pl.CostEstimate(flops=100, bytes_accessed=100, transcendentals=0),
         compiler_params=pltpu.CompilerParams(vmem_limit_bytes=4 << 20),
@@ -502,7 +502,7 @@
 def local(mixed_qkv, conv_weight, beta_logit, log_decay, gate_in, norm_gain):
     at = lax.axis_index("seq")
     last = at // (2 * CHIPS) == lax.axis_size("seq") // (2 * CHIPS) - 1
-    place = jnp.stack([at % 2, (at // 2) % CHIPS, last.astype(at.dtype)])
+    place = jnp.stack([at % 2, (at // 2) % CHIPS, last.astype(at.dtype), (at < 2 * CHIPS).astype(at.dtype)])
     x, weight, last_rows = load(mixed_qkv, conv_weight)
     rim = shift(last_rows, 1)
     (rows,) = local_call(
@@ -515,7 +515,8 @@
     conv_out = early_conv(place, x, weight)
     shared = (x, rim, weight, conv_out, rows, jnp.asarray(level_masks()))
     chips = range(CHIPS)
-    finals = [[], []]
+    hop = swap if lax.axis_size("seq") == 4 * CHIPS else shift
+    parts, terms, done = [], [], []
     (gates,) = local_call(
         gates_kernel,
         [gate_in, norm_gain[None]],
@@ -543,7 +544,7 @@
                 [order_shape, state_shape],
                 name="gather",
             )
-            entering = shift(leaving, 2 * CHIPS)
+            entering = hop(leaving, 2 * CHIPS)
         spread = local_call(
             functools.partial(spread_kernel, keys),
             [place, order, entering],
@@ -559,10 +560,11 @@
             [states_shape, states_shape],
             name="enter",
         )
-        for own, state in enumerate((swap(send, 1), keep)):
-            finals[own] += [state, *queries[own]]
-    done = finish(place, gates, finals[1])
-    return finish_last(place, gates, done, finals[0])
+        for own, state in ((1, keep), (0, swap(send, 1))):
+            parts.append((keys, own))
+            terms.append([state, *queries[own]])
+    done = finish(parts[:-1], place, gates, terms[:-1])
+    return finish_last(parts[:-1], parts[-1], place, gates, done, terms[-1])
 
 
 def solution(mesh):

time: 59.5 us -> 57.9 us (0.973)
  starting transfers between devices: 26.2 us -> 24.8 us
    ppermute x3 -> x1, starting transfers between devices: 8.13 us -> 2.36 us  [shift(): lax.ppermute(block, 'seq', [(i, i + distance) for i in range(count - dist...]
    ppermute x16 -> x18, starting transfers between devices: 18 us -> 22.4 us  [swap(): lax.ppermute(block, 'seq', [(i, i ^ distance) for i in range(lax.axis_siz...]
    ppermute x16 -> x18, waiting for transfers between devices: 3.5 us -> 3.3 us  [swap(): lax.ppermute(block, 'seq', [(i, i ^ distance) for i in range(lax.axis_siz...]
  transfers between devices with their start and end apart: 19 -> 19, of which waited for: 4 -> 4; matrix products, arithmetic and copies ran while one was open for 0% -> 0% of each run, Pallas kernels for 35% -> 36%
where the time goes in v5:
time: 57.9 us; the launch traced here: 57.8 us
  Pallas kernels  29.1 us (50%)
  starting transfers between devices  24.8 us (43%)
  waiting for transfers between devices  3.31 us (6%)
    pallas_call x16, Pallas kernels, local_call(): pl.pallas_call(kernel, out_shape=out_shape, in_specs=in_specs, out_specs=...  25.7 us
    ppermute x18, starting transfers between devices, swap(): lax.ppermute(block, 'seq', [(i, i ^ distance) for i in range(lax.axis_siz...  22.4 us
    ppermute x18, waiting for transfers between devices, swap(): lax.ppermute(block, 'seq', [(i, i ^ distance) for i in range(lax.axis_siz...  3.3 us
    ppermute x1, starting transfers between devices, shift(): lax.ppermute(block, 'seq', [(i, i + distance) for i in range(count - dist...  2.36 us
    pallas_call x1, Pallas kernels, finish_last(): pl.pallas_call(functools.partial(last_kernel, earlier, keys, own), out_sh...  1.7 us
    pallas_call x1, Pallas kernels, load(): pl.pallas_call(load_kernel, out_shape=[jax.ShapeDtypeStruct(mixed_qkv.sha...  1.66 us
  transfers between devices with their start and end apart: 19, of which 4 were waited for; matrix products, arithmetic and copies ran while one was open for 0% of the time, Pallas kernels for 36%

profile of v5, /device:TPU:0, one launch (start us, length us, event | category | flops | bytes accessed | tf_op | source)
XLA Modules:
  0.0 57.8 jit_solution(7747868502963041326)
XLA Ops:
  0.0 1.7 %load.1 = (bf16[128,8192]{1,0:T(8,128)(2,1)S(1)}, bf16[4,8192]{1,0:T(4,128)(2,1)S(1)}, bf16[4,8192]{1,0:T(4,128)(2,1)S(1)}) custom-call(bf16[128,8192]{1,0:T(8,128)(2,1)} %x_ref.1, bf16[4,8192]{1,0:T(4,128)(2,1)} %w_ref.1), custom_call_target="tpu_custom_call" | custom-call | flops 100 | bytes 100 | tf_op jit(solution)/shard_map/load/pallas_call | solution.py:91
  1.7 2.4 %collective-permute-start = (bf16[4,8192]{1,0:T(4,128)(2,1)S(1)}, bf16[4,8192]{1,0:T(4,128)(2,1)S(1)}, u32[]{:S(2)}, u32[]{:S(2)}) collective-permute-start(bf16[4,8192]{1,0:T(4,128)(2,1)S(1)} %get-tuple-element.61), channel_id=1, source_target_pairs={{0,1},{1,2},{2,3},{3,4},{4,5},{5,6},{6,7},{7,8},{8,9},{9,10},{10,1... | collective-permute-start | bytes 196616 | tf_op jit(solution)/shard_map/ppermute | solution.py:488
  4.4 2.1 %conv.1.conv_ref = bf16[128,8192]{1,0:T(8,128)(2,1)S(1)} custom-call(s32[4]{0:T(128)S(1)} %pad_add_fusion.sc_ref, bf16[128,8192]{1,0:T(8,128)(2,1)S(1)} %get-tuple-element.60.x_ref, bf16[4,8192]{1,0:T(4,128)(2,1)S(1)} %get-tuple-element.62.w_ref), custom_call_target="tpu_custom_call" | custom-call | flops 100 | bytes 100 | tf_op jit(solution)/shard_map/conv/pallas_call | solution.py:239
  6.5 4.7 %terms.3 = (bf16[4,272,256]{2,1,0:T(8,128)(2,1)S(1)}, bf16[4,2,128,256]{3,2,1,0:T(8,128)(2,1)S(1)}, bf16[4,1,128,128]{3,2,1,0:T(8,128)(2,1)S(1)}, bf16[4,272,256...) custom-call(s32[4]{0:T(128)S(1)} %pad_add_fusion.sc_ref, ...), custom_call_target="tpu_custom_call" | custom-call | flops 100 | bytes 100 | tf_op jit(solution)/shard_map/terms/pallas_call | solution.py:239
  11.2 2.7 %collective-permute-start.10 = (bf16[4,272,256]{2,1,0:T(8,128)(2,1)S(1)}, bf16[4,272,256]{2,1,0:T(8,128)(2,1)S(1)}, u32[]{:S(2)}, u32[]{:S(2)}) collective-permute-start(bf16[4,272,256]{2,1,0:T(8,128)(2,1)S(1)} %get-tuple-element.97), channel_id=1, source_target_pairs={{0,1},{1,0},{2,3},{3,2},{4,5},{5,4},{6,7},{7,6},{8,9},{9,8},{10,11... | collective-permute-start | bytes 1671176 | tf_op jit(solution)/shard_map/ppermute | solution.py:492
  13.9 4.7 %terms.2 = (bf16[4,272,256]{2,1,0:T(8,128)(2,1)S(1)}, bf16[4,2,128,256]{3,2,1,0:T(8,128)(2,1)S(1)}, bf16[4,1,128,128]{3,2,1,0:T(8,128)(2,1)S(1)}, bf16[4,272,256...) custom-call(s32[4]{0:T(128)S(1)} %pad_add_fusion.sc_ref, ...), custom_call_target="tpu_custom_call" | custom-call | flops 100 | bytes 100 | tf_op jit(solution)/shard_map/terms/pallas_call | solution.py:239
  18.7 0.9 %compose.3 = (bf16[4,272,256]{2,1,0:T(8,128)(2,1)S(1)}, bf16[272,256]{1,0:T(8,128)(2,1)S(1)}, bf16[272,256]{1,0:T(8,128)(2,1)S(1)}, bf16[272,256]{1,0:T(8,128)(2,1)S(1)}, bf16[272,256]{1,0:T(8,128)(2,1)S(1)}) custom-call(s32[4]{0:T(128)S(1)} %pad_add_fusion.sc_ref, bf16[4,272,256]{2,1,0:T(8,128)(2,1)S(1)} %get-tuple-element.96.mine_ref, ...), custom_call_target="tpu_custom_call" | custom-call | flops 100 | bytes 100 | tf_op jit(solution)/shard_map/compose/pallas_call | solution.py:239
  19.7 1.6 %collective-permute-start.11 = (bf16[272,256]{1,0:T(8,128)(2,1)S(1)}, bf16[272,256]{1,0:T(8,128)(2,1)S(1)}, u32[]{:S(2)}, u32[]{:S(2)}) collective-permute-start(bf16[272,256]{1,0:T(8,128)(2,1)S(1)} %get-tuple-element.100), channel_id=1, source_target_pairs={{0,2},{1,3},{2,0},{3,1},{4,6},{5,7},{6,4},{7,5},{8,10},{9,11},{10,... | collective-permute-start | bytes 417800 | tf_op jit(solution)/shard_map/ppermute | solution.py:492
  21.3 1.6 %collective-permute-start.12 = (bf16[272,256]{1,0:T(8,128)(2,1)S(1)}, bf16[272,256]{1,0:T(8,128)(2,1)S(1)}, u32[]{:S(2)}, u32[]{:S(2)}) collective-permute-start(bf16[272,256]{1,0:T(8,128)(2,1)S(1)} %get-tuple-element.101), channel_id=1, source_target_pairs={{0,4},{1,5},{2,6},{3,7},{4,0},{5,1},{6,2},{7,3},{8,12},{9,13},{10,... | collective-permute-start | bytes 417800 | tf_op jit(solution)/shard_map/ppermute | solution.py:492
  23.7 0.9 %compose.2 = (bf16[4,272,256]{2,1,0:T(8,128)(2,1)S(1)}, bf16[272,256]{1,0:T(8,128)(2,1)S(1)}, bf16[272,256]{1,0:T(8,128)(2,1)S(1)}, bf16[272,256]{1,0:T(8,128)(2,1)S(1)}, bf16[272,256]{1,0:T(8,128)(2,1)S(1)}) custom-call(s32[4]{0:T(128)S(1)} %pad_add_fusion.sc_ref, bf16[4,272,256]{2,1,0:T(8,128)(2,1)S(1)} %get-tuple-element.73.mine_ref, ...), custom_call_target="tpu_custom_call" | custom-call | flops 100 | bytes 100 | tf_op jit(solution)/shard_map/compose/pallas_call | solution.py:239
  24.7 1.1 %collective-permute-start.2 = (bf16[272,256]{1,0:T(8,128)(2,1)S(1)}, bf16[272,256]{1,0:T(8,128)(2,1)S(1)}, u32[]{:S(2)}, u32[]{:S(2)}) collective-permute-start(bf16[272,256]{1,0:T(8,128)(2,1)S(1)} %get-tuple-element.77), channel_id=1, source_target_pairs={{0,2},{1,3},{2,0},{3,1},{4,6},{5,7},{6,4},{7,5},{8,10},{9,11},{10,... | collective-permute-start | bytes 417800 | tf_op jit(solution)/shard_map/ppermute | solution.py:492
  25.8 1.6 %collective-permute-start.3 = (bf16[272,256]{1,0:T(8,128)(2,1)S(1)}, bf16[272,256]{1,0:T(8,128)(2,1)S(1)}, u32[]{:S(2)}, u32[]{:S(2)}) collective-permute-start(bf16[272,256]{1,0:T(8,128)(2,1)S(1)} %get-tuple-element.78), channel_id=1, source_target_pairs={{0,4},{1,5},{2,6},{3,7},{4,0},{5,1},{6,2},{7,3},{8,12},{9,13},{10,... | collective-permute-start | bytes 417800 | tf_op jit(solution)/shard_map/ppermute | solution.py:492
  27.4 1.0 %collective-permute-start.4 = (bf16[272,256]{1,0:T(8,128)(2,1)S(1)}, bf16[272,256]{1,0:T(8,128)(2,1)S(1)}, u32[]{:S(2)}, u32[]{:S(2)}) collective-permute-start(bf16[272,256]{1,0:T(8,128)(2,1)S(1)} %get-tuple-element.79), channel_id=1, source_target_pairs={{0,6},{1,7},{2,4},{3,5},{4,2},{5,3},{6,0},{7,1},{8,14},{9,15},{10,... | collective-permute-start | bytes 417800 | tf_op jit(solution)/shard_map/ppermute | solution.py:492
  28.4 2.2 %queries.3 = (f32[4,2,128,128]{3,2,1,0:T(8,128)S(1)}, bf16[4,2,128,128]{3,2,1,0:T(8,128)(2,1)S(1)}, f32[4,2,128,128]{3,2,1,0:T(8,128)S(1)}, bf16[4,2,128,128]{3,2,1,0:T(8,128)(2,1)S(1)}) custom-call(s32[4]{0:T(128)S(1)} %pad_add_fusion.sc_ref, bf16[128,8192]{1,0:T(8,128)(2,1)S(1)} %get-tuple-element.60.x_ref, ...), custom_call_target="tpu_custom_call" | custom-call | flops 100 | bytes 100 | tf_op jit(solution)/shard_map/queries/pallas_call | solution.py:239
  31.3 1.2 %gather.3 = (bf16[4,272,256]{2,1,0:T(8,128)(2,1)S(1)}, bf16[2,128,128]{2,1,0:T(8,128)(2,1)S(1)}) custom-call(s32[4]{0:T(128)S(1)} %pad_add_fusion.sc_ref, bf16[272,256]{1,0:T(8,128)(2,1)S(1)} %get-tuple-element.99.p0, bf16[272,256]{1,0:T(8,128)(2,1)S(1)} %collective-permute-done.11.p1, bf16[272,256]{1,0:T(8,128)(2,1)S(1)} %collective-permute-done.12.p2, ...), custom_call_target="tpu_custom_call" | custom-call | flops 100 | bytes 100 | tf_op jit(solution)/shard_map/gather/pallas_call | solution.py:239
  32.5 2.5 %collective-permute-start.14 = (bf16[2,128,128]{2,1,0:T(8,128)(2,1)S(1)}, bf16[2,128,128]{2,1,0:T(8,128)(2,1)S(1)}, u32[]{:S(2)}, u32[]{:S(2)}) collective-permute-start(bf16[2,128,128]{2,1,0:T(8,128)(2,1)S(1)} %get-tuple-element.104), channel_id=1, source_target_pairs={{0,8},{1,9},{2,10},{3,11},{4,12},{5,13},{6,14},{7,15},{8,0},{9,1},... | collective-permute-start | bytes 196616 | tf_op jit(solution)/shard_map/ppermute | solution.py:492
  35.0 2.0 %queries.2 = (f32[4,2,128,128]{3,2,1,0:T(8,128)S(1)}, bf16[4,2,128,128]{3,2,1,0:T(8,128)(2,1)S(1)}, f32[4,2,128,128]{3,2,1,0:T(8,128)S(1)}, bf16[4,2,128,128]{3,2,1,0:T(8,128)(2,1)S(1)}) custom-call(s32[4]{0:T(128)S(1)} %pad_add_fusion.sc_ref, bf16[128,8192]{1,0:T(8,128)(2,1)S(1)} %get-tuple-element.60.x_ref, ...), custom_call_target="tpu_custom_call" | custom-call | flops 100 | bytes 100 | tf_op jit(solution)/shard_map/queries/pallas_call | solution.py:239
  37.1 1.2 %gather.2 = (bf16[4,272,256]{2,1,0:T(8,128)(2,1)S(1)}, bf16[2,128,128]{2,1,0:T(8,128)(2,1)S(1)}) custom-call(s32[4]{0:T(128)S(1)} %pad_add_fusion.sc_ref, bf16[272,256]{1,0:T(8,128)(2,1)S(1)} %get-tuple-element.76.p0, bf16[272,256]{1,0:T(8,128)(2,1)S(1)} %collective-permute-done.2.p1, bf16[272,256]{1,0:T(8,128)(2,1)S(1)} %collective-permute-done.3.p2, ...), custom_call_target="tpu_custom_call" | custom-call | flops 100 | bytes 100 | tf_op jit(solution)/shard_map/gather/pallas_call | solution.py:239
  38.3 2.1 %collective-permute-start.5 = (bf16[2,128,128]{2,1,0:T(8,128)(2,1)S(1)}, bf16[2,128,128]{2,1,0:T(8,128)(2,1)S(1)}, u32[]{:S(2)}, u32[]{:S(2)}) collective-permute-start(bf16[2,128,128]{2,1,0:T(8,128)(2,1)S(1)} %get-tuple-element.81), channel_id=1, source_target_pairs={{0,8},{1,9},{2,10},{3,11},{4,12},{5,13},{6,14},{7,15},{8,0},{9,1},... | collective-permute-start | bytes 196616 | tf_op jit(solution)/shard_map/ppermute | solution.py:492
  40.4 1.0 %spread.3 = (bf16[2,128,128]{2,1,0:T(8,128)(2,1)S(1)}, bf16[2,128,128]{2,1,0:T(8,128)(2,1)S(1)}, bf16[2,128,128]{2,1,0:T(8,128)(2,1)S(1)}, bf16[2,128,128]{2,1,0:T(8,128)(2,1)S(1)}) custom-call(s32[4]{0:T(128)S(1)} %pad_add_fusion.sc_ref, bf16[4,272,256]{2,1,0:T(8,128)(2,1)S(1)} %get-tuple-element.103.order_ref, ...), custom_call_target="tpu_custom_call" | custom-call | flops 100 | bytes 100 | tf_op jit(solution)/shard_map/spread/pallas_call | solution.py:239
  41.4 1.2 %collective-permute-start.15 = (bf16[2,128,128]{2,1,0:T(8,128)(2,1)S(1)}, bf16[2,128,128]{2,1,0:T(8,128)(2,1)S(1)}, u32[]{:S(2)}, u32[]{:S(2)}) collective-permute-start(bf16[2,128,128]{2,1,0:T(8,128)(2,1)S(1)} %get-tuple-element.106), channel_id=1, source_target_pairs={{0,2},{1,3},{2,0},{3,1},{4,6},{5,7},{6,4},{7,5},{8,10},{9,11},{10,... | collective-permute-start | bytes 196616 | tf_op jit(solution)/shard_map/ppermute | solution.py:492
  42.6 1.1 %collective-permute-start.16 = (bf16[2,128,128]{2,1,0:T(8,128)(2,1)S(1)}, bf16[2,128,128]{2,1,0:T(8,128)(2,1)S(1)}, u32[]{:S(2)}, u32[]{:S(2)}) collective-permute-start(bf16[2,128,128]{2,1,0:T(8,128)(2,1)S(1)} %get-tuple-element.107), channel_id=1, source_target_pairs={{0,4},{1,5},{2,6},{3,7},{4,0},{5,1},{6,2},{7,3},{8,12},{9,13},{10,... | collective-permute-start | bytes 196616 | tf_op jit(solution)/shard_map/ppermute | solution.py:492
  43.7 1.3 %collective-permute-start.17 = (bf16[2,128,128]{2,1,0:T(8,128)(2,1)S(1)}, bf16[2,128,128]{2,1,0:T(8,128)(2,1)S(1)}, u32[]{:S(2)}, u32[]{:S(2)}) collective-permute-start(bf16[2,128,128]{2,1,0:T(8,128)(2,1)S(1)} %get-tuple-element.108), channel_id=1, source_target_pairs={{0,6},{1,7},{2,4},{3,5},{4,2},{5,3},{6,0},{7,1},{8,14},{9,15},{10,... | collective-permute-start | bytes 196616 | tf_op jit(solution)/shard_map/ppermute | solution.py:492
  45.0 1.0 %spread.2 = (bf16[2,128,128]{2,1,0:T(8,128)(2,1)S(1)}, bf16[2,128,128]{2,1,0:T(8,128)(2,1)S(1)}, bf16[2,128,128]{2,1,0:T(8,128)(2,1)S(1)}, bf16[2,128,128]{2,1,0:T(8,128)(2,1)S(1)}) custom-call(s32[4]{0:T(128)S(1)} %pad_add_fusion.sc_ref, bf16[4,272,256]{2,1,0:T(8,128)(2,1)S(1)} %get-tuple-element.80.order_ref, ...), custom_call_target="tpu_custom_call" | custom-call | flops 100 | bytes 100 | tf_op jit(solution)/shard_map/spread/pallas_call | solution.py:239
  46.0 1.2 %collective-permute-start.6 = (bf16[2,128,128]{2,1,0:T(8,128)(2,1)S(1)}, bf16[2,128,128]{2,1,0:T(8,128)(2,1)S(1)}, u32[]{:S(2)}, u32[]{:S(2)}) collective-permute-start(bf16[2,128,128]{2,1,0:T(8,128)(2,1)S(1)} %get-tuple-element.83), channel_id=1, source_target_pairs={{0,2},{1,3},{2,0},{3,1},{4,6},{5,7},{6,4},{7,5},{8,10},{9,11},{10,... | collective-permute-start | bytes 196616 | tf_op jit(solution)/shard_map/ppermute | solution.py:492
  47.2 1.1 %collective-permute-start.7 = (bf16[2,128,128]{2,1,0:T(8,128)(2,1)S(1)}, bf16[2,128,128]{2,1,0:T(8,128)(2,1)S(1)}, u32[]{:S(2)}, u32[]{:S(2)}) collective-permute-start(bf16[2,128,128]{2,1,0:T(8,128)(2,1)S(1)} %get-tuple-element.84), channel_id=1, source_target_pairs={{0,4},{1,5},{2,6},{3,7},{4,0},{5,1},{6,2},{7,3},{8,12},{9,13},{10,... | collective-permute-start | bytes 196616 | tf_op jit(solution)/shard_map/ppermute | solution.py:492
  48.3 1.3 %collective-permute-start.8 = (bf16[2,128,128]{2,1,0:T(8,128)(2,1)S(1)}, bf16[2,128,128]{2,1,0:T(8,128)(2,1)S(1)}, u32[]{:S(2)}, u32[]{:S(2)}) collective-permute-start(bf16[2,128,128]{2,1,0:T(8,128)(2,1)S(1)} %get-tuple-element.85), channel_id=1, source_target_pairs={{0,6},{1,7},{2,4},{3,5},{4,2},{5,3},{6,0},{7,1},{8,14},{9,15},{10,... | collective-permute-start | bytes 196616 | tf_op jit(solution)/shard_map/ppermute | solution.py:492
  50.2 0.8 %enter.3 = (bf16[4,2,128,128]{3,2,1,0:T(8,128)(2,1)S(1)}, bf16[4,2,128,128]{3,2,1,0:T(8,128)(2,1)S(1)}) custom-call(s32[4]{0:T(128)S(1)} %pad_add_fusion.sc_ref, bf16[4,272,256]{2,1,0:T(8,128)(2,1)S(1)} %get-tuple-element.98.first_ref, bf16[2,128,128]{2,1,0:T(8,128)(2,1)S(1)} %get-tuple-element.105.refs_0_, ...), custom_call_target="tpu_custom_call" | custom-call | flops 100 | bytes 100 | tf_op jit(solution)/shard_map/enter/pallas_call | solution.py:239
  51.4 2.0 %collective-permute-done.8.refs_3_ = bf16[2,128,128]{2,1,0:T(8,128)(2,1)S(1)} collective-permute-done((bf16[2,128,128]{2,1,0:T(8,128)(2,1)S(1)}, bf16[2,128,128]{2,1,0:T(8,128)(2,1)S(1)}, u32[]{:S(2)}, u32[]{:S(2)}) %collective-permute-start.8) | collective-permute-done | bytes 65568 | tf_op jit(solution)/shard_map/ppermute | solution.py:492
  53.5 0.8 %enter.2 = (bf16[4,2,128,128]{3,2,1,0:T(8,128)(2,1)S(1)}, bf16[4,2,128,128]{3,2,1,0:T(8,128)(2,1)S(1)}) custom-call(s32[4]{0:T(128)S(1)} %pad_add_fusion.sc_ref, bf16[4,272,256]{2,1,0:T(8,128)(2,1)S(1)} %get-tuple-element.75.first_ref, bf16[2,128,128]{2,1,0:T(8,128)(2,1)S(1)} %get-tuple-element.82.refs_0_, ...), custom_call_target="tpu_custom_call" | custom-call | flops 100 | bytes 100 | tf_op jit(solution)/shard_map/enter/pallas_call | solution.py:239
  54.4 1.3 %finish.1 = (bf16[4,128,256]{2,1,0:T(8,128)(2,1)S(1)}, bf16[4,128,256]{2,1,0:T(8,128)(2,1)S(1)}, bf16[4,128,256]{2,1,0:T(8,128)(2,1)S(1)}) custom-call(s32[4]{0:T(128)S(1)} %pad_add_fusion.sc_ref, f32[128,4096]{1,0:T(8,128)S(1)} %gates.1.gate_ref, bf16[4,2,128,128]{3,2,1,0:T(8,128)(2,1)S(1)} %get-tuple-element.109.refs_0_, ...), custom_call_target="tpu_custom_call" | custom-call | flops 100 | bytes 100 | tf_op jit(solution)/shard_map/finish/pallas_call | solution.py:239
  55.9 1.7 %finish_last.1 = bf16[128,4096]{1,0:T(8,128)(2,1)} custom-call(s32[4]{0:T(128)S(1)} %pad_add_fusion.sc_ref, f32[128,4096]{1,0:T(8,128)S(1)} %gates.1.gate_ref, bf16[4,2,128,128]{3,2,1,0:T(8,128)(2,1)S(1)} %collective-permute-done.9.state_ref, f32[4,2,128,128]{3,2,1,0:T(8,128)S(1)} %get-tuple-element.67.loc_ref, ...), custom_call_target="tpu_custom_call" | custom-call | flops 100 | bytes 100 | tf_op jit(solution)/shard_map/finish_last/pallas_call | solution.py:471
  (36 shorter events, 3.2 us)
Async XLA Ops:
  0.0 4.1 %copy-start.2 = (f32[128,32]{0,1:T(8,128)S(1)}, f32[128,32]{0,1:T(8,128)}, u32[]{:S(2)}) copy-start(f32[128,32]{0,1:T(8,128)} %param.10) | copy-start | bytes 49156
  0.0 4.1 %copy-start.3 = (bf16[128,32]{0,1:T(8,128)(2,1)S(1)}, bf16[128,32]{0,1:T(8,128)(2,1)}, u32[]{:S(2)}) copy-start(bf16[128,32]{0,1:T(8,128)(2,1)} %param.9) | copy-start | bytes 24580
  1.7 4.8 %collective-permute-start = (bf16[4,8192]{1,0:T(4,128)(2,1)S(1)}, bf16[4,8192]{1,0:T(4,128)(2,1)S(1)}, u32[]{:S(2)}, u32[]{:S(2)}) collective-permute-start(bf16[4,8192]{1,0:T(4,128)(2,1)S(1)} %get-tuple-element.61), channel_id=1, source_target_pairs={{0,1},{1,2},{2,3},{3,4},{4,5},{5,6},{6,7},{7,8},{8,9},{9,10},{10,1... | collective-permute-start | bytes 196616 | tf_op jit(solution)/shard_map/ppermute | solution.py:488
  4.4 2.1 %copy-start.1 = (bf16[7,128,128]{2,1,0:T(8,128)(2,1)S(1)}, bf16[7,128,128]{2,1,0:T(8,128)(2,1)}, u32[]{:S(2)}) copy-start(bf16[7,128,128]{2,1,0:T(8,128)(2,1)} %constant.54.clone.masks_ref) | copy-start | bytes 688132
  11.2 7.5 %collective-permute-start.10 = (bf16[4,272,256]{2,1,0:T(8,128)(2,1)S(1)}, bf16[4,272,256]{2,1,0:T(8,128)(2,1)S(1)}, u32[]{:S(2)}, u32[]{:S(2)}) collective-permute-start(bf16[4,272,256]{2,1,0:T(8,128)(2,1)S(1)} %get-tuple-element.97), channel_id=1, source_target_pairs={{0,1},{1,0},{2,3},{3,2},{4,5},{5,4},{6,7},{7,6},{8,9},{9,8},{10,11... | collective-permute-start | bytes 1671176 | tf_op jit(solution)/shard_map/ppermute | solution.py:492
  18.7 5.1 %collective-permute-start.1 = (bf16[4,272,256]{2,1,0:T(8,128)(2,1)S(1)}, bf16[4,272,256]{2,1,0:T(8,128)(2,1)S(1)}, u32[]{:S(2)}, u32[]{:S(2)}) collective-permute-start(bf16[4,272,256]{2,1,0:T(8,128)(2,1)S(1)} %get-tuple-element.74), channel_id=1, source_target_pairs={{0,1},{1,0},{2,3},{3,2},{4,5},{5,4},{6,7},{7,6},{8,9},{9,8},{10,11... | collective-permute-start | bytes 1671176 | tf_op jit(solution)/shard_map/ppermute | solution.py:492
  19.7 7.7 %collective-permute-start.11 = (bf16[272,256]{1,0:T(8,128)(2,1)S(1)}, bf16[272,256]{1,0:T(8,128)(2,1)S(1)}, u32[]{:S(2)}, u32[]{:S(2)}) collective-permute-start(bf16[272,256]{1,0:T(8,128)(2,1)S(1)} %get-tuple-element.100), channel_id=1, source_target_pairs={{0,2},{1,3},{2,0},{3,1},{4,6},{5,7},{6,4},{7,5},{8,10},{9,11},{10,... | collective-permute-start | bytes 417800 | tf_op jit(solution)/shard_map/ppermute | solution.py:492
  21.3 9.3 %collective-permute-start.12 = (bf16[272,256]{1,0:T(8,128)(2,1)S(1)}, bf16[272,256]{1,0:T(8,128)(2,1)S(1)}, u32[]{:S(2)}, u32[]{:S(2)}) collective-permute-start(bf16[272,256]{1,0:T(8,128)(2,1)S(1)} %get-tuple-element.101), channel_id=1, source_target_pairs={{0,4},{1,5},{2,6},{3,7},{4,0},{5,1},{6,2},{7,3},{8,12},{9,13},{10,... | collective-permute-start | bytes 417800 | tf_op jit(solution)/shard_map/ppermute | solution.py:492
  22.9 8.4 %collective-permute-start.13 = (bf16[272,256]{1,0:T(8,128)(2,1)S(1)}, bf16[272,256]{1,0:T(8,128)(2,1)S(1)}, u32[]{:S(2)}, u32[]{:S(2)}) collective-permute-start(bf16[272,256]{1,0:T(8,128)(2,1)S(1)} %get-tuple-element.102), channel_id=1, source_target_pairs={{0,6},{1,7},{2,4},{3,5},{4,2},{5,3},{6,0},{7,1},{8,14},{9,15},{10,... | collective-permute-start | bytes 417800 | tf_op jit(solution)/shard_map/ppermute | solution.py:492
  24.7 12.4 %collective-permute-start.2 = (bf16[272,256]{1,0:T(8,128)(2,1)S(1)}, bf16[272,256]{1,0:T(8,128)(2,1)S(1)}, u32[]{:S(2)}, u32[]{:S(2)}) collective-permute-start(bf16[272,256]{1,0:T(8,128)(2,1)S(1)} %get-tuple-element.77), channel_id=1, source_target_pairs={{0,2},{1,3},{2,0},{3,1},{4,6},{5,7},{6,4},{7,5},{8,10},{9,11},{10,... | collective-permute-start | bytes 417800 | tf_op jit(solution)/shard_map/ppermute | solution.py:492
  25.8 11.2 %collective-permute-start.3 = (bf16[272,256]{1,0:T(8,128)(2,1)S(1)}, bf16[272,256]{1,0:T(8,128)(2,1)S(1)}, u32[]{:S(2)}, u32[]{:S(2)}) collective-permute-start(bf16[272,256]{1,0:T(8,128)(2,1)S(1)} %get-tuple-element.78), channel_id=1, source_target_pairs={{0,4},{1,5},{2,6},{3,7},{4,0},{5,1},{6,2},{7,3},{8,12},{9,13},{10,... | collective-permute-start | bytes 417800 | tf_op jit(solution)/shard_map/ppermute | solution.py:492
  27.4 9.7 %collective-permute-start.4 = (bf16[272,256]{1,0:T(8,128)(2,1)S(1)}, bf16[272,256]{1,0:T(8,128)(2,1)S(1)}, u32[]{:S(2)}, u32[]{:S(2)}) collective-permute-start(bf16[272,256]{1,0:T(8,128)(2,1)S(1)} %get-tuple-element.79), channel_id=1, source_target_pairs={{0,6},{1,7},{2,4},{3,5},{4,2},{5,3},{6,0},{7,1},{8,14},{9,15},{10,... | collective-permute-start | bytes 417800 | tf_op jit(solution)/shard_map/ppermute | solution.py:492
  32.5 7.9 %collective-permute-start.14 = (bf16[2,128,128]{2,1,0:T(8,128)(2,1)S(1)}, bf16[2,128,128]{2,1,0:T(8,128)(2,1)S(1)}, u32[]{:S(2)}, u32[]{:S(2)}) collective-permute-start(bf16[2,128,128]{2,1,0:T(8,128)(2,1)S(1)} %get-tuple-element.104), channel_id=1, source_target_pairs={{0,8},{1,9},{2,10},{3,11},{4,12},{5,13},{6,14},{7,15},{8,0},{9,1},... | collective-permute-start | bytes 196616 | tf_op jit(solution)/shard_map/ppermute | solution.py:492
  35.0 14.6 %copy-start = (bf16[128,4096]{1,0:T(8,128)(2,1)S(1)}, bf16[128,4096]{1,0:T(8,128)(2,1)}, u32[]{:S(2)}) copy-start(bf16[128,4096]{1,0:T(8,128)(2,1)} %gate_ref.1) | copy-start | bytes 3145732
  35.0 14.6 %copy-start.4 = (f32[128]{0:T(128)S(1)}, f32[128]{0:T(128)}, u32[]{:S(2)}) copy-start(f32[128]{0:T(128)} %param.12) | copy-start | bytes 1540
  38.3 6.7 %collective-permute-start.5 = (bf16[2,128,128]{2,1,0:T(8,128)(2,1)S(1)}, bf16[2,128,128]{2,1,0:T(8,128)(2,1)S(1)}, u32[]{:S(2)}, u32[]{:S(2)}) collective-permute-start(bf16[2,128,128]{2,1,0:T(8,128)(2,1)S(1)} %get-tuple-element.81), channel_id=1, source_target_pairs={{0,8},{1,9},{2,10},{3,11},{4,12},{5,13},{6,14},{7,15},{8,0},{9,1},... | collective-permute-start | bytes 196616 | tf_op jit(solution)/shard_map/ppermute | solution.py:492
  41.4 6.9 %collective-permute-start.15 = (bf16[2,128,128]{2,1,0:T(8,128)(2,1)S(1)}, bf16[2,128,128]{2,1,0:T(8,128)(2,1)S(1)}, u32[]{:S(2)}, u32[]{:S(2)}) collective-permute-start(bf16[2,128,128]{2,1,0:T(8,128)(2,1)S(1)} %get-tuple-element.106), channel_id=1, source_target_pairs={{0,2},{1,3},{2,0},{3,1},{4,6},{5,7},{6,4},{7,5},{8,10},{9,11},{10,... | collective-permute-start | bytes 196616 | tf_op jit(solution)/shard_map/ppermute | solution.py:492
  42.6 7.6 %collective-permute-start.16 = (bf16[2,128,128]{2,1,0:T(8,128)(2,1)S(1)}, bf16[2,128,128]{2,1,0:T(8,128)(2,1)S(1)}, u32[]{:S(2)}, u32[]{:S(2)}) collective-permute-start(bf16[2,128,128]{2,1,0:T(8,128)(2,1)S(1)} %get-tuple-element.107), channel_id=1, source_target_pairs={{0,4},{1,5},{2,6},{3,7},{4,0},{5,1},{6,2},{7,3},{8,12},{9,13},{10,... | collective-permute-start | bytes 196616 | tf_op jit(solution)/shard_map/ppermute | solution.py:492
  43.7 6.5 %collective-permute-start.17 = (bf16[2,128,128]{2,1,0:T(8,128)(2,1)S(1)}, bf16[2,128,128]{2,1,0:T(8,128)(2,1)S(1)}, u32[]{:S(2)}, u32[]{:S(2)}) collective-permute-start(bf16[2,128,128]{2,1,0:T(8,128)(2,1)S(1)} %get-tuple-element.108), channel_id=1, source_target_pairs={{0,6},{1,7},{2,4},{3,5},{4,2},{5,3},{6,0},{7,1},{8,14},{9,15},{10,... | collective-permute-start | bytes 196616 | tf_op jit(solution)/shard_map/ppermute | solution.py:492
  46.0 5.1 %collective-permute-start.6 = (bf16[2,128,128]{2,1,0:T(8,128)(2,1)S(1)}, bf16[2,128,128]{2,1,0:T(8,128)(2,1)S(1)}, u32[]{:S(2)}, u32[]{:S(2)}) collective-permute-start(bf16[2,128,128]{2,1,0:T(8,128)(2,1)S(1)} %get-tuple-element.83), channel_id=1, source_target_pairs={{0,2},{1,3},{2,0},{3,1},{4,6},{5,7},{6,4},{7,5},{8,10},{9,11},{10,... | collective-permute-start | bytes 196616 | tf_op jit(solution)/shard_map/ppermute | solution.py:492
  47.2 4.3 %collective-permute-start.7 = (bf16[2,128,128]{2,1,0:T(8,128)(2,1)S(1)}, bf16[2,128,128]{2,1,0:T(8,128)(2,1)S(1)}, u32[]{:S(2)}, u32[]{:S(2)}) collective-permute-start(bf16[2,128,128]{2,1,0:T(8,128)(2,1)S(1)} %get-tuple-element.84), channel_id=1, source_target_pairs={{0,4},{1,5},{2,6},{3,7},{4,0},{5,1},{6,2},{7,3},{8,12},{9,13},{10,... | collective-permute-start | bytes 196616 | tf_op jit(solution)/shard_map/ppermute | solution.py:492
  48.3 5.2 %collective-permute-start.8 = (bf16[2,128,128]{2,1,0:T(8,128)(2,1)S(1)}, bf16[2,128,128]{2,1,0:T(8,128)(2,1)S(1)}, u32[]{:S(2)}, u32[]{:S(2)}) collective-permute-start(bf16[2,128,128]{2,1,0:T(8,128)(2,1)S(1)} %get-tuple-element.85), channel_id=1, source_target_pairs={{0,6},{1,7},{2,4},{3,5},{4,2},{5,3},{6,0},{7,1},{8,14},{9,15},{10,... | collective-permute-start | bytes 196616 | tf_op jit(solution)/shard_map/ppermute | solution.py:492
  51.0 3.4 %collective-permute-start.18 = (bf16[4,2,128,128]{3,2,1,0:T(8,128)(2,1)S(1)}, bf16[4,2,128,128]{3,2,1,0:T(8,128)(2,1)S(1)}, u32[]{:S(2)}, u32[]{:S(2)}) collective-permute-start(bf16[4,2,128,128]{3,2,1,0:T(8,128)(2,1)S(1)} %get-tuple-element.110), channel_id=1, source_target_pairs={{0,1},{1,0},{2,3},{3,2},{4,5},{5,4},{6,7},{7,6},{8,9},{9,8},{10,11... | collective-permute-start | bytes 786440 | tf_op jit(solution)/shard_map/ppermute | solution.py:492
  54.3 1.6 %collective-permute-start.9 = (bf16[4,2,128,128]{3,2,1,0:T(8,128)(2,1)S(1)}, bf16[4,2,128,128]{3,2,1,0:T(8,128)(2,1)S(1)}, u32[]{:S(2)}, u32[]{:S(2)}) collective-permute-start(bf16[4,2,128,128]{3,2,1,0:T(8,128)(2,1)S(1)} %get-tuple-element.86), channel_id=1, source_target_pairs={{0,1},{1,0},{2,3},{3,2},{4,5},{5,4},{6,7},{7,6},{8,9},{9,8},{10,11... | collective-permute-start | bytes 786440 | tf_op jit(solution)/shard_map/ppermute | solution.py:492

commit v6 on v5

--- a/solution.py
+++ b/solution.py
@@ -32,17 +32,18 @@
 
 
 def decay_rows(decays):
-    high, low = halves(decays)
-    return jnp.concatenate([high, low], axis=0)
+    decays = decays[:PIECE]
+    high = decays.astype(BF16).astype(F32)
+    return jnp.concatenate([high, decays - high], axis=0).astype(BF16)
 
 
 def rows_of(keys):
-    return 2 * len(keys) * DH + 16
+    return 2 * len(keys) * DH + 2 * PIECE
 
 
 def decays_of(rows):
     rows = rows.astype(F32)
-    return rows[:8] + rows[8:]
+    return rows[:PIECE] + rows[PIECE:]
 
 
 def head_slice(h):
@@ -104,7 +105,8 @@
     )(*(pltpu.with_memory_space_constraint(a, pltpu.HBM) for a in (mixed_qkv, conv_weight)))
 
 
-def conv_kernel(sc_ref, x_ref, w_ref, out_ref, scr):
+def conv_kernel(sc_ref, x_ref, w_ref, decay_ref, logit_ref, out_ref, rows_ref, scr):
+    rows_kernel(decay_ref, logit_ref, rows_ref)
     owner = 1 - sc_ref[0]
     width = scr.shape[2]
     keys, values = KH // 2 * DH // width, VH // 2 * DH // width
@@ -117,16 +119,18 @@
         out_ref[8:, cols] = taps(lambda tap: scr[i % 2, 5 + tap : 5 + tap + CH - 8, :], w, CH - 8)
 
 
-def early_conv(place, x, conv_weight):
+def early_conv(place, x, conv_weight, log_decay, beta_logit):
     return local_call(
         conv_kernel,
-        [place, x, conv_weight],
-        [jax.ShapeDtypeStruct(x.shape, BF16)],
+        [place, x, conv_weight, log_decay.T, beta_logit.T],
+        [
+            jax.ShapeDtypeStruct(x.shape, BF16),
+            jax.ShapeDtypeStruct((VH // PIECE, 2 * PIECE, CH), F32),
+        ],
         [pltpu.VMEM((2, CH, 512), F32)],
-        flops=10_000_000,
         vmem_mib=4,
         name="conv",
-    )[0]
+    )
 
 
 def convolved(x_ref, rim_ref, w_ref, scr, slot, column, width, conv_ref=None):
@@ -267,27 +271,31 @@
 
 def compose_kernel(keys, sc_ref, mine_ref, other_ref, first_ref, *sent_refs):
     count = 2 * len(keys)
-    is_first = sc_ref[0] == 0
-    for offset in range(CHIPS):
-        mine_g, theirs_g = decays_at(mine_ref, offset), decays_at(other_ref, offset)
-        first_g = jnp.where(is_first, mine_g, theirs_g)
-        second_g = jnp.where(is_first, theirs_g, mine_g)
-        first_ref[offset, count * DH :, :] = decay_rows(first_g)
-        sent_refs[offset][count * DH :, :] = decay_rows(first_g * second_g)
-        for h in range(count):
-            mine, theirs = mine_ref[offset, head_slice(h)], other_ref[offset, head_slice(h)]
-            first = jnp.where(is_first, mine, theirs)
-            second = jnp.where(is_first, theirs, mine)
-            first_ref[offset, head_slice(h), :] = first
-            product = dot(second[:, :DH], first)
-            at = 2 * keys[0] + h
-            kept = jnp.concatenate(
-                [second[:, :DH].astype(F32) * first_g[at : at + 1, :DH], second[:, DH:].astype(F32)],
-                axis=1,
-            )
-            sent_refs[offset][head_slice(h), :] = (
-                first.astype(F32) * second_g[at : at + 1] - product + kept
-            ).astype(BF16)
+
+    def join(first_in, second_in):
+        for offset in range(CHIPS):
+            first_g, second_g = decays_at(first_in, offset), decays_at(second_in, offset)
+            first_ref[offset] = first_in[offset]
+            sent_refs[offset][count * DH :, :] = decay_rows(first_g * second_g)
+            for h in range(count):
+                first, second = first_in[offset, head_slice(h)], second_in[offset, head_slice(h)]
+                product = dot(second[:, :DH], first)
+                at = 2 * keys[0] + h
+                decay = first_g[at : at + 1, :DH]
+                kept = jnp.concatenate(
+                    [second[:, :DH].astype(F32) * decay, second[:, DH:].astype(F32)], axis=1
+                )
+                sent_refs[offset][head_slice(h), :] = (
+                    first.astype(F32) * second_g[at : at + 1] - product + kept
+                ).astype(BF16)
+
+    @pl.when(sc_ref[0] == 0)
+    def _():
+        join(mine_ref, other_ref)
+
+    @pl.when(sc_ref[0] == 1)
+    def _():
+        join(other_ref, mine_ref)
 
 
 def compose(keys, place, mine, other):
@@ -302,17 +310,21 @@
     return first, sent
 
 
-def queries_kernel(keys, sc_ref, x_ref, rim_ref, w_ref, rows_ref, *refs):
-    ins, outs, scr = (refs[0:2], refs[2:4]), (refs[4:6], refs[6:8]), refs[8]
+def queries_kernel(sc_ref, x_ref, rim_ref, w_ref, rows_ref, *refs):
+    count = len(BANDS)
+    ins, outs, scr = refs[: 4 * count], refs[4 * count : 8 * count], refs[-1]
     t_at, s_at = token_order()
     heads = []
-    for own, ((solved_ref, key_ref), out) in enumerate(zip(ins, outs)):
+    for n in range(2 * count):
+        keys, own = BANDS[n // 2], n % 2
+        solved_ref, key_ref = ins[2 * n : 2 * n + 2]
+        out = outs[2 * n : 2 * n + 2]
         owner = sc_ref[0] if own else 1 - sc_ref[0]
         for offset in range(CHIPS):
             piece = owner * (VH // 2 // PIECE) + (sc_ref[1] ^ offset)
             kd = len(keys) * DH
             key_at = piece * PIECE // 2 + keys[0]
-            cq = convolved(x_ref, rim_ref, w_ref, scr, own * CHIPS + offset, key_at * DH, kd)
+            cq = convolved(x_ref, rim_ref, w_ref, scr, n * CHIPS + offset, key_at * DH, kd)
             rows = rows_ref[piece]
             cols = rows.T
             grow_cols = jnp.exp(cols)
@@ -334,25 +346,25 @@
         car_ref[offset, h] = (query - both[:, :DH]).astype(BF16)
 
 
-def block_queries(keys, place, shared, theirs, mine):
-    count = 2 * len(keys)
+def block_queries(place, shared, solved):
+    outs = []
+    for keys in BANDS:
+        rows = (CHIPS, 2 * len(keys), CH, DH)
+        outs += [jax.ShapeDtypeStruct(rows, F32), jax.ShapeDtypeStruct(rows, BF16)] * 2
+    width = max(len(keys) for keys in BANDS) * DH
     out = local_call(
-        functools.partial(queries_kernel, keys),
-        [place, *shared[:3], shared[4], *theirs, *mine],
-        [
-            jax.ShapeDtypeStruct((CHIPS, count, CH, DH), F32),
-            jax.ShapeDtypeStruct((CHIPS, count, CH, DH), BF16),
-        ]
-        * 2,
-        [pltpu.VMEM((2 * CHIPS, CH + 8, len(keys) * DH), F32)],
-        vmem_mib=24,
+        queries_kernel,
+        [place, *shared[:3], shared[4], *solved],
+        outs,
+        [pltpu.VMEM((2 * len(BANDS) * CHIPS, CH + 8, width), F32)],
+        vmem_mib=28,
         name="queries",
     )
-    return out[:2], out[2:]
+    return [(out[4 * b : 4 * b + 2], out[4 * b + 2 : 4 * b + 4]) for b in range(len(BANDS))]
 
 
 def decays_at(ref, slot):
-    return decays_of(ref[slot, ref.shape[1] - 16 :])
+    return decays_of(ref[slot, ref.shape[1] - 2 * PIECE :])
 
 
 def advance(keys, ref, slot, h, decays, state):
@@ -505,14 +517,7 @@
     place = jnp.stack([at % 2, (at // 2) % CHIPS, last.astype(at.dtype), (at < 2 * CHIPS).astype(at.dtype)])
     x, weight, last_rows = load(mixed_qkv, conv_weight)
     rim = shift(last_rows, 1)
-    (rows,) = local_call(
-        rows_kernel,
-        [log_decay.T, beta_logit.T],
-        [jax.ShapeDtypeStruct((VH // PIECE, 2 * PIECE, CH), F32)],
-        scalars=0,
-        name="rows",
-    )
-    conv_out = early_conv(place, x, weight)
+    conv_out, rows = early_conv(place, x, weight, log_decay, beta_logit)
     shared = (x, rim, weight, conv_out, rows, jnp.asarray(level_masks()))
     chips = range(CHIPS)
     hop = swap if lax.axis_size("seq") == 4 * CHIPS else shift
@@ -525,14 +530,18 @@
         vmem_mib=4,
         name="gates",
     )
+    firsts, traveled, solved = [], [], []
     for keys in BANDS:
         theirs, mine = block_terms(keys, place, shared)
         other = swap(theirs[0], 1)
         first, sent = compose(keys, place, mine[0], other)
-        pieces = [swap(sent[n], 2 * n) if n else sent[0] for n in range(CHIPS)]
-        queries = block_queries(keys, place, shared, theirs[1:], mine[1:])
-        turn, _ = lax.optimization_barrier((place, queries))
-
+        firsts.append(first)
+        traveled.append([swap(sent[n], 2 * n) if n else sent[0] for n in range(CHIPS)])
+        solved += [*theirs[1:], *mine[1:]]
+    all_queries = block_queries(place, shared, solved)
+    turn, _ = lax.optimization_barrier((place, all_queries))
+
+    for keys, first, pieces, queries in zip(BANDS, firsts, traveled, all_queries):
         count = 2 * len(keys)
         state_shape = jax.ShapeDtypeStruct((count, DH, DH), BF16)
         order_shape = jax.ShapeDtypeStruct((CHIPS, rows_of(keys), WIDE), BF16)

time: 57.9 us -> 57.1 us (0.986)
  waiting for transfers between devices: 3.31 us -> 2.38 us
  starting transfers between devices: 24.8 us -> 25.6 us
  Pallas kernels: 29.1 us -> 28.4 us
    ppermute x18, waiting for transfers between devices: 3.3 us -> 2.38 us  [swap(): lax.ppermute(block, 'seq', [(i, i ^ distance) for i in range(lax.axis_siz...]
    ppermute x18, starting transfers between devices: 22.4 us -> 23.2 us  [swap(): lax.ppermute(block, 'seq', [(i, i ^ distance) for i in range(lax.axis_siz...]
    pallas_call x16 -> x14, Pallas kernels: 25.7 us -> 25 us  [local_call(): pl.pallas_call(kernel, out_shape=out_shape, in_specs=in_specs, out_specs=...]
where the time goes in v6:
time: 57.1 us; the launch traced here: 56.9 us
  Pallas kernels  28.4 us (50%)
  starting transfers between devices  25.6 us (45%)
  waiting for transfers between devices  2.38 us (4%)
    pallas_call x14, Pallas kernels, local_call(): pl.pallas_call(kernel, out_shape=out_shape, in_specs=in_specs, out_specs=...  25 us
    ppermute x18, starting transfers between devices, swap(): lax.ppermute(block, 'seq', [(i, i ^ distance) for i in range(lax.axis_siz...  23.2 us
    ppermute x18, waiting for transfers between devices, swap(): lax.ppermute(block, 'seq', [(i, i ^ distance) for i in range(lax.axis_siz...  2.38 us
    ppermute x1, starting transfers between devices, shift(): lax.ppermute(block, 'seq', [(i, i + distance) for i in range(count - dist...  2.37 us
    pallas_call x1, Pallas kernels, finish_last(): pl.pallas_call(functools.partial(last_kernel, earlier, keys, own), out_sh...  1.7 us
    pallas_call x1, Pallas kernels, load(): pl.pallas_call(load_kernel, out_shape=[jax.ShapeDtypeStruct(mixed_qkv.sha...  1.68 us
  transfers between devices with their start and end apart: 19, of which 4 were waited for; matrix products, arithmetic and copies ran while one was open for 0% of the time, Pallas kernels for 36%

profile of v6, /device:TPU:0, one launch (start us, length us, event | category | flops | bytes accessed | tf_op | source)
XLA Modules:
  0.0 56.9 jit_solution(712629587991032662)
XLA Ops:
  0.0 1.7 %load.1 = (bf16[128,8192]{1,0:T(8,128)(2,1)S(1)}, bf16[4,8192]{1,0:T(4,128)(2,1)S(1)}, bf16[4,8192]{1,0:T(4,128)(2,1)S(1)}) custom-call(bf16[128,8192]{1,0:T(8,128)(2,1)} %x_ref.1, bf16[4,8192]{1,0:T(4,128)(2,1)} %w_ref.1), custom_call_target="tpu_custom_call" | custom-call | flops 100 | bytes 100 | tf_op jit(solution)/shard_map/load/pallas_call | solution.py:92
  1.7 2.4 %collective-permute-start = (bf16[4,8192]{1,0:T(4,128)(2,1)S(1)}, bf16[4,8192]{1,0:T(4,128)(2,1)S(1)}, u32[]{:S(2)}, u32[]{:S(2)}) collective-permute-start(bf16[4,8192]{1,0:T(4,128)(2,1)S(1)} %get-tuple-element.62), channel_id=1, source_target_pairs={{0,1},{1,2},{2,3},{3,4},{4,5},{5,6},{6,7},{7,8},{8,9},{9,10},{10,1... | collective-permute-start | bytes 196616 | tf_op jit(solution)/shard_map/ppermute | solution.py:500
  4.2 2.2 %conv.1 = (bf16[128,8192]{1,0:T(8,128)(2,1)S(1)}, f32[8,8,128]{2,1,0:T(8,128)S(1)}) custom-call(s32[4]{0:T(128)S(1)} %pad_add_fusion.sc_ref, bf16[128,8192]{1,0:T(8,128)(2,1)S(1)} %get-tuple-element.61.x_ref, bf16[4,8192]{1,0:T(4,128)(2,1)S(1)} %get-tuple-element.63.w_ref, f32[32,128]{1,0:T(8,128)S(1)} %bitcast.7, bf16[32,128]{1,0:T(8,128)(2,1)S(1)} %bitcast.8), custom_call_target="tpu_custom_call" | custom-call | flops 100 | bytes 100 | tf_op jit(solution)/shard_map/conv/pallas_call | solution.py:243
  6.4 4.7 %terms.2 = (bf16[4,264,256]{2,1,0:T(8,128)(2,1)S(1)}, bf16[4,2,128,256]{3,2,1,0:T(8,128)(2,1)S(1)}, bf16[4,1,128,128]{3,2,1,0:T(8,128)(2,1)S(1)}, bf16[4,264,256...) custom-call(s32[4]{0:T(128)S(1)} %pad_add_fusion.sc_ref, ...), custom_call_target="tpu_custom_call" | custom-call | flops 100 | bytes 100 | tf_op jit(solution)/shard_map/terms/pallas_call | solution.py:243
  11.1 2.7 %collective-permute-start.10 = (bf16[4,264,256]{2,1,0:T(8,128)(2,1)S(1)}, bf16[4,264,256]{2,1,0:T(8,128)(2,1)S(1)}, u32[]{:S(2)}, u32[]{:S(2)}) collective-permute-start(bf16[4,264,256]{2,1,0:T(8,128)(2,1)S(1)} %get-tuple-element.99), channel_id=1, source_target_pairs={{0,1},{1,0},{2,3},{3,2},{4,5},{5,4},{6,7},{7,6},{8,9},{9,8},{10,11... | collective-permute-start | bytes 1622024 | tf_op jit(solution)/shard_map/ppermute | solution.py:504
  13.8 4.7 %terms.3 = (bf16[4,264,256]{2,1,0:T(8,128)(2,1)S(1)}, bf16[4,2,128,256]{3,2,1,0:T(8,128)(2,1)S(1)}, bf16[4,1,128,128]{3,2,1,0:T(8,128)(2,1)S(1)}, bf16[4,264,256...) custom-call(s32[4]{0:T(128)S(1)} %pad_add_fusion.sc_ref, ...), custom_call_target="tpu_custom_call" | custom-call | flops 100 | bytes 100 | tf_op jit(solution)/shard_map/terms/pallas_call | solution.py:243
  18.6 0.9 %compose.3 = (bf16[4,264,256]{2,1,0:T(8,128)(2,1)S(1)}, bf16[264,256]{1,0:T(8,128)(2,1)S(1)}, bf16[264,256]{1,0:T(8,128)(2,1)S(1)}, bf16[264,256]{1,0:T(8,128)(2,1)S(1)}, bf16[264,256]{1,0:T(8,128)(2,1)S(1)}) custom-call(s32[4]{0:T(128)S(1)} %pad_add_fusion.sc_ref, bf16[4,264,256]{2,1,0:T(8,128)(2,1)S(1)} %get-tuple-element.98.mine_ref, ...), custom_call_target="tpu_custom_call" | custom-call | flops 100 | bytes 100 | tf_op jit(solution)/shard_map/compose/pallas_call | solution.py:243
  19.5 1.8 %collective-permute-start.11 = (bf16[264,256]{1,0:T(8,128)(2,1)S(1)}, bf16[264,256]{1,0:T(8,128)(2,1)S(1)}, u32[]{:S(2)}, u32[]{:S(2)}) collective-permute-start(bf16[264,256]{1,0:T(8,128)(2,1)S(1)} %get-tuple-element.102), channel_id=1, source_target_pairs={{0,2},{1,3},{2,0},{3,1},{4,6},{5,7},{6,4},{7,5},{8,10},{9,11},{10,... | collective-permute-start | bytes 405512 | tf_op jit(solution)/shard_map/ppermute | solution.py:504
  21.3 1.6 %collective-permute-start.12 = (bf16[264,256]{1,0:T(8,128)(2,1)S(1)}, bf16[264,256]{1,0:T(8,128)(2,1)S(1)}, u32[]{:S(2)}, u32[]{:S(2)}) collective-permute-start(bf16[264,256]{1,0:T(8,128)(2,1)S(1)} %get-tuple-element.103), channel_id=1, source_target_pairs={{0,4},{1,5},{2,6},{3,7},{4,0},{5,1},{6,2},{7,3},{8,12},{9,13},{10,... | collective-permute-start | bytes 405512 | tf_op jit(solution)/shard_map/ppermute | solution.py:504
  22.9 0.8 %collective-permute-start.13 = (bf16[264,256]{1,0:T(8,128)(2,1)S(1)}, bf16[264,256]{1,0:T(8,128)(2,1)S(1)}, u32[]{:S(2)}, u32[]{:S(2)}) collective-permute-start(bf16[264,256]{1,0:T(8,128)(2,1)S(1)} %get-tuple-element.104), channel_id=1, source_target_pairs={{0,6},{1,7},{2,4},{3,5},{4,2},{5,3},{6,0},{7,1},{8,14},{9,15},{10,... | collective-permute-start | bytes 405512 | tf_op jit(solution)/shard_map/ppermute | solution.py:504
  23.7 1.1 %compose.2 = (bf16[4,264,256]{2,1,0:T(8,128)(2,1)S(1)}, bf16[264,256]{1,0:T(8,128)(2,1)S(1)}, bf16[264,256]{1,0:T(8,128)(2,1)S(1)}, bf16[264,256]{1,0:T(8,128)(2,1)S(1)}, bf16[264,256]{1,0:T(8,128)(2,1)S(1)}) custom-call(s32[4]{0:T(128)S(1)} %pad_add_fusion.sc_ref, bf16[4,264,256]{2,1,0:T(8,128)(2,1)S(1)} %get-tuple-element.84.mine_ref, ...), custom_call_target="tpu_custom_call" | custom-call | flops 100 | bytes 100 | tf_op jit(solution)/shard_map/compose/pallas_call | solution.py:243
  24.8 1.1 %collective-permute-start.2 = (bf16[264,256]{1,0:T(8,128)(2,1)S(1)}, bf16[264,256]{1,0:T(8,128)(2,1)S(1)}, u32[]{:S(2)}, u32[]{:S(2)}) collective-permute-start(bf16[264,256]{1,0:T(8,128)(2,1)S(1)} %get-tuple-element.88), channel_id=1, source_target_pairs={{0,2},{1,3},{2,0},{3,1},{4,6},{5,7},{6,4},{7,5},{8,10},{9,11},{10,... | collective-permute-start | bytes 405512 | tf_op jit(solution)/shard_map/ppermute | solution.py:504
  25.9 1.6 %collective-permute-start.3 = (bf16[264,256]{1,0:T(8,128)(2,1)S(1)}, bf16[264,256]{1,0:T(8,128)(2,1)S(1)}, u32[]{:S(2)}, u32[]{:S(2)}) collective-permute-start(bf16[264,256]{1,0:T(8,128)(2,1)S(1)} %get-tuple-element.89), channel_id=1, source_target_pairs={{0,4},{1,5},{2,6},{3,7},{4,0},{5,1},{6,2},{7,3},{8,12},{9,13},{10,... | collective-permute-start | bytes 405512 | tf_op jit(solution)/shard_map/ppermute | solution.py:504
  27.5 0.8 %collective-permute-start.4 = (bf16[264,256]{1,0:T(8,128)(2,1)S(1)}, bf16[264,256]{1,0:T(8,128)(2,1)S(1)}, u32[]{:S(2)}, u32[]{:S(2)}) collective-permute-start(bf16[264,256]{1,0:T(8,128)(2,1)S(1)} %get-tuple-element.90), channel_id=1, source_target_pairs={{0,6},{1,7},{2,4},{3,5},{4,2},{5,3},{6,0},{7,1},{8,14},{9,15},{10,... | collective-permute-start | bytes 405512 | tf_op jit(solution)/shard_map/ppermute | solution.py:504
  28.4 3.6 %queries.1 = (f32[4,2,128,128]{3,2,1,0:T(8,128)S(1)}, bf16[4,2,128,128]{3,2,1,0:T(8,128)(2,1)S(1)}, f32[4,2,128,128]{3,2,1,0:T(8,128)S(1)}, bf16[4,2,128,128]{3,...) custom-call(s32[4]{0:T(128)S(1)} %pad_add_fusion.sc_ref, ...), custom_call_target="tpu_custom_call" | custom-call | flops 100 | bytes 100 | tf_op jit(solution)/shard_map/queries/pallas_call | solution.py:243
  32.0 1.2 %gather.3 = (bf16[4,264,256]{2,1,0:T(8,128)(2,1)S(1)}, bf16[2,128,128]{2,1,0:T(8,128)(2,1)S(1)}) custom-call(s32[4]{0:T(128)S(1)} %pad_add_fusion.sc_ref, bf16[264,256]{1,0:T(8,128)(2,1)S(1)} %get-tuple-element.101.p0, bf16[264,256]{1,0:T(8,128)(2,1)S(1)} %collective-permute-done.11.p1, bf16[264,256]{1,0:T(8,128)(2,1)S(1)} %collective-permute-done.12.p2, ...), custom_call_target="tpu_custom_call" | custom-call | flops 100 | bytes 100 | tf_op jit(solution)/shard_map/gather/pallas_call | solution.py:243
  33.2 2.5 %collective-permute-start.14 = (bf16[2,128,128]{2,1,0:T(8,128)(2,1)S(1)}, bf16[2,128,128]{2,1,0:T(8,128)(2,1)S(1)}, u32[]{:S(2)}, u32[]{:S(2)}) collective-permute-start(bf16[2,128,128]{2,1,0:T(8,128)(2,1)S(1)} %get-tuple-element.106), channel_id=1, source_target_pairs={{0,8},{1,9},{2,10},{3,11},{4,12},{5,13},{6,14},{7,15},{8,0},{9,1},... | collective-permute-start | bytes 196616 | tf_op jit(solution)/shard_map/ppermute | solution.py:504
  35.9 1.2 %gather.2 = (bf16[4,264,256]{2,1,0:T(8,128)(2,1)S(1)}, bf16[2,128,128]{2,1,0:T(8,128)(2,1)S(1)}) custom-call(s32[4]{0:T(128)S(1)} %pad_add_fusion.sc_ref, bf16[264,256]{1,0:T(8,128)(2,1)S(1)} %get-tuple-element.87.p0, bf16[264,256]{1,0:T(8,128)(2,1)S(1)} %collective-permute-done.2.p1, bf16[264,256]{1,0:T(8,128)(2,1)S(1)} %collective-permute-done.3.p2, ...), custom_call_target="tpu_custom_call" | custom-call | flops 100 | bytes 100 | tf_op jit(solution)/shard_map/gather/pallas_call | solution.py:243
  37.1 2.9 %collective-permute-start.5 = (bf16[2,128,128]{2,1,0:T(8,128)(2,1)S(1)}, bf16[2,128,128]{2,1,0:T(8,128)(2,1)S(1)}, u32[]{:S(2)}, u32[]{:S(2)}) collective-permute-start(bf16[2,128,128]{2,1,0:T(8,128)(2,1)S(1)} %get-tuple-element.92), channel_id=1, source_target_pairs={{0,8},{1,9},{2,10},{3,11},{4,12},{5,13},{6,14},{7,15},{8,0},{9,1},... | collective-permute-start | bytes 196616 | tf_op jit(solution)/shard_map/ppermute | solution.py:504
  40.0 1.0 %spread.3 = (bf16[2,128,128]{2,1,0:T(8,128)(2,1)S(1)}, bf16[2,128,128]{2,1,0:T(8,128)(2,1)S(1)}, bf16[2,128,128]{2,1,0:T(8,128)(2,1)S(1)}, bf16[2,128,128]{2,1,0:T(8,128)(2,1)S(1)}) custom-call(s32[4]{0:T(128)S(1)} %pad_add_fusion.sc_ref, bf16[4,264,256]{2,1,0:T(8,128)(2,1)S(1)} %get-tuple-element.105.order_ref, ...), custom_call_target="tpu_custom_call" | custom-call | flops 100 | bytes 100 | tf_op jit(solution)/shard_map/spread/pallas_call | solution.py:243
  41.0 1.0 %collective-permute-start.15 = (bf16[2,128,128]{2,1,0:T(8,128)(2,1)S(1)}, bf16[2,128,128]{2,1,0:T(8,128)(2,1)S(1)}, u32[]{:S(2)}, u32[]{:S(2)}) collective-permute-start(bf16[2,128,128]{2,1,0:T(8,128)(2,1)S(1)} %get-tuple-element.108), channel_id=1, source_target_pairs={{0,2},{1,3},{2,0},{3,1},{4,6},{5,7},{6,4},{7,5},{8,10},{9,11},{10,... | collective-permute-start | bytes 196616 | tf_op jit(solution)/shard_map/ppermute | solution.py:504
  42.0 0.8 %collective-permute-start.16 = (bf16[2,128,128]{2,1,0:T(8,128)(2,1)S(1)}, bf16[2,128,128]{2,1,0:T(8,128)(2,1)S(1)}, u32[]{:S(2)}, u32[]{:S(2)}) collective-permute-start(bf16[2,128,128]{2,1,0:T(8,128)(2,1)S(1)} %get-tuple-element.109), channel_id=1, source_target_pairs={{0,4},{1,5},{2,6},{3,7},{4,0},{5,1},{6,2},{7,3},{8,12},{9,13},{10,... | collective-permute-start | bytes 196616 | tf_op jit(solution)/shard_map/ppermute | solution.py:504
  42.9 1.7 %collective-permute-start.17 = (bf16[2,128,128]{2,1,0:T(8,128)(2,1)S(1)}, bf16[2,128,128]{2,1,0:T(8,128)(2,1)S(1)}, u32[]{:S(2)}, u32[]{:S(2)}) collective-permute-start(bf16[2,128,128]{2,1,0:T(8,128)(2,1)S(1)} %get-tuple-element.110), channel_id=1, source_target_pairs={{0,6},{1,7},{2,4},{3,5},{4,2},{5,3},{6,0},{7,1},{8,14},{9,15},{10,... | collective-permute-start | bytes 196616 | tf_op jit(solution)/shard_map/ppermute | solution.py:504
  44.6 1.0 %spread.2 = (bf16[2,128,128]{2,1,0:T(8,128)(2,1)S(1)}, bf16[2,128,128]{2,1,0:T(8,128)(2,1)S(1)}, bf16[2,128,128]{2,1,0:T(8,128)(2,1)S(1)}, bf16[2,128,128]{2,1,0:T(8,128)(2,1)S(1)}) custom-call(s32[4]{0:T(128)S(1)} %pad_add_fusion.sc_ref, bf16[4,264,256]{2,1,0:T(8,128)(2,1)S(1)} %get-tuple-element.91.order_ref, ...), custom_call_target="tpu_custom_call" | custom-call | flops 100 | bytes 100 | tf_op jit(solution)/shard_map/spread/pallas_call | solution.py:243
  45.6 1.0 %collective-permute-start.6 = (bf16[2,128,128]{2,1,0:T(8,128)(2,1)S(1)}, bf16[2,128,128]{2,1,0:T(8,128)(2,1)S(1)}, u32[]{:S(2)}, u32[]{:S(2)}) collective-permute-start(bf16[2,128,128]{2,1,0:T(8,128)(2,1)S(1)} %get-tuple-element.94), channel_id=1, source_target_pairs={{0,2},{1,3},{2,0},{3,1},{4,6},{5,7},{6,4},{7,5},{8,10},{9,11},{10,... | collective-permute-start | bytes 196616 | tf_op jit(solution)/shard_map/ppermute | solution.py:504
  46.6 0.8 %collective-permute-start.7 = (bf16[2,128,128]{2,1,0:T(8,128)(2,1)S(1)}, bf16[2,128,128]{2,1,0:T(8,128)(2,1)S(1)}, u32[]{:S(2)}, u32[]{:S(2)}) collective-permute-start(bf16[2,128,128]{2,1,0:T(8,128)(2,1)S(1)} %get-tuple-element.95), channel_id=1, source_target_pairs={{0,4},{1,5},{2,6},{3,7},{4,0},{5,1},{6,2},{7,3},{8,12},{9,13},{10,... | collective-permute-start | bytes 196616 | tf_op jit(solution)/shard_map/ppermute | solution.py:504
  47.4 1.7 %collective-permute-start.8 = (bf16[2,128,128]{2,1,0:T(8,128)(2,1)S(1)}, bf16[2,128,128]{2,1,0:T(8,128)(2,1)S(1)}, u32[]{:S(2)}, u32[]{:S(2)}) collective-permute-start(bf16[2,128,128]{2,1,0:T(8,128)(2,1)S(1)} %get-tuple-element.96), channel_id=1, source_target_pairs={{0,6},{1,7},{2,4},{3,5},{4,2},{5,3},{6,0},{7,1},{8,14},{9,15},{10,... | collective-permute-start | bytes 196616 | tf_op jit(solution)/shard_map/ppermute | solution.py:504
  49.8 0.8 %enter.3 = (bf16[4,2,128,128]{3,2,1,0:T(8,128)(2,1)S(1)}, bf16[4,2,128,128]{3,2,1,0:T(8,128)(2,1)S(1)}) custom-call(s32[4]{0:T(128)S(1)} %pad_add_fusion.sc_ref, bf16[4,264,256]{2,1,0:T(8,128)(2,1)S(1)} %get-tuple-element.100.first_ref, bf16[2,128,128]{2,1,0:T(8,128)(2,1)S(1)} %get-tuple-element.107.refs_0_, ...), custom_call_target="tpu_custom_call" | custom-call | flops 100 | bytes 100 | tf_op jit(solution)/shard_map/enter/pallas_call | solution.py:243
  50.9 1.7 %collective-permute-done.8.refs_3_ = bf16[2,128,128]{2,1,0:T(8,128)(2,1)S(1)} collective-permute-done((bf16[2,128,128]{2,1,0:T(8,128)(2,1)S(1)}, bf16[2,128,128]{2,1,0:T(8,128)(2,1)S(1)}, u32[]{:S(2)}, u32[]{:S(2)}) %collective-permute-start.8) | collective-permute-done | bytes 65568 | tf_op jit(solution)/shard_map/ppermute | solution.py:504
  52.6 0.8 %enter.2 = (bf16[4,2,128,128]{3,2,1,0:T(8,128)(2,1)S(1)}, bf16[4,2,128,128]{3,2,1,0:T(8,128)(2,1)S(1)}) custom-call(s32[4]{0:T(128)S(1)} %pad_add_fusion.sc_ref, bf16[4,264,256]{2,1,0:T(8,128)(2,1)S(1)} %get-tuple-element.86.first_ref, bf16[2,128,128]{2,1,0:T(8,128)(2,1)S(1)} %get-tuple-element.93.refs_0_, ...), custom_call_target="tpu_custom_call" | custom-call | flops 100 | bytes 100 | tf_op jit(solution)/shard_map/enter/pallas_call | solution.py:243
  53.5 1.3 %finish.1 = (bf16[4,128,256]{2,1,0:T(8,128)(2,1)S(1)}, bf16[4,128,256]{2,1,0:T(8,128)(2,1)S(1)}, bf16[4,128,256]{2,1,0:T(8,128)(2,1)S(1)}) custom-call(s32[4]{0:T(128)S(1)} %pad_add_fusion.sc_ref, f32[128,4096]{1,0:T(8,128)S(1)} %gates.1.gate_ref, bf16[4,2,128,128]{3,2,1,0:T(8,128)(2,1)S(1)} %get-tuple-element.111.refs_0_, ...), custom_call_target="tpu_custom_call" | custom-call | flops 100 | bytes 100 | tf_op jit(solution)/shard_map/finish/pallas_call | solution.py:243
  55.1 1.7 %finish_last.1 = bf16[128,4096]{1,0:T(8,128)(2,1)} custom-call(s32[4]{0:T(128)S(1)} %pad_add_fusion.sc_ref, f32[128,4096]{1,0:T(8,128)S(1)} %gates.1.gate_ref, bf16[4,2,128,128]{3,2,1,0:T(8,128)(2,1)S(1)} %collective-permute-done.9.state_ref, f32[4,2,128,128]{3,2,1,0:T(8,128)S(1)} %get-tuple-element.78.loc_ref, ...), custom_call_target="tpu_custom_call" | custom-call | flops 100 | bytes 100 | tf_op jit(solution)/shard_map/finish_last/pallas_call | solution.py:483
  (34 shorter events, 1.6 us)
Async XLA Ops:
  0.0 6.4 %copy-start.1 = (bf16[7,128,128]{2,1,0:T(8,128)(2,1)S(1)}, bf16[7,128,128]{2,1,0:T(8,128)(2,1)}, u32[]{:S(2)}) copy-start(bf16[7,128,128]{2,1,0:T(8,128)(2,1)} %constant.54.clone.masks_ref) | copy-start | bytes 688132
  0.0 4.2 %copy-start.2 = (f32[128,32]{0,1:T(8,128)S(1)}, f32[128,32]{0,1:T(8,128)}, u32[]{:S(2)}) copy-start(f32[128,32]{0,1:T(8,128)} %param.10) | copy-start | bytes 49156
  0.0 4.2 %copy-start.3 = (bf16[128,32]{0,1:T(8,128)(2,1)S(1)}, bf16[128,32]{0,1:T(8,128)(2,1)}, u32[]{:S(2)}) copy-start(bf16[128,32]{0,1:T(8,128)(2,1)} %param.9) | copy-start | bytes 24580
  1.7 4.7 %collective-permute-start = (bf16[4,8192]{1,0:T(4,128)(2,1)S(1)}, bf16[4,8192]{1,0:T(4,128)(2,1)S(1)}, u32[]{:S(2)}, u32[]{:S(2)}) collective-permute-start(bf16[4,8192]{1,0:T(4,128)(2,1)S(1)} %get-tuple-element.62), channel_id=1, source_target_pairs={{0,1},{1,2},{2,3},{3,4},{4,5},{5,6},{6,7},{7,8},{8,9},{9,10},{10,1... | collective-permute-start | bytes 196616 | tf_op jit(solution)/shard_map/ppermute | solution.py:500
  11.1 7.5 %collective-permute-start.10 = (bf16[4,264,256]{2,1,0:T(8,128)(2,1)S(1)}, bf16[4,264,256]{2,1,0:T(8,128)(2,1)S(1)}, u32[]{:S(2)}, u32[]{:S(2)}) collective-permute-start(bf16[4,264,256]{2,1,0:T(8,128)(2,1)S(1)} %get-tuple-element.99), channel_id=1, source_target_pairs={{0,1},{1,0},{2,3},{3,2},{4,5},{5,4},{6,7},{7,6},{8,9},{9,8},{10,11... | collective-permute-start | bytes 1622024 | tf_op jit(solution)/shard_map/ppermute | solution.py:504
  18.5 5.2 %collective-permute-start.1 = (bf16[4,264,256]{2,1,0:T(8,128)(2,1)S(1)}, bf16[4,264,256]{2,1,0:T(8,128)(2,1)S(1)}, u32[]{:S(2)}, u32[]{:S(2)}) collective-permute-start(bf16[4,264,256]{2,1,0:T(8,128)(2,1)S(1)} %get-tuple-element.85), channel_id=1, source_target_pairs={{0,1},{1,0},{2,3},{3,2},{4,5},{5,4},{6,7},{7,6},{8,9},{9,8},{10,11... | collective-permute-start | bytes 1622024 | tf_op jit(solution)/shard_map/ppermute | solution.py:504
  19.5 8.0 %collective-permute-start.11 = (bf16[264,256]{1,0:T(8,128)(2,1)S(1)}, bf16[264,256]{1,0:T(8,128)(2,1)S(1)}, u32[]{:S(2)}, u32[]{:S(2)}) collective-permute-start(bf16[264,256]{1,0:T(8,128)(2,1)S(1)} %get-tuple-element.102), channel_id=1, source_target_pairs={{0,2},{1,3},{2,0},{3,1},{4,6},{5,7},{6,4},{7,5},{8,10},{9,11},{10,... | collective-permute-start | bytes 405512 | tf_op jit(solution)/shard_map/ppermute | solution.py:504
  21.3 10.7 %collective-permute-start.12 = (bf16[264,256]{1,0:T(8,128)(2,1)S(1)}, bf16[264,256]{1,0:T(8,128)(2,1)S(1)}, u32[]{:S(2)}, u32[]{:S(2)}) collective-permute-start(bf16[264,256]{1,0:T(8,128)(2,1)S(1)} %get-tuple-element.103), channel_id=1, source_target_pairs={{0,4},{1,5},{2,6},{3,7},{4,0},{5,1},{6,2},{7,3},{8,12},{9,13},{10,... | collective-permute-start | bytes 405512 | tf_op jit(solution)/shard_map/ppermute | solution.py:504
  22.9 9.1 %collective-permute-start.13 = (bf16[264,256]{1,0:T(8,128)(2,1)S(1)}, bf16[264,256]{1,0:T(8,128)(2,1)S(1)}, u32[]{:S(2)}, u32[]{:S(2)}) collective-permute-start(bf16[264,256]{1,0:T(8,128)(2,1)S(1)} %get-tuple-element.104), channel_id=1, source_target_pairs={{0,6},{1,7},{2,4},{3,5},{4,2},{5,3},{6,0},{7,1},{8,14},{9,15},{10,... | collective-permute-start | bytes 405512 | tf_op jit(solution)/shard_map/ppermute | solution.py:504
  24.8 10.9 %collective-permute-start.2 = (bf16[264,256]{1,0:T(8,128)(2,1)S(1)}, bf16[264,256]{1,0:T(8,128)(2,1)S(1)}, u32[]{:S(2)}, u32[]{:S(2)}) collective-permute-start(bf16[264,256]{1,0:T(8,128)(2,1)S(1)} %get-tuple-element.88), channel_id=1, source_target_pairs={{0,2},{1,3},{2,0},{3,1},{4,6},{5,7},{6,4},{7,5},{8,10},{9,11},{10,... | collective-permute-start | bytes 405512 | tf_op jit(solution)/shard_map/ppermute | solution.py:504
  25.9 9.8 %collective-permute-start.3 = (bf16[264,256]{1,0:T(8,128)(2,1)S(1)}, bf16[264,256]{1,0:T(8,128)(2,1)S(1)}, u32[]{:S(2)}, u32[]{:S(2)}) collective-permute-start(bf16[264,256]{1,0:T(8,128)(2,1)S(1)} %get-tuple-element.89), channel_id=1, source_target_pairs={{0,4},{1,5},{2,6},{3,7},{4,0},{5,1},{6,2},{7,3},{8,12},{9,13},{10,... | collective-permute-start | bytes 405512 | tf_op jit(solution)/shard_map/ppermute | solution.py:504
  27.5 8.4 %collective-permute-start.4 = (bf16[264,256]{1,0:T(8,128)(2,1)S(1)}, bf16[264,256]{1,0:T(8,128)(2,1)S(1)}, u32[]{:S(2)}, u32[]{:S(2)}) collective-permute-start(bf16[264,256]{1,0:T(8,128)(2,1)S(1)} %get-tuple-element.90), channel_id=1, source_target_pairs={{0,6},{1,7},{2,4},{3,5},{4,2},{5,3},{6,0},{7,1},{8,14},{9,15},{10,... | collective-permute-start | bytes 405512 | tf_op jit(solution)/shard_map/ppermute | solution.py:504
  31.9 17.2 %copy-start = (bf16[128,4096]{1,0:T(8,128)(2,1)S(1)}, bf16[128,4096]{1,0:T(8,128)(2,1)}, u32[]{:S(2)}) copy-start(bf16[128,4096]{1,0:T(8,128)(2,1)} %gate_ref.1) | copy-start | bytes 3145732
  32.0 17.2 %copy-start.4 = (f32[128]{0:T(128)S(1)}, f32[128]{0:T(128)}, u32[]{:S(2)}) copy-start(f32[128]{0:T(128)} %param.12) | copy-start | bytes 1540
  33.2 6.8 %collective-permute-start.14 = (bf16[2,128,128]{2,1,0:T(8,128)(2,1)S(1)}, bf16[2,128,128]{2,1,0:T(8,128)(2,1)S(1)}, u32[]{:S(2)}, u32[]{:S(2)}) collective-permute-start(bf16[2,128,128]{2,1,0:T(8,128)(2,1)S(1)} %get-tuple-element.106), channel_id=1, source_target_pairs={{0,8},{1,9},{2,10},{3,11},{4,12},{5,13},{6,14},{7,15},{8,0},{9,1},... | collective-permute-start | bytes 196616 | tf_op jit(solution)/shard_map/ppermute | solution.py:504
  37.1 7.5 %collective-permute-start.5 = (bf16[2,128,128]{2,1,0:T(8,128)(2,1)S(1)}, bf16[2,128,128]{2,1,0:T(8,128)(2,1)S(1)}, u32[]{:S(2)}, u32[]{:S(2)}) collective-permute-start(bf16[2,128,128]{2,1,0:T(8,128)(2,1)S(1)} %get-tuple-element.92), channel_id=1, source_target_pairs={{0,8},{1,9},{2,10},{3,11},{4,12},{5,13},{6,14},{7,15},{8,0},{9,1},... | collective-permute-start | bytes 196616 | tf_op jit(solution)/shard_map/ppermute | solution.py:504
  41.0 6.4 %collective-permute-start.15 = (bf16[2,128,128]{2,1,0:T(8,128)(2,1)S(1)}, bf16[2,128,128]{2,1,0:T(8,128)(2,1)S(1)}, u32[]{:S(2)}, u32[]{:S(2)}) collective-permute-start(bf16[2,128,128]{2,1,0:T(8,128)(2,1)S(1)} %get-tuple-element.108), channel_id=1, source_target_pairs={{0,2},{1,3},{2,0},{3,1},{4,6},{5,7},{6,4},{7,5},{8,10},{9,11},{10,... | collective-permute-start | bytes 196616 | tf_op jit(solution)/shard_map/ppermute | solution.py:504
  42.0 7.8 %collective-permute-start.16 = (bf16[2,128,128]{2,1,0:T(8,128)(2,1)S(1)}, bf16[2,128,128]{2,1,0:T(8,128)(2,1)S(1)}, u32[]{:S(2)}, u32[]{:S(2)}) collective-permute-start(bf16[2,128,128]{2,1,0:T(8,128)(2,1)S(1)} %get-tuple-element.109), channel_id=1, source_target_pairs={{0,4},{1,5},{2,6},{3,7},{4,0},{5,1},{6,2},{7,3},{8,12},{9,13},{10,... | collective-permute-start | bytes 196616 | tf_op jit(solution)/shard_map/ppermute | solution.py:504
  42.9 6.9 %collective-permute-start.17 = (bf16[2,128,128]{2,1,0:T(8,128)(2,1)S(1)}, bf16[2,128,128]{2,1,0:T(8,128)(2,1)S(1)}, u32[]{:S(2)}, u32[]{:S(2)}) collective-permute-start(bf16[2,128,128]{2,1,0:T(8,128)(2,1)S(1)} %get-tuple-element.110), channel_id=1, source_target_pairs={{0,6},{1,7},{2,4},{3,5},{4,2},{5,3},{6,0},{7,1},{8,14},{9,15},{10,... | collective-permute-start | bytes 196616 | tf_op jit(solution)/shard_map/ppermute | solution.py:504
  45.6 5.1 %collective-permute-start.6 = (bf16[2,128,128]{2,1,0:T(8,128)(2,1)S(1)}, bf16[2,128,128]{2,1,0:T(8,128)(2,1)S(1)}, u32[]{:S(2)}, u32[]{:S(2)}) collective-permute-start(bf16[2,128,128]{2,1,0:T(8,128)(2,1)S(1)} %get-tuple-element.94), channel_id=1, source_target_pairs={{0,2},{1,3},{2,0},{3,1},{4,6},{5,7},{6,4},{7,5},{8,10},{9,11},{10,... | collective-permute-start | bytes 196616 | tf_op jit(solution)/shard_map/ppermute | solution.py:504
  46.6 4.3 %collective-permute-start.7 = (bf16[2,128,128]{2,1,0:T(8,128)(2,1)S(1)}, bf16[2,128,128]{2,1,0:T(8,128)(2,1)S(1)}, u32[]{:S(2)}, u32[]{:S(2)}) collective-permute-start(bf16[2,128,128]{2,1,0:T(8,128)(2,1)S(1)} %get-tuple-element.95), channel_id=1, source_target_pairs={{0,4},{1,5},{2,6},{3,7},{4,0},{5,1},{6,2},{7,3},{8,12},{9,13},{10,... | collective-permute-start | bytes 196616 | tf_op jit(solution)/shard_map/ppermute | solution.py:504
  47.4 5.2 %collective-permute-start.8 = (bf16[2,128,128]{2,1,0:T(8,128)(2,1)S(1)}, bf16[2,128,128]{2,1,0:T(8,128)(2,1)S(1)}, u32[]{:S(2)}, u32[]{:S(2)}) collective-permute-start(bf16[2,128,128]{2,1,0:T(8,128)(2,1)S(1)} %get-tuple-element.96), channel_id=1, source_target_pairs={{0,6},{1,7},{2,4},{3,5},{4,2},{5,3},{6,0},{7,1},{8,14},{9,15},{10,... | collective-permute-start | bytes 196616 | tf_op jit(solution)/shard_map/ppermute | solution.py:504
  50.6 2.9 %collective-permute-start.18 = (bf16[4,2,128,128]{3,2,1,0:T(8,128)(2,1)S(1)}, bf16[4,2,128,128]{3,2,1,0:T(8,128)(2,1)S(1)}, u32[]{:S(2)}, u32[]{:S(2)}) collective-permute-start(bf16[4,2,128,128]{3,2,1,0:T(8,128)(2,1)S(1)} %get-tuple-element.112), channel_id=1, source_target_pairs={{0,1},{1,0},{2,3},{3,2},{4,5},{5,4},{6,7},{7,6},{8,9},{9,8},{10,11... | collective-permute-start | bytes 786440 | tf_op jit(solution)/shard_map/ppermute | solution.py:504
  53.5 1.6 %collective-permute-start.9 = (bf16[4,2,128,128]{3,2,1,0:T(8,128)(2,1)S(1)}, bf16[4,2,128,128]{3,2,1,0:T(8,128)(2,1)S(1)}, u32[]{:S(2)}, u32[]{:S(2)}) collective-permute-start(bf16[4,2,128,128]{3,2,1,0:T(8,128)(2,1)S(1)} %get-tuple-element.97), channel_id=1, source_target_pairs={{0,1},{1,0},{2,3},{3,2},{4,5},{5,4},{6,7},{7,6},{8,9},{9,8},{10,11... | collective-permute-start | bytes 786440 | tf_op jit(solution)/shard_map/ppermute | solution.py:504

commit v7 on v6

--- a/solution.py
+++ b/solution.py
@@ -202,13 +202,12 @@
                     system = jnp.where(strict, system, 0.0).astype(BF16)
                     beta_row = rows[4 + h : 5 + h]
                     gains = jnp.broadcast_to(beta_row * following[4 + h : 5 + h], (CH, CH)).astype(BF16)
-                    high, low = halves(jnp.broadcast_to(beta_row, (CH, CH)))
+                    high = jnp.broadcast_to(beta_row, (CH, CH)).astype(BF16)
                     heads.append(
                         dict(
                             out=(ma_ref, solved_ref, offset, 2 * g + i),
                             system=system,
                             inv=unit * high - system * masks_ref[0] * gains,
-                            inv_low=unit * low,
                             value=cv[:, head_slice(2 * g + i)].astype(BF16),
                             key=(k_f * (grow_cols[:, h : h + 1] * rk_col)).astype(BF16),
                             tail=(k_t * (rk_row * tail_rows[h : h + 1])).astype(BF16),
@@ -225,8 +224,8 @@
     for p in heads:
         right = jnp.concatenate([p["key"], p["value"]], axis=1)
         p["solved"] = dot(
-            jnp.concatenate([p["inv"], p["inv_low"]], axis=1),
-            jnp.concatenate([right, right], axis=0),
+            p["inv"],
+            right,
         ).astype(BF16)
     for p in heads:
         ma_ref, solved_ref, offset, h = p["out"]
@@ -407,14 +406,22 @@
 
 def enter_kernel(keys, sc_ref, first_ref, *refs):
     starts, (keep_ref, send_ref) = refs[:CHIPS], refs[CHIPS:]
-    is_first = sc_ref[0] == 0
-    for offset in range(CHIPS):
-        decays = decays_at(first_ref, offset)
-        for h in range(2 * len(keys)):
-            start = starts[offset][h]
-            after = advance(keys, first_ref, offset, h, decays, start)
-            keep_ref[offset, h] = jnp.where(is_first, start, after)
-            send_ref[offset, h] = jnp.where(is_first, after, start)
+
+    def fill(start_ref, after_ref):
+        for offset in range(CHIPS):
+            decays = decays_at(first_ref, offset)
+            for h in range(2 * len(keys)):
+                start = starts[offset][h]
+                start_ref[offset, h] = start
+                after_ref[offset, h] = advance(keys, first_ref, offset, h, decays, start)
+
+    @pl.when(sc_ref[0] == 0)
+    def _():
+        fill(keep_ref, send_ref)
+
+    @pl.when(sc_ref[0] == 1)
+    def _():
+        fill(send_ref, keep_ref)
 
 
 def gates_kernel(gate_ref, gain_ref, out_ref):

time: 57.1 us -> 56.9 us (level)
  no operation moved by 1% of the time
where the time goes in v7:
time: 56.9 us; the launch traced here: 56.7 us
  Pallas kernels  28.2 us (50%)
  starting transfers between devices  25.6 us (45%)
  waiting for transfers between devices  2.38 us (4%)
    pallas_call x14, Pallas kernels, local_call(): pl.pallas_call(kernel, out_shape=out_shape, in_specs=in_specs, out_specs=...  24.8 us
    ppermute x18, starting transfers between devices, swap(): lax.ppermute(block, 'seq', [(i, i ^ distance) for i in range(lax.axis_siz...  23.2 us
    ppermute x18, waiting for transfers between devices, swap(): lax.ppermute(block, 'seq', [(i, i ^ distance) for i in range(lax.axis_siz...  2.38 us
    ppermute x1, starting transfers between devices, shift(): lax.ppermute(block, 'seq', [(i, i + distance) for i in range(count - dist...  2.37 us
    pallas_call x1, Pallas kernels, finish_last(): pl.pallas_call(functools.partial(last_kernel, earlier, keys, own), out_sh...  1.7 us
    pallas_call x1, Pallas kernels, load(): pl.pallas_call(load_kernel, out_shape=[jax.ShapeDtypeStruct(mixed_qkv.sha...  1.68 us
  transfers between devices with their start and end apart: 19, of which 4 were waited for; matrix products, arithmetic and copies ran while one was open for 0% of the time, Pallas kernels for 36%

profile of v7, /device:TPU:0, one launch (start us, length us, event | category | flops | bytes accessed | tf_op | source)
XLA Modules:
  0.0 56.7 jit_solution(400387036329780947)
XLA Ops:
  0.0 1.7 %load.1 = (bf16[128,8192]{1,0:T(8,128)(2,1)S(1)}, bf16[4,8192]{1,0:T(4,128)(2,1)S(1)}, bf16[4,8192]{1,0:T(4,128)(2,1)S(1)}) custom-call(bf16[128,8192]{1,0:T(8,128)(2,1)} %x_ref.1, bf16[4,8192]{1,0:T(4,128)(2,1)} %w_ref.1), custom_call_target="tpu_custom_call" | custom-call | flops 100 | bytes 100 | tf_op jit(solution)/shard_map/load/pallas_call | solution.py:92
  1.7 2.4 %collective-permute-start = (bf16[4,8192]{1,0:T(4,128)(2,1)S(1)}, bf16[4,8192]{1,0:T(4,128)(2,1)S(1)}, u32[]{:S(2)}, u32[]{:S(2)}) collective-permute-start(bf16[4,8192]{1,0:T(4,128)(2,1)S(1)} %get-tuple-element.62), channel_id=1, source_target_pairs={{0,1},{1,2},{2,3},{3,4},{4,5},{5,6},{6,7},{7,8},{8,9},{9,10},{10,1... | collective-permute-start | bytes 196616 | tf_op jit(solution)/shard_map/ppermute | solution.py:507
  4.2 2.2 %conv.1 = (bf16[128,8192]{1,0:T(8,128)(2,1)S(1)}, f32[8,8,128]{2,1,0:T(8,128)S(1)}) custom-call(s32[4]{0:T(128)S(1)} %pad_add_fusion.sc_ref, bf16[128,8192]{1,0:T(8,128)(2,1)S(1)} %get-tuple-element.61.x_ref, bf16[4,8192]{1,0:T(4,128)(2,1)S(1)} %get-tuple-element.63.w_ref, f32[32,128]{1,0:T(8,128)S(1)} %bitcast.7, bf16[32,128]{1,0:T(8,128)(2,1)S(1)} %bitcast.8), custom_call_target="tpu_custom_call" | custom-call | flops 100 | bytes 100 | tf_op jit(solution)/shard_map/conv/pallas_call | solution.py:242
  6.4 4.6 %terms.2 = (bf16[4,264,256]{2,1,0:T(8,128)(2,1)S(1)}, bf16[4,2,128,256]{3,2,1,0:T(8,128)(2,1)S(1)}, bf16[4,1,128,128]{3,2,1,0:T(8,128)(2,1)S(1)}, bf16[4,264,256...) custom-call(s32[4]{0:T(128)S(1)} %pad_add_fusion.sc_ref, ...), custom_call_target="tpu_custom_call" | custom-call | flops 100 | bytes 100 | tf_op jit(solution)/shard_map/terms/pallas_call | solution.py:242
  11.0 2.7 %collective-permute-start.10 = (bf16[4,264,256]{2,1,0:T(8,128)(2,1)S(1)}, bf16[4,264,256]{2,1,0:T(8,128)(2,1)S(1)}, u32[]{:S(2)}, u32[]{:S(2)}) collective-permute-start(bf16[4,264,256]{2,1,0:T(8,128)(2,1)S(1)} %get-tuple-element.99), channel_id=1, source_target_pairs={{0,1},{1,0},{2,3},{3,2},{4,5},{5,4},{6,7},{7,6},{8,9},{9,8},{10,11... | collective-permute-start | bytes 1622024 | tf_op jit(solution)/shard_map/ppermute | solution.py:511
  13.7 4.6 %terms.3 = (bf16[4,264,256]{2,1,0:T(8,128)(2,1)S(1)}, bf16[4,2,128,256]{3,2,1,0:T(8,128)(2,1)S(1)}, bf16[4,1,128,128]{3,2,1,0:T(8,128)(2,1)S(1)}, bf16[4,264,256...) custom-call(s32[4]{0:T(128)S(1)} %pad_add_fusion.sc_ref, ...), custom_call_target="tpu_custom_call" | custom-call | flops 100 | bytes 100 | tf_op jit(solution)/shard_map/terms/pallas_call | solution.py:242
  18.4 0.9 %compose.3 = (bf16[4,264,256]{2,1,0:T(8,128)(2,1)S(1)}, bf16[264,256]{1,0:T(8,128)(2,1)S(1)}, bf16[264,256]{1,0:T(8,128)(2,1)S(1)}, bf16[264,256]{1,0:T(8,128)(2,1)S(1)}, bf16[264,256]{1,0:T(8,128)(2,1)S(1)}) custom-call(s32[4]{0:T(128)S(1)} %pad_add_fusion.sc_ref, bf16[4,264,256]{2,1,0:T(8,128)(2,1)S(1)} %get-tuple-element.98.mine_ref, ...), custom_call_target="tpu_custom_call" | custom-call | flops 100 | bytes 100 | tf_op jit(solution)/shard_map/compose/pallas_call | solution.py:242
  19.4 1.8 %collective-permute-start.11 = (bf16[264,256]{1,0:T(8,128)(2,1)S(1)}, bf16[264,256]{1,0:T(8,128)(2,1)S(1)}, u32[]{:S(2)}, u32[]{:S(2)}) collective-permute-start(bf16[264,256]{1,0:T(8,128)(2,1)S(1)} %get-tuple-element.102), channel_id=1, source_target_pairs={{0,2},{1,3},{2,0},{3,1},{4,6},{5,7},{6,4},{7,5},{8,10},{9,11},{10,... | collective-permute-start | bytes 405512 | tf_op jit(solution)/shard_map/ppermute | solution.py:511
  21.2 1.6 %collective-permute-start.12 = (bf16[264,256]{1,0:T(8,128)(2,1)S(1)}, bf16[264,256]{1,0:T(8,128)(2,1)S(1)}, u32[]{:S(2)}, u32[]{:S(2)}) collective-permute-start(bf16[264,256]{1,0:T(8,128)(2,1)S(1)} %get-tuple-element.103), channel_id=1, source_target_pairs={{0,4},{1,5},{2,6},{3,7},{4,0},{5,1},{6,2},{7,3},{8,12},{9,13},{10,... | collective-permute-start | bytes 405512 | tf_op jit(solution)/shard_map/ppermute | solution.py:511
  22.7 0.8 %collective-permute-start.13 = (bf16[264,256]{1,0:T(8,128)(2,1)S(1)}, bf16[264,256]{1,0:T(8,128)(2,1)S(1)}, u32[]{:S(2)}, u32[]{:S(2)}) collective-permute-start(bf16[264,256]{1,0:T(8,128)(2,1)S(1)} %get-tuple-element.104), channel_id=1, source_target_pairs={{0,6},{1,7},{2,4},{3,5},{4,2},{5,3},{6,0},{7,1},{8,14},{9,15},{10,... | collective-permute-start | bytes 405512 | tf_op jit(solution)/shard_map/ppermute | solution.py:511
  23.6 1.1 %compose.2 = (bf16[4,264,256]{2,1,0:T(8,128)(2,1)S(1)}, bf16[264,256]{1,0:T(8,128)(2,1)S(1)}, bf16[264,256]{1,0:T(8,128)(2,1)S(1)}, bf16[264,256]{1,0:T(8,128)(2,1)S(1)}, bf16[264,256]{1,0:T(8,128)(2,1)S(1)}) custom-call(s32[4]{0:T(128)S(1)} %pad_add_fusion.sc_ref, bf16[4,264,256]{2,1,0:T(8,128)(2,1)S(1)} %get-tuple-element.84.mine_ref, ...), custom_call_target="tpu_custom_call" | custom-call | flops 100 | bytes 100 | tf_op jit(solution)/shard_map/compose/pallas_call | solution.py:242
  24.7 1.1 %collective-permute-start.2 = (bf16[264,256]{1,0:T(8,128)(2,1)S(1)}, bf16[264,256]{1,0:T(8,128)(2,1)S(1)}, u32[]{:S(2)}, u32[]{:S(2)}) collective-permute-start(bf16[264,256]{1,0:T(8,128)(2,1)S(1)} %get-tuple-element.88), channel_id=1, source_target_pairs={{0,2},{1,3},{2,0},{3,1},{4,6},{5,7},{6,4},{7,5},{8,10},{9,11},{10,... | collective-permute-start | bytes 405512 | tf_op jit(solution)/shard_map/ppermute | solution.py:511
  25.8 1.6 %collective-permute-start.3 = (bf16[264,256]{1,0:T(8,128)(2,1)S(1)}, bf16[264,256]{1,0:T(8,128)(2,1)S(1)}, u32[]{:S(2)}, u32[]{:S(2)}) collective-permute-start(bf16[264,256]{1,0:T(8,128)(2,1)S(1)} %get-tuple-element.89), channel_id=1, source_target_pairs={{0,4},{1,5},{2,6},{3,7},{4,0},{5,1},{6,2},{7,3},{8,12},{9,13},{10,... | collective-permute-start | bytes 405512 | tf_op jit(solution)/shard_map/ppermute | solution.py:511
  27.4 0.8 %collective-permute-start.4 = (bf16[264,256]{1,0:T(8,128)(2,1)S(1)}, bf16[264,256]{1,0:T(8,128)(2,1)S(1)}, u32[]{:S(2)}, u32[]{:S(2)}) collective-permute-start(bf16[264,256]{1,0:T(8,128)(2,1)S(1)} %get-tuple-element.90), channel_id=1, source_target_pairs={{0,6},{1,7},{2,4},{3,5},{4,2},{5,3},{6,0},{7,1},{8,14},{9,15},{10,... | collective-permute-start | bytes 405512 | tf_op jit(solution)/shard_map/ppermute | solution.py:511
  28.2 3.6 %queries.1 = (f32[4,2,128,128]{3,2,1,0:T(8,128)S(1)}, bf16[4,2,128,128]{3,2,1,0:T(8,128)(2,1)S(1)}, f32[4,2,128,128]{3,2,1,0:T(8,128)S(1)}, bf16[4,2,128,128]{3,...) custom-call(s32[4]{0:T(128)S(1)} %pad_add_fusion.sc_ref, ...), custom_call_target="tpu_custom_call" | custom-call | flops 100 | bytes 100 | tf_op jit(solution)/shard_map/queries/pallas_call | solution.py:242
  31.9 1.2 %gather.3 = (bf16[4,264,256]{2,1,0:T(8,128)(2,1)S(1)}, bf16[2,128,128]{2,1,0:T(8,128)(2,1)S(1)}) custom-call(s32[4]{0:T(128)S(1)} %pad_add_fusion.sc_ref, bf16[264,256]{1,0:T(8,128)(2,1)S(1)} %get-tuple-element.101.p0, bf16[264,256]{1,0:T(8,128)(2,1)S(1)} %collective-permute-done.11.p1, bf16[264,256]{1,0:T(8,128)(2,1)S(1)} %collective-permute-done.12.p2, ...), custom_call_target="tpu_custom_call" | custom-call | flops 100 | bytes 100 | tf_op jit(solution)/shard_map/gather/pallas_call | solution.py:242
  33.0 2.5 %collective-permute-start.14 = (bf16[2,128,128]{2,1,0:T(8,128)(2,1)S(1)}, bf16[2,128,128]{2,1,0:T(8,128)(2,1)S(1)}, u32[]{:S(2)}, u32[]{:S(2)}) collective-permute-start(bf16[2,128,128]{2,1,0:T(8,128)(2,1)S(1)} %get-tuple-element.106), channel_id=1, source_target_pairs={{0,8},{1,9},{2,10},{3,11},{4,12},{5,13},{6,14},{7,15},{8,0},{9,1},... | collective-permute-start | bytes 196616 | tf_op jit(solution)/shard_map/ppermute | solution.py:511
  35.8 1.2 %gather.2 = (bf16[4,264,256]{2,1,0:T(8,128)(2,1)S(1)}, bf16[2,128,128]{2,1,0:T(8,128)(2,1)S(1)}) custom-call(s32[4]{0:T(128)S(1)} %pad_add_fusion.sc_ref, bf16[264,256]{1,0:T(8,128)(2,1)S(1)} %get-tuple-element.87.p0, bf16[264,256]{1,0:T(8,128)(2,1)S(1)} %collective-permute-done.2.p1, bf16[264,256]{1,0:T(8,128)(2,1)S(1)} %collective-permute-done.3.p2, ...), custom_call_target="tpu_custom_call" | custom-call | flops 100 | bytes 100 | tf_op jit(solution)/shard_map/gather/pallas_call | solution.py:242
  37.0 2.9 %collective-permute-start.5 = (bf16[2,128,128]{2,1,0:T(8,128)(2,1)S(1)}, bf16[2,128,128]{2,1,0:T(8,128)(2,1)S(1)}, u32[]{:S(2)}, u32[]{:S(2)}) collective-permute-start(bf16[2,128,128]{2,1,0:T(8,128)(2,1)S(1)} %get-tuple-element.92), channel_id=1, source_target_pairs={{0,8},{1,9},{2,10},{3,11},{4,12},{5,13},{6,14},{7,15},{8,0},{9,1},... | collective-permute-start | bytes 196616 | tf_op jit(solution)/shard_map/ppermute | solution.py:511
  39.9 1.0 %spread.3 = (bf16[2,128,128]{2,1,0:T(8,128)(2,1)S(1)}, bf16[2,128,128]{2,1,0:T(8,128)(2,1)S(1)}, bf16[2,128,128]{2,1,0:T(8,128)(2,1)S(1)}, bf16[2,128,128]{2,1,0:T(8,128)(2,1)S(1)}) custom-call(s32[4]{0:T(128)S(1)} %pad_add_fusion.sc_ref, bf16[4,264,256]{2,1,0:T(8,128)(2,1)S(1)} %get-tuple-element.105.order_ref, ...), custom_call_target="tpu_custom_call" | custom-call | flops 100 | bytes 100 | tf_op jit(solution)/shard_map/spread/pallas_call | solution.py:242
  40.9 1.0 %collective-permute-start.15 = (bf16[2,128,128]{2,1,0:T(8,128)(2,1)S(1)}, bf16[2,128,128]{2,1,0:T(8,128)(2,1)S(1)}, u32[]{:S(2)}, u32[]{:S(2)}) collective-permute-start(bf16[2,128,128]{2,1,0:T(8,128)(2,1)S(1)} %get-tuple-element.108), channel_id=1, source_target_pairs={{0,2},{1,3},{2,0},{3,1},{4,6},{5,7},{6,4},{7,5},{8,10},{9,11},{10,... | collective-permute-start | bytes 196616 | tf_op jit(solution)/shard_map/ppermute | solution.py:511
  41.9 0.8 %collective-permute-start.16 = (bf16[2,128,128]{2,1,0:T(8,128)(2,1)S(1)}, bf16[2,128,128]{2,1,0:T(8,128)(2,1)S(1)}, u32[]{:S(2)}, u32[]{:S(2)}) collective-permute-start(bf16[2,128,128]{2,1,0:T(8,128)(2,1)S(1)} %get-tuple-element.109), channel_id=1, source_target_pairs={{0,4},{1,5},{2,6},{3,7},{4,0},{5,1},{6,2},{7,3},{8,12},{9,13},{10,... | collective-permute-start | bytes 196616 | tf_op jit(solution)/shard_map/ppermute | solution.py:511
  42.7 1.8 %collective-permute-start.17 = (bf16[2,128,128]{2,1,0:T(8,128)(2,1)S(1)}, bf16[2,128,128]{2,1,0:T(8,128)(2,1)S(1)}, u32[]{:S(2)}, u32[]{:S(2)}) collective-permute-start(bf16[2,128,128]{2,1,0:T(8,128)(2,1)S(1)} %get-tuple-element.110), channel_id=1, source_target_pairs={{0,6},{1,7},{2,4},{3,5},{4,2},{5,3},{6,0},{7,1},{8,14},{9,15},{10,... | collective-permute-start | bytes 196616 | tf_op jit(solution)/shard_map/ppermute | solution.py:511
  44.5 1.0 %spread.2 = (bf16[2,128,128]{2,1,0:T(8,128)(2,1)S(1)}, bf16[2,128,128]{2,1,0:T(8,128)(2,1)S(1)}, bf16[2,128,128]{2,1,0:T(8,128)(2,1)S(1)}, bf16[2,128,128]{2,1,0:T(8,128)(2,1)S(1)}) custom-call(s32[4]{0:T(128)S(1)} %pad_add_fusion.sc_ref, bf16[4,264,256]{2,1,0:T(8,128)(2,1)S(1)} %get-tuple-element.91.order_ref, ...), custom_call_target="tpu_custom_call" | custom-call | flops 100 | bytes 100 | tf_op jit(solution)/shard_map/spread/pallas_call | solution.py:242
  45.5 1.0 %collective-permute-start.6 = (bf16[2,128,128]{2,1,0:T(8,128)(2,1)S(1)}, bf16[2,128,128]{2,1,0:T(8,128)(2,1)S(1)}, u32[]{:S(2)}, u32[]{:S(2)}) collective-permute-start(bf16[2,128,128]{2,1,0:T(8,128)(2,1)S(1)} %get-tuple-element.94), channel_id=1, source_target_pairs={{0,2},{1,3},{2,0},{3,1},{4,6},{5,7},{6,4},{7,5},{8,10},{9,11},{10,... | collective-permute-start | bytes 196616 | tf_op jit(solution)/shard_map/ppermute | solution.py:511
  46.5 0.8 %collective-permute-start.7 = (bf16[2,128,128]{2,1,0:T(8,128)(2,1)S(1)}, bf16[2,128,128]{2,1,0:T(8,128)(2,1)S(1)}, u32[]{:S(2)}, u32[]{:S(2)}) collective-permute-start(bf16[2,128,128]{2,1,0:T(8,128)(2,1)S(1)} %get-tuple-element.95), channel_id=1, source_target_pairs={{0,4},{1,5},{2,6},{3,7},{4,0},{5,1},{6,2},{7,3},{8,12},{9,13},{10,... | collective-permute-start | bytes 196616 | tf_op jit(solution)/shard_map/ppermute | solution.py:511
  47.3 1.8 %collective-permute-start.8 = (bf16[2,128,128]{2,1,0:T(8,128)(2,1)S(1)}, bf16[2,128,128]{2,1,0:T(8,128)(2,1)S(1)}, u32[]{:S(2)}, u32[]{:S(2)}) collective-permute-start(bf16[2,128,128]{2,1,0:T(8,128)(2,1)S(1)} %get-tuple-element.96), channel_id=1, source_target_pairs={{0,6},{1,7},{2,4},{3,5},{4,2},{5,3},{6,0},{7,1},{8,14},{9,15},{10,... | collective-permute-start | bytes 196616 | tf_op jit(solution)/shard_map/ppermute | solution.py:511
  49.7 0.8 %enter.3 = (bf16[4,2,128,128]{3,2,1,0:T(8,128)(2,1)S(1)}, bf16[4,2,128,128]{3,2,1,0:T(8,128)(2,1)S(1)}) custom-call(s32[4]{0:T(128)S(1)} %pad_add_fusion.sc_ref, bf16[4,264,256]{2,1,0:T(8,128)(2,1)S(1)} %get-tuple-element.100.first_ref, bf16[2,128,128]{2,1,0:T(8,128)(2,1)S(1)} %get-tuple-element.107.refs_0_, ...), custom_call_target="tpu_custom_call" | custom-call | flops 100 | bytes 100 | tf_op jit(solution)/shard_map/enter/pallas_call | solution.py:242
  50.8 1.7 %collective-permute-done.8.refs_3_ = bf16[2,128,128]{2,1,0:T(8,128)(2,1)S(1)} collective-permute-done((bf16[2,128,128]{2,1,0:T(8,128)(2,1)S(1)}, bf16[2,128,128]{2,1,0:T(8,128)(2,1)S(1)}, u32[]{:S(2)}, u32[]{:S(2)}) %collective-permute-start.8) | collective-permute-done | bytes 65568 | tf_op jit(solution)/shard_map/ppermute | solution.py:511
  52.5 0.8 %enter.2 = (bf16[4,2,128,128]{3,2,1,0:T(8,128)(2,1)S(1)}, bf16[4,2,128,128]{3,2,1,0:T(8,128)(2,1)S(1)}) custom-call(s32[4]{0:T(128)S(1)} %pad_add_fusion.sc_ref, bf16[4,264,256]{2,1,0:T(8,128)(2,1)S(1)} %get-tuple-element.86.first_ref, bf16[2,128,128]{2,1,0:T(8,128)(2,1)S(1)} %get-tuple-element.93.refs_0_, ...), custom_call_target="tpu_custom_call" | custom-call | flops 100 | bytes 100 | tf_op jit(solution)/shard_map/enter/pallas_call | solution.py:242
  53.4 1.3 %finish.1 = (bf16[4,128,256]{2,1,0:T(8,128)(2,1)S(1)}, bf16[4,128,256]{2,1,0:T(8,128)(2,1)S(1)}, bf16[4,128,256]{2,1,0:T(8,128)(2,1)S(1)}) custom-call(s32[4]{0:T(128)S(1)} %pad_add_fusion.sc_ref, f32[128,4096]{1,0:T(8,128)S(1)} %gates.1.gate_ref, bf16[4,2,128,128]{3,2,1,0:T(8,128)(2,1)S(1)} %get-tuple-element.111.refs_0_, ...), custom_call_target="tpu_custom_call" | custom-call | flops 100 | bytes 100 | tf_op jit(solution)/shard_map/finish/pallas_call | solution.py:242
  54.9 1.7 %finish_last.1 = bf16[128,4096]{1,0:T(8,128)(2,1)} custom-call(s32[4]{0:T(128)S(1)} %pad_add_fusion.sc_ref, f32[128,4096]{1,0:T(8,128)S(1)} %gates.1.gate_ref, bf16[4,2,128,128]{3,2,1,0:T(8,128)(2,1)S(1)} %collective-permute-done.9.state_ref, f32[4,2,128,128]{3,2,1,0:T(8,128)S(1)} %get-tuple-element.78.loc_ref, ...), custom_call_target="tpu_custom_call" | custom-call | flops 100 | bytes 100 | tf_op jit(solution)/shard_map/finish_last/pallas_call | solution.py:490
  (34 shorter events, 1.6 us)
Async XLA Ops:
  0.0 6.4 %copy-start.1 = (bf16[7,128,128]{2,1,0:T(8,128)(2,1)S(1)}, bf16[7,128,128]{2,1,0:T(8,128)(2,1)}, u32[]{:S(2)}) copy-start(bf16[7,128,128]{2,1,0:T(8,128)(2,1)} %constant.54.clone.masks_ref) | copy-start | bytes 688132
  0.0 4.2 %copy-start.2 = (f32[128,32]{0,1:T(8,128)S(1)}, f32[128,32]{0,1:T(8,128)}, u32[]{:S(2)}) copy-start(f32[128,32]{0,1:T(8,128)} %param.10) | copy-start | bytes 49156
  0.0 4.2 %copy-start.3 = (bf16[128,32]{0,1:T(8,128)(2,1)S(1)}, bf16[128,32]{0,1:T(8,128)(2,1)}, u32[]{:S(2)}) copy-start(bf16[128,32]{0,1:T(8,128)(2,1)} %param.9) | copy-start | bytes 24580
  1.7 4.7 %collective-permute-start = (bf16[4,8192]{1,0:T(4,128)(2,1)S(1)}, bf16[4,8192]{1,0:T(4,128)(2,1)S(1)}, u32[]{:S(2)}, u32[]{:S(2)}) collective-permute-start(bf16[4,8192]{1,0:T(4,128)(2,1)S(1)} %get-tuple-element.62), channel_id=1, source_target_pairs={{0,1},{1,2},{2,3},{3,4},{4,5},{5,6},{6,7},{7,8},{8,9},{9,10},{10,1... | collective-permute-start | bytes 196616 | tf_op jit(solution)/shard_map/ppermute | solution.py:507
  11.0 7.4 %collective-permute-start.10 = (bf16[4,264,256]{2,1,0:T(8,128)(2,1)S(1)}, bf16[4,264,256]{2,1,0:T(8,128)(2,1)S(1)}, u32[]{:S(2)}, u32[]{:S(2)}) collective-permute-start(bf16[4,264,256]{2,1,0:T(8,128)(2,1)S(1)} %get-tuple-element.99), channel_id=1, source_target_pairs={{0,1},{1,0},{2,3},{3,2},{4,5},{5,4},{6,7},{7,6},{8,9},{9,8},{10,11... | collective-permute-start | bytes 1622024 | tf_op jit(solution)/shard_map/ppermute | solution.py:511
  18.4 5.2 %collective-permute-start.1 = (bf16[4,264,256]{2,1,0:T(8,128)(2,1)S(1)}, bf16[4,264,256]{2,1,0:T(8,128)(2,1)S(1)}, u32[]{:S(2)}, u32[]{:S(2)}) collective-permute-start(bf16[4,264,256]{2,1,0:T(8,128)(2,1)S(1)} %get-tuple-element.85), channel_id=1, source_target_pairs={{0,1},{1,0},{2,3},{3,2},{4,5},{5,4},{6,7},{7,6},{8,9},{9,8},{10,11... | collective-permute-start | bytes 1622024 | tf_op jit(solution)/shard_map/ppermute | solution.py:511
  19.4 8.0 %collective-permute-start.11 = (bf16[264,256]{1,0:T(8,128)(2,1)S(1)}, bf16[264,256]{1,0:T(8,128)(2,1)S(1)}, u32[]{:S(2)}, u32[]{:S(2)}) collective-permute-start(bf16[264,256]{1,0:T(8,128)(2,1)S(1)} %get-tuple-element.102), channel_id=1, source_target_pairs={{0,2},{1,3},{2,0},{3,1},{4,6},{5,7},{6,4},{7,5},{8,10},{9,11},{10,... | collective-permute-start | bytes 405512 | tf_op jit(solution)/shard_map/ppermute | solution.py:511
  21.2 10.7 %collective-permute-start.12 = (bf16[264,256]{1,0:T(8,128)(2,1)S(1)}, bf16[264,256]{1,0:T(8,128)(2,1)S(1)}, u32[]{:S(2)}, u32[]{:S(2)}) collective-permute-start(bf16[264,256]{1,0:T(8,128)(2,1)S(1)} %get-tuple-element.103), channel_id=1, source_target_pairs={{0,4},{1,5},{2,6},{3,7},{4,0},{5,1},{6,2},{7,3},{8,12},{9,13},{10,... | collective-permute-start | bytes 405512 | tf_op jit(solution)/shard_map/ppermute | solution.py:511
  22.7 9.1 %collective-permute-start.13 = (bf16[264,256]{1,0:T(8,128)(2,1)S(1)}, bf16[264,256]{1,0:T(8,128)(2,1)S(1)}, u32[]{:S(2)}, u32[]{:S(2)}) collective-permute-start(bf16[264,256]{1,0:T(8,128)(2,1)S(1)} %get-tuple-element.104), channel_id=1, source_target_pairs={{0,6},{1,7},{2,4},{3,5},{4,2},{5,3},{6,0},{7,1},{8,14},{9,15},{10,... | collective-permute-start | bytes 405512 | tf_op jit(solution)/shard_map/ppermute | solution.py:511
  24.7 10.9 %collective-permute-start.2 = (bf16[264,256]{1,0:T(8,128)(2,1)S(1)}, bf16[264,256]{1,0:T(8,128)(2,1)S(1)}, u32[]{:S(2)}, u32[]{:S(2)}) collective-permute-start(bf16[264,256]{1,0:T(8,128)(2,1)S(1)} %get-tuple-element.88), channel_id=1, source_target_pairs={{0,2},{1,3},{2,0},{3,1},{4,6},{5,7},{6,4},{7,5},{8,10},{9,11},{10,... | collective-permute-start | bytes 405512 | tf_op jit(solution)/shard_map/ppermute | solution.py:511
  25.8 9.8 %collective-permute-start.3 = (bf16[264,256]{1,0:T(8,128)(2,1)S(1)}, bf16[264,256]{1,0:T(8,128)(2,1)S(1)}, u32[]{:S(2)}, u32[]{:S(2)}) collective-permute-start(bf16[264,256]{1,0:T(8,128)(2,1)S(1)} %get-tuple-element.89), channel_id=1, source_target_pairs={{0,4},{1,5},{2,6},{3,7},{4,0},{5,1},{6,2},{7,3},{8,12},{9,13},{10,... | collective-permute-start | bytes 405512 | tf_op jit(solution)/shard_map/ppermute | solution.py:511
  27.4 8.4 %collective-permute-start.4 = (bf16[264,256]{1,0:T(8,128)(2,1)S(1)}, bf16[264,256]{1,0:T(8,128)(2,1)S(1)}, u32[]{:S(2)}, u32[]{:S(2)}) collective-permute-start(bf16[264,256]{1,0:T(8,128)(2,1)S(1)} %get-tuple-element.90), channel_id=1, source_target_pairs={{0,6},{1,7},{2,4},{3,5},{4,2},{5,3},{6,0},{7,1},{8,14},{9,15},{10,... | collective-permute-start | bytes 405512 | tf_op jit(solution)/shard_map/ppermute | solution.py:511
  31.8 17.3 %copy-start = (bf16[128,4096]{1,0:T(8,128)(2,1)S(1)}, bf16[128,4096]{1,0:T(8,128)(2,1)}, u32[]{:S(2)}) copy-start(bf16[128,4096]{1,0:T(8,128)(2,1)} %gate_ref.1) | copy-start | bytes 3145732
  31.8 17.2 %copy-start.4 = (f32[128]{0:T(128)S(1)}, f32[128]{0:T(128)}, u32[]{:S(2)}) copy-start(f32[128]{0:T(128)} %param.12) | copy-start | bytes 1540
  33.0 6.8 %collective-permute-start.14 = (bf16[2,128,128]{2,1,0:T(8,128)(2,1)S(1)}, bf16[2,128,128]{2,1,0:T(8,128)(2,1)S(1)}, u32[]{:S(2)}, u32[]{:S(2)}) collective-permute-start(bf16[2,128,128]{2,1,0:T(8,128)(2,1)S(1)} %get-tuple-element.106), channel_id=1, source_target_pairs={{0,8},{1,9},{2,10},{3,11},{4,12},{5,13},{6,14},{7,15},{8,0},{9,1},... | collective-permute-start | bytes 196616 | tf_op jit(solution)/shard_map/ppermute | solution.py:511
  37.0 7.5 %collective-permute-start.5 = (bf16[2,128,128]{2,1,0:T(8,128)(2,1)S(1)}, bf16[2,128,128]{2,1,0:T(8,128)(2,1)S(1)}, u32[]{:S(2)}, u32[]{:S(2)}) collective-permute-start(bf16[2,128,128]{2,1,0:T(8,128)(2,1)S(1)} %get-tuple-element.92), channel_id=1, source_target_pairs={{0,8},{1,9},{2,10},{3,11},{4,12},{5,13},{6,14},{7,15},{8,0},{9,1},... | collective-permute-start | bytes 196616 | tf_op jit(solution)/shard_map/ppermute | solution.py:511
  40.9 6.4 %collective-permute-start.15 = (bf16[2,128,128]{2,1,0:T(8,128)(2,1)S(1)}, bf16[2,128,128]{2,1,0:T(8,128)(2,1)S(1)}, u32[]{:S(2)}, u32[]{:S(2)}) collective-permute-start(bf16[2,128,128]{2,1,0:T(8,128)(2,1)S(1)} %get-tuple-element.108), channel_id=1, source_target_pairs={{0,2},{1,3},{2,0},{3,1},{4,6},{5,7},{6,4},{7,5},{8,10},{9,11},{10,... | collective-permute-start | bytes 196616 | tf_op jit(solution)/shard_map/ppermute | solution.py:511
  41.9 7.7 %collective-permute-start.16 = (bf16[2,128,128]{2,1,0:T(8,128)(2,1)S(1)}, bf16[2,128,128]{2,1,0:T(8,128)(2,1)S(1)}, u32[]{:S(2)}, u32[]{:S(2)}) collective-permute-start(bf16[2,128,128]{2,1,0:T(8,128)(2,1)S(1)} %get-tuple-element.109), channel_id=1, source_target_pairs={{0,4},{1,5},{2,6},{3,7},{4,0},{5,1},{6,2},{7,3},{8,12},{9,13},{10,... | collective-permute-start | bytes 196616 | tf_op jit(solution)/shard_map/ppermute | solution.py:511
  42.7 7.0 %collective-permute-start.17 = (bf16[2,128,128]{2,1,0:T(8,128)(2,1)S(1)}, bf16[2,128,128]{2,1,0:T(8,128)(2,1)S(1)}, u32[]{:S(2)}, u32[]{:S(2)}) collective-permute-start(bf16[2,128,128]{2,1,0:T(8,128)(2,1)S(1)} %get-tuple-element.110), channel_id=1, source_target_pairs={{0,6},{1,7},{2,4},{3,5},{4,2},{5,3},{6,0},{7,1},{8,14},{9,15},{10,... | collective-permute-start | bytes 196616 | tf_op jit(solution)/shard_map/ppermute | solution.py:511
  45.5 5.1 %collective-permute-start.6 = (bf16[2,128,128]{2,1,0:T(8,128)(2,1)S(1)}, bf16[2,128,128]{2,1,0:T(8,128)(2,1)S(1)}, u32[]{:S(2)}, u32[]{:S(2)}) collective-permute-start(bf16[2,128,128]{2,1,0:T(8,128)(2,1)S(1)} %get-tuple-element.94), channel_id=1, source_target_pairs={{0,2},{1,3},{2,0},{3,1},{4,6},{5,7},{6,4},{7,5},{8,10},{9,11},{10,... | collective-permute-start | bytes 196616 | tf_op jit(solution)/shard_map/ppermute | solution.py:511
  46.5 4.3 %collective-permute-start.7 = (bf16[2,128,128]{2,1,0:T(8,128)(2,1)S(1)}, bf16[2,128,128]{2,1,0:T(8,128)(2,1)S(1)}, u32[]{:S(2)}, u32[]{:S(2)}) collective-permute-start(bf16[2,128,128]{2,1,0:T(8,128)(2,1)S(1)} %get-tuple-element.95), channel_id=1, source_target_pairs={{0,4},{1,5},{2,6},{3,7},{4,0},{5,1},{6,2},{7,3},{8,12},{9,13},{10,... | collective-permute-start | bytes 196616 | tf_op jit(solution)/shard_map/ppermute | solution.py:511
  47.3 5.2 %collective-permute-start.8 = (bf16[2,128,128]{2,1,0:T(8,128)(2,1)S(1)}, bf16[2,128,128]{2,1,0:T(8,128)(2,1)S(1)}, u32[]{:S(2)}, u32[]{:S(2)}) collective-permute-start(bf16[2,128,128]{2,1,0:T(8,128)(2,1)S(1)} %get-tuple-element.96), channel_id=1, source_target_pairs={{0,6},{1,7},{2,4},{3,5},{4,2},{5,3},{6,0},{7,1},{8,14},{9,15},{10,... | collective-permute-start | bytes 196616 | tf_op jit(solution)/shard_map/ppermute | solution.py:511
  50.5 2.9 %collective-permute-start.18 = (bf16[4,2,128,128]{3,2,1,0:T(8,128)(2,1)S(1)}, bf16[4,2,128,128]{3,2,1,0:T(8,128)(2,1)S(1)}, u32[]{:S(2)}, u32[]{:S(2)}) collective-permute-start(bf16[4,2,128,128]{3,2,1,0:T(8,128)(2,1)S(1)} %get-tuple-element.112), channel_id=1, source_target_pairs={{0,1},{1,0},{2,3},{3,2},{4,5},{5,4},{6,7},{7,6},{8,9},{9,8},{10,11... | collective-permute-start | bytes 786440 | tf_op jit(solution)/shard_map/ppermute | solution.py:511
  53.3 1.6 %collective-permute-start.9 = (bf16[4,2,128,128]{3,2,1,0:T(8,128)(2,1)S(1)}, bf16[4,2,128,128]{3,2,1,0:T(8,128)(2,1)S(1)}, u32[]{:S(2)}, u32[]{:S(2)}) collective-permute-start(bf16[4,2,128,128]{3,2,1,0:T(8,128)(2,1)S(1)} %get-tuple-element.97), channel_id=1, source_target_pairs={{0,1},{1,0},{2,3},{3,2},{4,5},{5,4},{6,7},{7,6},{8,9},{9,8},{10,11... | collective-permute-start | bytes 786440 | tf_op jit(solution)/shard_map/ppermute | solution.py:511

commit v8 on v7

--- a/solution.py
+++ b/solution.py
@@ -556,7 +556,7 @@
         for _ in range(max(lax.axis_size("seq") // (2 * CHIPS) - 1, 1)):
             order, leaving = local_call(
                 functools.partial(gather_kernel, keys),
-                [turn, *pieces, entering],
+                [place if keys == BANDS[0] else turn, *pieces, entering],
                 [order_shape, state_shape],
                 name="gather",
             )

time: 56.9 us -> 58.2 us (1.023)
  waiting for transfers between devices: 2.38 us -> 5.98 us
  starting transfers between devices: 25.6 us -> 23.2 us
    ppermute x18, waiting for transfers between devices: 2.38 us -> 5.98 us  [swap(): lax.ppermute(block, 'seq', [(i, i ^ distance) for i in range(lax.axis_siz...]
    ppermute x18, starting transfers between devices: 23.2 us -> 20.9 us  [swap(): lax.ppermute(block, 'seq', [(i, i ^ distance) for i in range(lax.axis_siz...]
  transfers between devices with their start and end apart: 19 -> 19, of which waited for: 4 -> 4; matrix products, arithmetic and copies ran while one was open for 0% -> 0% of each run, Pallas kernels for 36% -> 35%
where the time goes in v8:
time: 58.2 us; the launch traced here: 58 us
  Pallas kernels  28.2 us (48%)
  starting transfers between devices  23.2 us (40%)
  waiting for transfers between devices  5.98 us (10%)
    pallas_call x14, Pallas kernels, local_call(): pl.pallas_call(kernel, out_shape=out_shape, in_specs=in_specs, out_specs=...  24.8 us
    ppermute x18, starting transfers between devices, swap(): lax.ppermute(block, 'seq', [(i, i ^ distance) for i in range(lax.axis_siz...  20.9 us
    ppermute x18, waiting for transfers between devices, swap(): lax.ppermute(block, 'seq', [(i, i ^ distance) for i in range(lax.axis_siz...  5.98 us
    ppermute x1, starting transfers between devices, shift(): lax.ppermute(block, 'seq', [(i, i + distance) for i in range(count - dist...  2.37 us
    pallas_call x1, Pallas kernels, finish_last(): pl.pallas_call(functools.partial(last_kernel, earlier, keys, own), out_sh...  1.7 us
    pallas_call x1, Pallas kernels, load(): pl.pallas_call(load_kernel, out_shape=[jax.ShapeDtypeStruct(mixed_qkv.sha...  1.68 us
  transfers between devices with their start and end apart: 19, of which 4 were waited for; matrix products, arithmetic and copies ran while one was open for 0% of the time, Pallas kernels for 35%

profile of v8, /device:TPU:0, one launch (start us, length us, event | category | flops | bytes accessed | tf_op | source)
XLA Modules:
  0.0 58.0 jit_solution(3528192005890647924)
XLA Ops:
  0.0 1.7 %load.1 = (bf16[128,8192]{1,0:T(8,128)(2,1)S(1)}, bf16[4,8192]{1,0:T(4,128)(2,1)S(1)}, bf16[4,8192]{1,0:T(4,128)(2,1)S(1)}) custom-call(bf16[128,8192]{1,0:T(8,128)(2,1)} %x_ref.1, bf16[4,8192]{1,0:T(4,128)(2,1)} %w_ref.1), custom_call_target="tpu_custom_call" | custom-call | flops 100 | bytes 100 | tf_op jit(solution)/shard_map/load/pallas_call | solution.py:92
  1.7 2.4 %collective-permute-start = (bf16[4,8192]{1,0:T(4,128)(2,1)S(1)}, bf16[4,8192]{1,0:T(4,128)(2,1)S(1)}, u32[]{:S(2)}, u32[]{:S(2)}) collective-permute-start(bf16[4,8192]{1,0:T(4,128)(2,1)S(1)} %get-tuple-element.62), channel_id=1, source_target_pairs={{0,1},{1,2},{2,3},{3,4},{4,5},{5,6},{6,7},{7,8},{8,9},{9,10},{10,1... | collective-permute-start | bytes 196616 | tf_op jit(solution)/shard_map/ppermute | solution.py:507
  4.2 2.2 %conv.1 = (bf16[128,8192]{1,0:T(8,128)(2,1)S(1)}, f32[8,8,128]{2,1,0:T(8,128)S(1)}) custom-call(s32[4]{0:T(128)S(1)} %pad_add_fusion.sc_ref, bf16[128,8192]{1,0:T(8,128)(2,1)S(1)} %get-tuple-element.61.x_ref, bf16[4,8192]{1,0:T(4,128)(2,1)S(1)} %get-tuple-element.63.w_ref, f32[32,128]{1,0:T(8,128)S(1)} %bitcast.7, bf16[32,128]{1,0:T(8,128)(2,1)S(1)} %bitcast.8), custom_call_target="tpu_custom_call" | custom-call | flops 100 | bytes 100 | tf_op jit(solution)/shard_map/conv/pallas_call | solution.py:242
  6.4 4.6 %terms.2 = (bf16[4,264,256]{2,1,0:T(8,128)(2,1)S(1)}, bf16[4,2,128,256]{3,2,1,0:T(8,128)(2,1)S(1)}, bf16[4,1,128,128]{3,2,1,0:T(8,128)(2,1)S(1)}, bf16[4,264,256...) custom-call(s32[4]{0:T(128)S(1)} %pad_add_fusion.sc_ref, ...), custom_call_target="tpu_custom_call" | custom-call | flops 100 | bytes 100 | tf_op jit(solution)/shard_map/terms/pallas_call | solution.py:242
  11.0 2.7 %collective-permute-start.10 = (bf16[4,264,256]{2,1,0:T(8,128)(2,1)S(1)}, bf16[4,264,256]{2,1,0:T(8,128)(2,1)S(1)}, u32[]{:S(2)}, u32[]{:S(2)}) collective-permute-start(bf16[4,264,256]{2,1,0:T(8,128)(2,1)S(1)} %get-tuple-element.99), channel_id=1, source_target_pairs={{0,1},{1,0},{2,3},{3,2},{4,5},{5,4},{6,7},{7,6},{8,9},{9,8},{10,11... | collective-permute-start | bytes 1622024 | tf_op jit(solution)/shard_map/ppermute | solution.py:511
  13.7 4.6 %terms.3 = (bf16[4,264,256]{2,1,0:T(8,128)(2,1)S(1)}, bf16[4,2,128,256]{3,2,1,0:T(8,128)(2,1)S(1)}, bf16[4,1,128,128]{3,2,1,0:T(8,128)(2,1)S(1)}, bf16[4,264,256...) custom-call(s32[4]{0:T(128)S(1)} %pad_add_fusion.sc_ref, ...), custom_call_target="tpu_custom_call" | custom-call | flops 100 | bytes 100 | tf_op jit(solution)/shard_map/terms/pallas_call | solution.py:242
  18.4 0.9 %compose.3 = (bf16[4,264,256]{2,1,0:T(8,128)(2,1)S(1)}, bf16[264,256]{1,0:T(8,128)(2,1)S(1)}, bf16[264,256]{1,0:T(8,128)(2,1)S(1)}, bf16[264,256]{1,0:T(8,128)(2,1)S(1)}, bf16[264,256]{1,0:T(8,128)(2,1)S(1)}) custom-call(s32[4]{0:T(128)S(1)} %pad_add_fusion.sc_ref, bf16[4,264,256]{2,1,0:T(8,128)(2,1)S(1)} %get-tuple-element.98.mine_ref, ...), custom_call_target="tpu_custom_call" | custom-call | flops 100 | bytes 100 | tf_op jit(solution)/shard_map/compose/pallas_call | solution.py:242
  19.4 1.8 %collective-permute-start.11 = (bf16[264,256]{1,0:T(8,128)(2,1)S(1)}, bf16[264,256]{1,0:T(8,128)(2,1)S(1)}, u32[]{:S(2)}, u32[]{:S(2)}) collective-permute-start(bf16[264,256]{1,0:T(8,128)(2,1)S(1)} %get-tuple-element.102), channel_id=1, source_target_pairs={{0,2},{1,3},{2,0},{3,1},{4,6},{5,7},{6,4},{7,5},{8,10},{9,11},{10,... | collective-permute-start | bytes 405512 | tf_op jit(solution)/shard_map/ppermute | solution.py:511
  21.2 1.6 %collective-permute-start.12 = (bf16[264,256]{1,0:T(8,128)(2,1)S(1)}, bf16[264,256]{1,0:T(8,128)(2,1)S(1)}, u32[]{:S(2)}, u32[]{:S(2)}) collective-permute-start(bf16[264,256]{1,0:T(8,128)(2,1)S(1)} %get-tuple-element.103), channel_id=1, source_target_pairs={{0,4},{1,5},{2,6},{3,7},{4,0},{5,1},{6,2},{7,3},{8,12},{9,13},{10,... | collective-permute-start | bytes 405512 | tf_op jit(solution)/shard_map/ppermute | solution.py:511
  22.7 0.8 %collective-permute-start.13 = (bf16[264,256]{1,0:T(8,128)(2,1)S(1)}, bf16[264,256]{1,0:T(8,128)(2,1)S(1)}, u32[]{:S(2)}, u32[]{:S(2)}) collective-permute-start(bf16[264,256]{1,0:T(8,128)(2,1)S(1)} %get-tuple-element.104), channel_id=1, source_target_pairs={{0,6},{1,7},{2,4},{3,5},{4,2},{5,3},{6,0},{7,1},{8,14},{9,15},{10,... | collective-permute-start | bytes 405512 | tf_op jit(solution)/shard_map/ppermute | solution.py:511
  23.6 1.1 %compose.2 = (bf16[4,264,256]{2,1,0:T(8,128)(2,1)S(1)}, bf16[264,256]{1,0:T(8,128)(2,1)S(1)}, bf16[264,256]{1,0:T(8,128)(2,1)S(1)}, bf16[264,256]{1,0:T(8,128)(2,1)S(1)}, bf16[264,256]{1,0:T(8,128)(2,1)S(1)}) custom-call(s32[4]{0:T(128)S(1)} %pad_add_fusion.sc_ref, bf16[4,264,256]{2,1,0:T(8,128)(2,1)S(1)} %get-tuple-element.84.mine_ref, ...), custom_call_target="tpu_custom_call" | custom-call | flops 100 | bytes 100 | tf_op jit(solution)/shard_map/compose/pallas_call | solution.py:242
  24.7 1.1 %collective-permute-start.2 = (bf16[264,256]{1,0:T(8,128)(2,1)S(1)}, bf16[264,256]{1,0:T(8,128)(2,1)S(1)}, u32[]{:S(2)}, u32[]{:S(2)}) collective-permute-start(bf16[264,256]{1,0:T(8,128)(2,1)S(1)} %get-tuple-element.88), channel_id=1, source_target_pairs={{0,2},{1,3},{2,0},{3,1},{4,6},{5,7},{6,4},{7,5},{8,10},{9,11},{10,... | collective-permute-start | bytes 405512 | tf_op jit(solution)/shard_map/ppermute | solution.py:511
  25.8 1.6 %collective-permute-start.3 = (bf16[264,256]{1,0:T(8,128)(2,1)S(1)}, bf16[264,256]{1,0:T(8,128)(2,1)S(1)}, u32[]{:S(2)}, u32[]{:S(2)}) collective-permute-start(bf16[264,256]{1,0:T(8,128)(2,1)S(1)} %get-tuple-element.89), channel_id=1, source_target_pairs={{0,4},{1,5},{2,6},{3,7},{4,0},{5,1},{6,2},{7,3},{8,12},{9,13},{10,... | collective-permute-start | bytes 405512 | tf_op jit(solution)/shard_map/ppermute | solution.py:511
  27.4 0.8 %collective-permute-start.4 = (bf16[264,256]{1,0:T(8,128)(2,1)S(1)}, bf16[264,256]{1,0:T(8,128)(2,1)S(1)}, u32[]{:S(2)}, u32[]{:S(2)}) collective-permute-start(bf16[264,256]{1,0:T(8,128)(2,1)S(1)} %get-tuple-element.90), channel_id=1, source_target_pairs={{0,6},{1,7},{2,4},{3,5},{4,2},{5,3},{6,0},{7,1},{8,14},{9,15},{10,... | collective-permute-start | bytes 405512 | tf_op jit(solution)/shard_map/ppermute | solution.py:511
  28.2 2.7 %collective-permute-done.13.p3 = bf16[264,256]{1,0:T(8,128)(2,1)S(1)} collective-permute-done((bf16[264,256]{1,0:T(8,128)(2,1)S(1)}, bf16[264,256]{1,0:T(8,128)(2,1)S(1)}, u32[]{:S(2)}, u32[]{:S(2)}) %collective-permute-start.13) | collective-permute-done | bytes 135200 | tf_op jit(solution)/shard_map/ppermute | solution.py:511
  30.9 1.2 %gather.3 = (bf16[4,264,256]{2,1,0:T(8,128)(2,1)S(1)}, bf16[2,128,128]{2,1,0:T(8,128)(2,1)S(1)}) custom-call(s32[4]{0:T(128)S(1)} %pad_add_fusion.sc_ref, bf16[264,256]{1,0:T(8,128)(2,1)S(1)} %get-tuple-element.101.p0, bf16[264,256]{1,0:T(8,128)(2,1)S(1)} %collective-permute-done.11.p1, bf16[264,256]{1,0:T(8,128)(2,1)S(1)} %collective-permute-done.12.p2, ...), custom_call_target="tpu_custom_call" | custom-call | flops 100 | bytes 100 | tf_op jit(solution)/shard_map/gather/pallas_call | solution.py:242
  32.1 2.5 %collective-permute-start.14 = (bf16[2,128,128]{2,1,0:T(8,128)(2,1)S(1)}, bf16[2,128,128]{2,1,0:T(8,128)(2,1)S(1)}, u32[]{:S(2)}, u32[]{:S(2)}) collective-permute-start(bf16[2,128,128]{2,1,0:T(8,128)(2,1)S(1)} %get-tuple-element.106), channel_id=1, source_target_pairs={{0,8},{1,9},{2,10},{3,11},{4,12},{5,13},{6,14},{7,15},{8,0},{9,1},... | collective-permute-start | bytes 196616 | tf_op jit(solution)/shard_map/ppermute | solution.py:511
  34.6 3.6 %queries.1 = (f32[4,2,128,128]{3,2,1,0:T(8,128)S(1)}, bf16[4,2,128,128]{3,2,1,0:T(8,128)(2,1)S(1)}, f32[4,2,128,128]{3,2,1,0:T(8,128)S(1)}, bf16[4,2,128,128]{3,...) custom-call(s32[4]{0:T(128)S(1)} %pad_add_fusion.sc_ref, ...), custom_call_target="tpu_custom_call" | custom-call | flops 100 | bytes 100 | tf_op jit(solution)/shard_map/queries/pallas_call | solution.py:242
  38.3 1.2 %gather.2 = (bf16[4,264,256]{2,1,0:T(8,128)(2,1)S(1)}, bf16[2,128,128]{2,1,0:T(8,128)(2,1)S(1)}) custom-call(s32[4]{0:T(128)S(1)} %pad_add_fusion.sc_ref, bf16[264,256]{1,0:T(8,128)(2,1)S(1)} %get-tuple-element.87.p0, bf16[264,256]{1,0:T(8,128)(2,1)S(1)} %collective-permute-done.2.p1, bf16[264,256]{1,0:T(8,128)(2,1)S(1)} %collective-permute-done.3.p2, ...), custom_call_target="tpu_custom_call" | custom-call | flops 100 | bytes 100 | tf_op jit(solution)/shard_map/gather/pallas_call | solution.py:242
  39.9 1.0 %spread.3 = (bf16[2,128,128]{2,1,0:T(8,128)(2,1)S(1)}, bf16[2,128,128]{2,1,0:T(8,128)(2,1)S(1)}, bf16[2,128,128]{2,1,0:T(8,128)(2,1)S(1)}, bf16[2,128,128]{2,1,0:T(8,128)(2,1)S(1)}) custom-call(s32[4]{0:T(128)S(1)} %pad_add_fusion.sc_ref, bf16[4,264,256]{2,1,0:T(8,128)(2,1)S(1)} %get-tuple-element.105.order_ref, ...), custom_call_target="tpu_custom_call" | custom-call | flops 100 | bytes 100 | tf_op jit(solution)/shard_map/spread/pallas_call | solution.py:242
  40.9 1.0 %collective-permute-start.15 = (bf16[2,128,128]{2,1,0:T(8,128)(2,1)S(1)}, bf16[2,128,128]{2,1,0:T(8,128)(2,1)S(1)}, u32[]{:S(2)}, u32[]{:S(2)}) collective-permute-start(bf16[2,128,128]{2,1,0:T(8,128)(2,1)S(1)} %get-tuple-element.108), channel_id=1, source_target_pairs={{0,2},{1,3},{2,0},{3,1},{4,6},{5,7},{6,4},{7,5},{8,10},{9,11},{10,... | collective-permute-start | bytes 196616 | tf_op jit(solution)/shard_map/ppermute | solution.py:511
  41.9 1.3 %collective-permute-start.16 = (bf16[2,128,128]{2,1,0:T(8,128)(2,1)S(1)}, bf16[2,128,128]{2,1,0:T(8,128)(2,1)S(1)}, u32[]{:S(2)}, u32[]{:S(2)}) collective-permute-start(bf16[2,128,128]{2,1,0:T(8,128)(2,1)S(1)} %get-tuple-element.109), channel_id=1, source_target_pairs={{0,4},{1,5},{2,6},{3,7},{4,0},{5,1},{6,2},{7,3},{8,12},{9,13},{10,... | collective-permute-start | bytes 196616 | tf_op jit(solution)/shard_map/ppermute | solution.py:511
  43.2 1.3 %collective-permute-start.17 = (bf16[2,128,128]{2,1,0:T(8,128)(2,1)S(1)}, bf16[2,128,128]{2,1,0:T(8,128)(2,1)S(1)}, u32[]{:S(2)}, u32[]{:S(2)}) collective-permute-start(bf16[2,128,128]{2,1,0:T(8,128)(2,1)S(1)} %get-tuple-element.110), channel_id=1, source_target_pairs={{0,6},{1,7},{2,4},{3,5},{4,2},{5,3},{6,0},{7,1},{8,14},{9,15},{10,... | collective-permute-start | bytes 196616 | tf_op jit(solution)/shard_map/ppermute | solution.py:511
  44.7 1.0 %spread.2 = (bf16[2,128,128]{2,1,0:T(8,128)(2,1)S(1)}, bf16[2,128,128]{2,1,0:T(8,128)(2,1)S(1)}, bf16[2,128,128]{2,1,0:T(8,128)(2,1)S(1)}, bf16[2,128,128]{2,1,0:T(8,128)(2,1)S(1)}) custom-call(s32[4]{0:T(128)S(1)} %pad_add_fusion.sc_ref, bf16[4,264,256]{2,1,0:T(8,128)(2,1)S(1)} %get-tuple-element.91.order_ref, ...), custom_call_target="tpu_custom_call" | custom-call | flops 100 | bytes 100 | tf_op jit(solution)/shard_map/spread/pallas_call | solution.py:242
  45.7 0.8 %collective-permute-start.6 = (bf16[2,128,128]{2,1,0:T(8,128)(2,1)S(1)}, bf16[2,128,128]{2,1,0:T(8,128)(2,1)S(1)}, u32[]{:S(2)}, u32[]{:S(2)}) collective-permute-start(bf16[2,128,128]{2,1,0:T(8,128)(2,1)S(1)} %get-tuple-element.94), channel_id=1, source_target_pairs={{0,2},{1,3},{2,0},{3,1},{4,6},{5,7},{6,4},{7,5},{8,10},{9,11},{10,... | collective-permute-start | bytes 196616 | tf_op jit(solution)/shard_map/ppermute | solution.py:511
  46.5 2.1 %collective-permute-start.7 = (bf16[2,128,128]{2,1,0:T(8,128)(2,1)S(1)}, bf16[2,128,128]{2,1,0:T(8,128)(2,1)S(1)}, u32[]{:S(2)}, u32[]{:S(2)}) collective-permute-start(bf16[2,128,128]{2,1,0:T(8,128)(2,1)S(1)} %get-tuple-element.95), channel_id=1, source_target_pairs={{0,4},{1,5},{2,6},{3,7},{4,0},{5,1},{6,2},{7,3},{8,12},{9,13},{10,... | collective-permute-start | bytes 196616 | tf_op jit(solution)/shard_map/ppermute | solution.py:511
  48.6 0.9 %collective-permute-start.8 = (bf16[2,128,128]{2,1,0:T(8,128)(2,1)S(1)}, bf16[2,128,128]{2,1,0:T(8,128)(2,1)S(1)}, u32[]{:S(2)}, u32[]{:S(2)}) collective-permute-start(bf16[2,128,128]{2,1,0:T(8,128)(2,1)S(1)} %get-tuple-element.96), channel_id=1, source_target_pairs={{0,6},{1,7},{2,4},{3,5},{4,2},{5,3},{6,0},{7,1},{8,14},{9,15},{10,... | collective-permute-start | bytes 196616 | tf_op jit(solution)/shard_map/ppermute | solution.py:511
  50.0 0.8 %enter.3 = (bf16[4,2,128,128]{3,2,1,0:T(8,128)(2,1)S(1)}, bf16[4,2,128,128]{3,2,1,0:T(8,128)(2,1)S(1)}) custom-call(s32[4]{0:T(128)S(1)} %pad_add_fusion.sc_ref, bf16[4,264,256]{2,1,0:T(8,128)(2,1)S(1)} %get-tuple-element.100.first_ref, bf16[2,128,128]{2,1,0:T(8,128)(2,1)S(1)} %get-tuple-element.107.refs_0_, ...), custom_call_target="tpu_custom_call" | custom-call | flops 100 | bytes 100 | tf_op jit(solution)/shard_map/enter/pallas_call | solution.py:242
  50.9 2.8 %collective-permute-done.8.refs_3_ = bf16[2,128,128]{2,1,0:T(8,128)(2,1)S(1)} collective-permute-done((bf16[2,128,128]{2,1,0:T(8,128)(2,1)S(1)}, bf16[2,128,128]{2,1,0:T(8,128)(2,1)S(1)}, u32[]{:S(2)}, u32[]{:S(2)}) %collective-permute-start.8) | collective-permute-done | bytes 65568 | tf_op jit(solution)/shard_map/ppermute | solution.py:511
  53.7 0.8 %enter.2 = (bf16[4,2,128,128]{3,2,1,0:T(8,128)(2,1)S(1)}, bf16[4,2,128,128]{3,2,1,0:T(8,128)(2,1)S(1)}) custom-call(s32[4]{0:T(128)S(1)} %pad_add_fusion.sc_ref, bf16[4,264,256]{2,1,0:T(8,128)(2,1)S(1)} %get-tuple-element.86.first_ref, bf16[2,128,128]{2,1,0:T(8,128)(2,1)S(1)} %get-tuple-element.93.refs_0_, ...), custom_call_target="tpu_custom_call" | custom-call | flops 100 | bytes 100 | tf_op jit(solution)/shard_map/enter/pallas_call | solution.py:242
  54.6 1.3 %finish.1 = (bf16[4,128,256]{2,1,0:T(8,128)(2,1)S(1)}, bf16[4,128,256]{2,1,0:T(8,128)(2,1)S(1)}, bf16[4,128,256]{2,1,0:T(8,128)(2,1)S(1)}) custom-call(s32[4]{0:T(128)S(1)} %pad_add_fusion.sc_ref, f32[128,4096]{1,0:T(8,128)S(1)} %gates.1.gate_ref, bf16[4,2,128,128]{3,2,1,0:T(8,128)(2,1)S(1)} %get-tuple-element.111.refs_0_, ...), custom_call_target="tpu_custom_call" | custom-call | flops 100 | bytes 100 | tf_op jit(solution)/shard_map/finish/pallas_call | solution.py:242
  56.1 1.7 %finish_last.1 = bf16[128,4096]{1,0:T(8,128)(2,1)} custom-call(s32[4]{0:T(128)S(1)} %pad_add_fusion.sc_ref, f32[128,4096]{1,0:T(8,128)S(1)} %gates.1.gate_ref, bf16[4,2,128,128]{3,2,1,0:T(8,128)(2,1)S(1)} %collective-permute-done.9.state_ref, f32[4,2,128,128]{3,2,1,0:T(8,128)S(1)} %get-tuple-element.78.loc_ref, ...), custom_call_target="tpu_custom_call" | custom-call | flops 100 | bytes 100 | tf_op jit(solution)/shard_map/finish_last/pallas_call | solution.py:490
  (34 shorter events, 1.8 us)
Async XLA Ops:
  0.0 6.4 %copy-start.1 = (bf16[7,128,128]{2,1,0:T(8,128)(2,1)S(1)}, bf16[7,128,128]{2,1,0:T(8,128)(2,1)}, u32[]{:S(2)}) copy-start(bf16[7,128,128]{2,1,0:T(8,128)(2,1)} %constant.54.clone.masks_ref) | copy-start | bytes 688132
  0.0 4.2 %copy-start.2 = (f32[128,32]{0,1:T(8,128)S(1)}, f32[128,32]{0,1:T(8,128)}, u32[]{:S(2)}) copy-start(f32[128,32]{0,1:T(8,128)} %param.10) | copy-start | bytes 49156
  0.0 4.2 %copy-start.3 = (bf16[128,32]{0,1:T(8,128)(2,1)S(1)}, bf16[128,32]{0,1:T(8,128)(2,1)}, u32[]{:S(2)}) copy-start(bf16[128,32]{0,1:T(8,128)(2,1)} %param.9) | copy-start | bytes 24580
  1.7 4.7 %collective-permute-start = (bf16[4,8192]{1,0:T(4,128)(2,1)S(1)}, bf16[4,8192]{1,0:T(4,128)(2,1)S(1)}, u32[]{:S(2)}, u32[]{:S(2)}) collective-permute-start(bf16[4,8192]{1,0:T(4,128)(2,1)S(1)} %get-tuple-element.62), channel_id=1, source_target_pairs={{0,1},{1,2},{2,3},{3,4},{4,5},{5,6},{6,7},{7,8},{8,9},{9,10},{10,1... | collective-permute-start | bytes 196616 | tf_op jit(solution)/shard_map/ppermute | solution.py:507
  11.0 7.4 %collective-permute-start.10 = (bf16[4,264,256]{2,1,0:T(8,128)(2,1)S(1)}, bf16[4,264,256]{2,1,0:T(8,128)(2,1)S(1)}, u32[]{:S(2)}, u32[]{:S(2)}) collective-permute-start(bf16[4,264,256]{2,1,0:T(8,128)(2,1)S(1)} %get-tuple-element.99), channel_id=1, source_target_pairs={{0,1},{1,0},{2,3},{3,2},{4,5},{5,4},{6,7},{7,6},{8,9},{9,8},{10,11... | collective-permute-start | bytes 1622024 | tf_op jit(solution)/shard_map/ppermute | solution.py:511
  18.4 5.2 %collective-permute-start.1 = (bf16[4,264,256]{2,1,0:T(8,128)(2,1)S(1)}, bf16[4,264,256]{2,1,0:T(8,128)(2,1)S(1)}, u32[]{:S(2)}, u32[]{:S(2)}) collective-permute-start(bf16[4,264,256]{2,1,0:T(8,128)(2,1)S(1)} %get-tuple-element.85), channel_id=1, source_target_pairs={{0,1},{1,0},{2,3},{3,2},{4,5},{5,4},{6,7},{7,6},{8,9},{9,8},{10,11... | collective-permute-start | bytes 1622024 | tf_op jit(solution)/shard_map/ppermute | solution.py:511
  19.4 8.0 %collective-permute-start.11 = (bf16[264,256]{1,0:T(8,128)(2,1)S(1)}, bf16[264,256]{1,0:T(8,128)(2,1)S(1)}, u32[]{:S(2)}, u32[]{:S(2)}) collective-permute-start(bf16[264,256]{1,0:T(8,128)(2,1)S(1)} %get-tuple-element.102), channel_id=1, source_target_pairs={{0,2},{1,3},{2,0},{3,1},{4,6},{5,7},{6,4},{7,5},{8,10},{9,11},{10,... | collective-permute-start | bytes 405512 | tf_op jit(solution)/shard_map/ppermute | solution.py:511
  21.2 7.1 %collective-permute-start.12 = (bf16[264,256]{1,0:T(8,128)(2,1)S(1)}, bf16[264,256]{1,0:T(8,128)(2,1)S(1)}, u32[]{:S(2)}, u32[]{:S(2)}) collective-permute-start(bf16[264,256]{1,0:T(8,128)(2,1)S(1)} %get-tuple-element.103), channel_id=1, source_target_pairs={{0,4},{1,5},{2,6},{3,7},{4,0},{5,1},{6,2},{7,3},{8,12},{9,13},{10,... | collective-permute-start | bytes 405512 | tf_op jit(solution)/shard_map/ppermute | solution.py:511
  22.7 8.2 %collective-permute-start.13 = (bf16[264,256]{1,0:T(8,128)(2,1)S(1)}, bf16[264,256]{1,0:T(8,128)(2,1)S(1)}, u32[]{:S(2)}, u32[]{:S(2)}) collective-permute-start(bf16[264,256]{1,0:T(8,128)(2,1)S(1)} %get-tuple-element.104), channel_id=1, source_target_pairs={{0,6},{1,7},{2,4},{3,5},{4,2},{5,3},{6,0},{7,1},{8,14},{9,15},{10,... | collective-permute-start | bytes 405512 | tf_op jit(solution)/shard_map/ppermute | solution.py:511
  24.7 13.6 %collective-permute-start.2 = (bf16[264,256]{1,0:T(8,128)(2,1)S(1)}, bf16[264,256]{1,0:T(8,128)(2,1)S(1)}, u32[]{:S(2)}, u32[]{:S(2)}) collective-permute-start(bf16[264,256]{1,0:T(8,128)(2,1)S(1)} %get-tuple-element.88), channel_id=1, source_target_pairs={{0,2},{1,3},{2,0},{3,1},{4,6},{5,7},{6,4},{7,5},{8,10},{9,11},{10,... | collective-permute-start | bytes 405512 | tf_op jit(solution)/shard_map/ppermute | solution.py:511
  25.8 12.4 %collective-permute-start.3 = (bf16[264,256]{1,0:T(8,128)(2,1)S(1)}, bf16[264,256]{1,0:T(8,128)(2,1)S(1)}, u32[]{:S(2)}, u32[]{:S(2)}) collective-permute-start(bf16[264,256]{1,0:T(8,128)(2,1)S(1)} %get-tuple-element.89), channel_id=1, source_target_pairs={{0,4},{1,5},{2,6},{3,7},{4,0},{5,1},{6,2},{7,3},{8,12},{9,13},{10,... | collective-permute-start | bytes 405512 | tf_op jit(solution)/shard_map/ppermute | solution.py:511
  27.4 10.9 %collective-permute-start.4 = (bf16[264,256]{1,0:T(8,128)(2,1)S(1)}, bf16[264,256]{1,0:T(8,128)(2,1)S(1)}, u32[]{:S(2)}, u32[]{:S(2)}) collective-permute-start(bf16[264,256]{1,0:T(8,128)(2,1)S(1)} %get-tuple-element.90), channel_id=1, source_target_pairs={{0,6},{1,7},{2,4},{3,5},{4,2},{5,3},{6,0},{7,1},{8,14},{9,15},{10,... | collective-permute-start | bytes 405512 | tf_op jit(solution)/shard_map/ppermute | solution.py:511
  32.1 7.8 %collective-permute-start.14 = (bf16[2,128,128]{2,1,0:T(8,128)(2,1)S(1)}, bf16[2,128,128]{2,1,0:T(8,128)(2,1)S(1)}, u32[]{:S(2)}, u32[]{:S(2)}) collective-permute-start(bf16[2,128,128]{2,1,0:T(8,128)(2,1)S(1)} %get-tuple-element.106), channel_id=1, source_target_pairs={{0,8},{1,9},{2,10},{3,11},{4,12},{5,13},{6,14},{7,15},{8,0},{9,1},... | collective-permute-start | bytes 196616 | tf_op jit(solution)/shard_map/ppermute | solution.py:511
  34.6 14.8 %copy-start.4 = (f32[128]{0:T(128)S(1)}, f32[128]{0:T(128)}, u32[]{:S(2)}) copy-start(f32[128]{0:T(128)} %param.12) | copy-start | bytes 1540
  38.2 11.2 %copy-start = (bf16[128,4096]{1,0:T(8,128)(2,1)S(1)}, bf16[128,4096]{1,0:T(8,128)(2,1)}, u32[]{:S(2)}) copy-start(bf16[128,4096]{1,0:T(8,128)(2,1)} %gate_ref.1) | copy-start | bytes 3145732
  39.4 5.2 %collective-permute-start.5 = (bf16[2,128,128]{2,1,0:T(8,128)(2,1)S(1)}, bf16[2,128,128]{2,1,0:T(8,128)(2,1)S(1)}, u32[]{:S(2)}, u32[]{:S(2)}) collective-permute-start(bf16[2,128,128]{2,1,0:T(8,128)(2,1)S(1)} %get-tuple-element.92), channel_id=1, source_target_pairs={{0,8},{1,9},{2,10},{3,11},{4,12},{5,13},{6,14},{7,15},{8,0},{9,1},... | collective-permute-start | bytes 196616 | tf_op jit(solution)/shard_map/ppermute | solution.py:511
  40.9 7.7 %collective-permute-start.15 = (bf16[2,128,128]{2,1,0:T(8,128)(2,1)S(1)}, bf16[2,128,128]{2,1,0:T(8,128)(2,1)S(1)}, u32[]{:S(2)}, u32[]{:S(2)}) collective-permute-start(bf16[2,128,128]{2,1,0:T(8,128)(2,1)S(1)} %get-tuple-element.108), channel_id=1, source_target_pairs={{0,2},{1,3},{2,0},{3,1},{4,6},{5,7},{6,4},{7,5},{8,10},{9,11},{10,... | collective-permute-start | bytes 196616 | tf_op jit(solution)/shard_map/ppermute | solution.py:511
  41.9 8.1 %collective-permute-start.16 = (bf16[2,128,128]{2,1,0:T(8,128)(2,1)S(1)}, bf16[2,128,128]{2,1,0:T(8,128)(2,1)S(1)}, u32[]{:S(2)}, u32[]{:S(2)}) collective-permute-start(bf16[2,128,128]{2,1,0:T(8,128)(2,1)S(1)} %get-tuple-element.109), channel_id=1, source_target_pairs={{0,4},{1,5},{2,6},{3,7},{4,0},{5,1},{6,2},{7,3},{8,12},{9,13},{10,... | collective-permute-start | bytes 196616 | tf_op jit(solution)/shard_map/ppermute | solution.py:511
  43.2 6.9 %collective-permute-start.17 = (bf16[2,128,128]{2,1,0:T(8,128)(2,1)S(1)}, bf16[2,128,128]{2,1,0:T(8,128)(2,1)S(1)}, u32[]{:S(2)}, u32[]{:S(2)}) collective-permute-start(bf16[2,128,128]{2,1,0:T(8,128)(2,1)S(1)} %get-tuple-element.110), channel_id=1, source_target_pairs={{0,6},{1,7},{2,4},{3,5},{4,2},{5,3},{6,0},{7,1},{8,14},{9,15},{10,... | collective-permute-start | bytes 196616 | tf_op jit(solution)/shard_map/ppermute | solution.py:511
  45.7 5.2 %collective-permute-start.6 = (bf16[2,128,128]{2,1,0:T(8,128)(2,1)S(1)}, bf16[2,128,128]{2,1,0:T(8,128)(2,1)S(1)}, u32[]{:S(2)}, u32[]{:S(2)}) collective-permute-start(bf16[2,128,128]{2,1,0:T(8,128)(2,1)S(1)} %get-tuple-element.94), channel_id=1, source_target_pairs={{0,2},{1,3},{2,0},{3,1},{4,6},{5,7},{6,4},{7,5},{8,10},{9,11},{10,... | collective-permute-start | bytes 196616 | tf_op jit(solution)/shard_map/ppermute | solution.py:511
  46.5 4.4 %collective-permute-start.7 = (bf16[2,128,128]{2,1,0:T(8,128)(2,1)S(1)}, bf16[2,128,128]{2,1,0:T(8,128)(2,1)S(1)}, u32[]{:S(2)}, u32[]{:S(2)}) collective-permute-start(bf16[2,128,128]{2,1,0:T(8,128)(2,1)S(1)} %get-tuple-element.95), channel_id=1, source_target_pairs={{0,4},{1,5},{2,6},{3,7},{4,0},{5,1},{6,2},{7,3},{8,12},{9,13},{10,... | collective-permute-start | bytes 196616 | tf_op jit(solution)/shard_map/ppermute | solution.py:511
  48.6 5.2 %collective-permute-start.8 = (bf16[2,128,128]{2,1,0:T(8,128)(2,1)S(1)}, bf16[2,128,128]{2,1,0:T(8,128)(2,1)S(1)}, u32[]{:S(2)}, u32[]{:S(2)}) collective-permute-start(bf16[2,128,128]{2,1,0:T(8,128)(2,1)S(1)} %get-tuple-element.96), channel_id=1, source_target_pairs={{0,6},{1,7},{2,4},{3,5},{4,2},{5,3},{6,0},{7,1},{8,14},{9,15},{10,... | collective-permute-start | bytes 196616 | tf_op jit(solution)/shard_map/ppermute | solution.py:511
  50.8 3.8 %collective-permute-start.18 = (bf16[4,2,128,128]{3,2,1,0:T(8,128)(2,1)S(1)}, bf16[4,2,128,128]{3,2,1,0:T(8,128)(2,1)S(1)}, u32[]{:S(2)}, u32[]{:S(2)}) collective-permute-start(bf16[4,2,128,128]{3,2,1,0:T(8,128)(2,1)S(1)} %get-tuple-element.112), channel_id=1, source_target_pairs={{0,1},{1,0},{2,3},{3,2},{4,5},{5,4},{6,7},{7,6},{8,9},{9,8},{10,11... | collective-permute-start | bytes 786440 | tf_op jit(solution)/shard_map/ppermute | solution.py:511
  54.5 1.6 %collective-permute-start.9 = (bf16[4,2,128,128]{3,2,1,0:T(8,128)(2,1)S(1)}, bf16[4,2,128,128]{3,2,1,0:T(8,128)(2,1)S(1)}, u32[]{:S(2)}, u32[]{:S(2)}) collective-permute-start(bf16[4,2,128,128]{3,2,1,0:T(8,128)(2,1)S(1)} %get-tuple-element.97), channel_id=1, source_target_pairs={{0,1},{1,0},{2,3},{3,2},{4,5},{5,4},{6,7},{7,6},{8,9},{9,8},{10,11... | collective-permute-start | bytes 786440 | tf_op jit(solution)/shard_map/ppermute | solution.py:511
